TPU v7x, 1024 devices: a whole 4x4x32 slice. The times are simulated.
1024 devices in a mesh: row: 8 (over x, core), col: 128 (over z, y).
Axes of the slice: x: 4, y: 4, z: 32, core: 2. Of those that a mesh axis runs over, the one named last changes fastest.
Arguments:
- features: bfloat16 [65536, 256], P(('row', 'col')), may hold values from -6 to 6
- adj_tiles: bfloat16 [8, 128, 96, 128, 128], P('row', 'col'), may hold values from -0.0546875 to 0.0546875
- tile_coord: int32 [8, 128, 96], P('row', 'col'), may hold values from 0 to 255, as said below
- tile_count: int32 [8, 128], P('row', 'col'), may hold values from 1 to 96, as said below
- weight: bfloat16 [256, 256], replicated, may hold values from -0.375 to 0.375
Outputs:
- out: bfloat16 [65536, 256], P(('col', 'row'))
Inputs may be any that keep to these rules, and one draw needn't show every extreme that they name: `tile_coord`: each entry is t * 64 + s for a target tile t and a source tile s; within one device's list all entries differ. `tile_count`: slots from this number on are not part of the adjacency.
All inputs are finite; a program needn't handle non-finite values.
Results may differ from a plain program's by a relative error of at most 0.0049.
Values may be sent and summed in bfloat16 or wider, within the bound.
No kernel may reach another device: no remote copies, remote signals or barrier semaphores. Data moves between devices by JAX's collectives and lax.ppermute only.
A program may use at most 128 MiB of HBM per device.

v0:
```python
import math

import jax
import jax.numpy as jnp
from jax import lax
from jax.sharding import PartitionSpec as P


def on_device(features, adj_tiles, tile_coord, tile_count, weight):
    tile_size = adj_tiles.shape[-1]
    feat_width = features.shape[1]
    slot_count = adj_tiles.shape[2]
    local_rows = features.shape[0]
    target_count = local_rows * lax.axis_size("row") // tile_size
    source_count = local_rows * lax.axis_size("col") // tile_size
    tile_vals = adj_tiles[0, 0]
    coord_list = tile_coord[0, 0]
    live_slot = jnp.arange(slot_count) < tile_count[0, 0]
    tile_vals = jnp.where(live_slot[:, None, None], tile_vals, jnp.zeros_like(tile_vals))
    target = coord_list // source_count
    source = coord_list % source_count
    gathered = lax.all_gather(features, "col", axis=0, tiled=True)
    source_tiles = gathered.reshape(source_count, tile_size, feat_width)
    group_size = math.gcd(slot_count, 16)
    steps_count = slot_count // group_size
    inputs = (
        tile_vals.reshape(steps_count, group_size, tile_size, tile_size),
        source.reshape(steps_count, group_size),
        target.reshape(steps_count, group_size),
    )

    def add_group(total, items):
        tile_group, src_group, target_group = items
        feat_rows = source_tiles[src_group]
        products = jnp.einsum(
            "kij,kjf->kif", tile_group, feat_rows, preferred_element_type=jnp.float32
        )
        total = total.at[target_group].add(products)
        return (total, None)

    start_total = jnp.zeros((target_count, tile_size, feat_width), jnp.float32)
    total, unused = lax.scan(add_group, start_total, inputs)
    partial_value = total.reshape(target_count * tile_size, feat_width)
    hidden = lax.psum_scatter(partial_value, "row", scatter_dimension=0, tiled=True).astype(
        jnp.bfloat16
    )
    mixed = jnp.dot(hidden, weight, preferred_element_type=jnp.float32)
    return jax.nn.relu(mixed).astype(jnp.bfloat16)


def solution(mesh):
    return jax.shard_map(
        on_device,
        mesh=mesh,
        in_specs=(
            P(("row", "col"), None),
            P("row", "col", None, None, None),
            P("row", "col", None),
            P("row", "col"),
            P(),
        ),
        out_specs=P(("col", "row"), None),
        check_vma=False,
    )
```

profile of v0, /device:TPU:1, one launch (start us, length us, event | category | flops | bytes accessed | tf_op | source)
XLA Modules:
  0.0 387.8 jit_solution(11985972110191295938)
XLA Ops:
  6.5 0.0 copy-start
  6.5 0.0 all-gather.2.cloned.1.call-start
  6.5 0.7 all-gather.2.cloned.1.call-update
  7.3 0.0 reduce-scatter.2.cloned.1.call-start
  7.3 0.5 broadcast.81
  7.8 1.2 reduce.3
  9.0 0.1 squeeze.20
  9.8 3.9 broadcast_select_fusion
  13.7 261.0 %all-gather.2.cloned.1.call-done = bf16[8192,256]{1,0:T(8,128)(2,1)} async-done(((bf16[64,256]{1,0:T(8,128)(2,1)}), bf16[8192,256]{1,0:T(8,128)(2,1)}) %all-gather.2.cloned.1.call-update) | async-done | bytes 4194320 | tf_op jit(solution)/shard_map/all_gather | solution.py:22
  274.7 47.0 %while.10 = (s32[]{:T(128)}, f32[4,128,256]{2,1,0:T(8,128)S(1)}, s32[6,16]{1,0:T(8,128)S(1)}, bf16[6,16,128,128]{3,2,1,0:T(8,128)(2,1)}, s32[6,16]{1,0:T(8,128)S(1)}, /*index=5*/bf16[64,128,256]{2,1,0:T(8,128)(2,1)}, s32[]{:T(128)}) while((s32[]{:T(128)}, f32[4,128,256]{2,1,0:T(8,128)S(1)}, s32[6,16]{1,0:T(8,128)S(1)}, ...), condition=%wide.region_2.3_spmd, body=%wide.region_0.2_spmd.sunk | while | flops 134743136 | bytes 12063761 | solution.py:42
  274.7 3.8 gather_fusion
  278.5 1.8 fusion.21
  280.3 2.2 scatter_fusion
  282.6 3.8 gather_fusion
  286.4 1.8 fusion.21
  288.2 2.2 scatter_fusion
  290.4 3.8 gather_fusion
  294.2 1.8 fusion.21
  296.0 2.2 scatter_fusion
  298.2 3.8 gather_fusion
  302.0 1.8 fusion.21
  303.8 2.2 scatter_fusion
  306.1 3.8 gather_fusion
  309.9 1.8 fusion.21
  311.7 2.2 scatter_fusion
  313.9 3.8 gather_fusion
  317.7 1.8 fusion.21
  319.5 2.2 scatter_fusion
  321.7 0.0 copy-start.1
  321.7 0.8 copy-done.1
  322.5 0.0 reduce-scatter.2.cloned.1.call-update
  322.5 56.9 %reduce-scatter.2.cloned.1.call-done = f32[64,256]{1,0:T(8,128)} async-done(((f32[512,256]{1,0:T(8,128)}), f32[64,256]{1,0:T(8,128)}) %reduce-scatter.2.cloned.1.call-update) | async-done | bytes 65552 | tf_op jit(solution)/shard_map/reduce_scatter | solution.py:44
  379.4 0.0 copy-done
  379.4 1.6 fusion.8
  (15 shorter events, 0.1 us)
Async XLA Ops:
  6.5 372.9 %copy-start = (bf16[256,256]{1,0:T(8,128)(2,1)S(1)}, bf16[256,256]{1,0:T(8,128)(2,1)}, u32[]{:S(2)}) copy-start(bf16[256,256]{1,0:T(8,128)(2,1)} %param.11) | copy-start | bytes 393220
  6.5 268.1 %all-gather.2.cloned.1.call-start = ((), (), s32[]{:S(2)}) async-start(), calls=%async_computation.1 | async-start | bytes 4227072 | tf_op jit(solution)/shard_map/all_gather | solution.py:22
  7.3 372.1 %reduce-scatter.2.cloned.1.call-start = ((), (), s32[]{:S(2)}) async-start(), calls=%async_computation.2 | async-start | bytes 589824 | tf_op jit(solution)/shard_map/reduce_scatter | solution.py:44
  321.7 0.8 copy-start.1
Sparse Core Ops, SparseCore 0:
  11.5 263.1 all-gather.1
  322.6 56.7 reduce-scatter.1
where the time goes:
time: 388 us
  waiting for transfers between devices  319 us (82%)
  local copies, waits for them, and re-layouts  24.1 us (6%)
  other arithmetic  18.3 us (5%)
  between operations  14.1 us (4%)
  matrix products  12.4 us (3%)
    all_gather x1, waiting for transfers between devices, on_device(): gathered = lax.all_gather(features, 'col', axis=0, tiled=True)  261 us
    reduce_scatter x1, waiting for transfers between devices, on_device(): lax.psum_scatter(partial_value, 'row', scatter_dimension=0, tiled=True)  56.9 us
    gather x6, local copies, waits for them, and re-layouts, add_group(): feat_rows = source_tiles[src_group]  22.7 us
    scatter-add x6, other arithmetic, add_group(): total = total.at[target_group].add(products)  13.1 us
    dot_general x6, matrix products, add_group(): jnp.einsum('kij,kjf->kif', tile_group, feat_rows, preferred_element_type=...  10.8 us
  transfers between devices with their start and end apart: 2, of which 2 were waited for; matrix products, arithmetic and copies ran while one was open for 1% of the time, Pallas kernels for 0%

commit v1 on v0

v1 whole, which is shorter than its diff:
```python
import functools

import jax
import jax.numpy as jnp
from jax import lax
from jax.experimental import pallas as pl
from jax.experimental.pallas import tpu as pltpu
from jax.sharding import Mesh, PartitionSpec as P

Y_RING = 4


def ring_shift(value, axis, step):
    size = lax.axis_size(axis)
    return lax.ppermute(value, axis, [(i, (i + step) % size) for i in range(size)])


def trade_halves(value, axis):
    half = value.shape[0] // 2
    return ring_shift(value[:half], axis, 1), ring_shift(value[half:], axis, -1)


def gather_ring(value):
    half = value.shape[0] // 2
    previous = ring_shift(value, "y", 1)
    following = ring_shift(value, "y", -1)
    return (
        previous,
        following,
        ring_shift(previous[:half], "y", 1),
        ring_shift(following[half:], "y", -1),
    )


def aggregate_kernel(
    place_ref, coord_ref, count_ref, adj_ref, *refs, pieces, source_count, tile
):
    piece_refs = refs[: len(pieces)]
    out_ref, dense, feats, tile_sem, feat_sem = refs[len(pieces) :]
    own_half, own_y = place_ref[0], place_ref[1]
    copies = []
    for index, (ref, (other, offset, start, length)) in enumerate(zip(piece_refs, pieces)):
        half = (own_half + other) % 2
        ring_at = (own_y + offset) % Y_RING
        copy = pltpu.make_async_copy(
            ref, feats.at[pl.ds(start, length), half, ring_at], feat_sem.at[index]
        )
        copy.start()
        copies.append(copy)

    def clear(index, carry):
        dense[index] = jnp.zeros(dense.shape[1:], dense.dtype)
        return carry

    lax.fori_loop(0, source_count, clear, 0)
    live = count_ref[0]

    def place(slot, carry):
        target = coord_ref[slot] // source_count
        source = coord_ref[slot] % source_count
        rows = pl.ds(pl.multiple_of(target * tile, tile), tile)
        pltpu.make_async_copy(adj_ref.at[slot], dense.at[source, rows], tile_sem).start()
        return carry

    lax.fori_loop(0, live, place, 0)

    def arrived(slot, carry):
        pltpu.make_async_copy(adj_ref.at[0], dense.at[0, pl.ds(0, tile)], tile_sem).wait()
        return carry

    lax.fori_loop(0, live, arrived, 0)
    for copy in copies:
        copy.wait()
    per_step = 4
    depth = feats.shape[2] * feats.shape[3]
    width = depth // tile

    def multiply(step, carry):
        left = jnp.concatenate(
            [dense[step * per_step * width + i] for i in range(per_step * width)], axis=1
        )
        right = feats[pl.ds(step * (per_step // 2), per_step // 2)]
        right = right.reshape(per_step * depth, feats.shape[-1])
        product = jnp.dot(left, right, preferred_element_type=jnp.float32)

        @pl.when(step == 0)
        def first():
            out_ref[...] = product

        @pl.when(step > 0)
        def later():
            out_ref[...] += product

        return carry

    lax.fori_loop(0, source_count // (per_step * width), multiply, 0)


def on_device(features, adj_tiles, tile_coord, tile_count, weight):
    tile = adj_tiles.shape[-1]
    rows, width = features.shape
    slots = adj_tiles.shape[2]
    z_size, y_size = lax.axis_size("z"), lax.axis_size("y")
    row_size = lax.axis_size("row")
    target_count = rows * row_size // tile
    source_count = rows * z_size * y_size // tile
    half_z = z_size // 2
    groups = [[i + 2 * j for j in range(half_z)] for i in range(2)]
    own = lax.all_gather(features, "z", axis=0, axis_index_groups=groups)
    other = jnp.concatenate(trade_halves(own, "z"), axis=0)
    arrays, pieces = [own, other], [(0, 0, 0, half_z), (1, 0, 0, half_z)]
    for which, value in ((0, own), (1, other)):
        previous, following, first, second = gather_ring(value)
        arrays += [previous, following, first, second]
        pieces += [
            (which, y_size - 1, 0, half_z),
            (which, 1, 0, half_z),
            (which, 2, 0, half_z // 2),
            (which, 2, half_z // 2, half_z // 2),
        ]
    place = jnp.stack([lax.axis_index("z") % 2, lax.axis_index("y")]).astype(jnp.int32)
    partial_value = pl.pallas_call(
        functools.partial(
            aggregate_kernel, pieces=pieces, source_count=source_count, tile=tile
        ),
        out_shape=jax.ShapeDtypeStruct((target_count * tile, width), jnp.float32),
        in_specs=[pl.BlockSpec(memory_space=pltpu.SMEM)] * 3
        + [pl.BlockSpec(memory_space=pl.ANY)] * (1 + len(arrays)),
        out_specs=pl.BlockSpec(memory_space=pltpu.VMEM),
        scratch_shapes=[
            pltpu.VMEM((source_count, target_count * tile, tile), jnp.bfloat16),
            pltpu.VMEM((half_z, 2, y_size, rows, width), jnp.bfloat16),
            pltpu.SemaphoreType.DMA(()),
            pltpu.SemaphoreType.DMA((len(arrays),)),
        ],
        compiler_params=pltpu.CompilerParams(vmem_limit_bytes=32 * 1024 * 1024),
    )(place, tile_coord[0, 0], tile_count[0], adj_tiles[0, 0], *arrays)
    parts = lax.all_to_all(
        partial_value.reshape(row_size, rows, width), "row", 0, 0, tiled=True
    )
    hidden = jnp.sum(parts, axis=0).astype(jnp.bfloat16)
    mixed = jnp.dot(hidden, weight, preferred_element_type=jnp.float32)
    return jax.nn.relu(mixed).astype(jnp.bfloat16)


def solution(mesh):
    devices = mesh.devices
    split = Mesh(
        devices.reshape(devices.shape[0], devices.shape[1] // Y_RING, Y_RING),
        ("row", "z", "y"),
    )
    col = ("z", "y")
    return jax.shard_map(
        on_device,
        mesh=split,
        in_specs=(
            P(("row", "z", "y"), None),
            P("row", col, None, None, None),
            P("row", col, None),
            P("row", col),
            P(),
        ),
        out_specs=P(("z", "y", "row"), None),
        check_vma=False,
    )
```

time: 388 us -> 130 us (0.34)
  waiting for transfers between devices: 319 us -> 10.5 us
  blocking collectives: 0 us -> 71.9 us
  starting transfers between devices: 0.04 us -> 31.3 us
  local copies, waits for them, and re-layouts: 24.1 us -> 4.84 us
  other arithmetic: 18.3 us -> 0.11 us
  between operations: 14.1 us -> 0.82 us
  matrix products: 12.4 us -> 0.77 us
  Pallas kernels: 0 us -> 9.59 us
    all_gather x1 -> x0, waiting for transfers between devices: 261 us -> none  [on_device(): gathered = lax.all_gather(features, 'col', axis=0, tiled=True)]
    reduce_scatter x1 -> x0, waiting for transfers between devices: 56.9 us -> none  [on_device(): lax.psum_scatter(partial_value, 'row', scatter_dimension=0, tiled=True)]
    all_gather x0 -> x1, blocking collectives: none -> 45.3 us  [on_device(): own = lax.all_gather(features, 'z', axis=0, axis_index_groups=groups)]
    ppermute x0 -> x10, starting transfers between devices: none -> 31.3 us  [ring_shift(): lax.ppermute(value, axis, [(i, (i + step) % size) for i in range(size)])]
    all_to_all x0 -> x1, blocking collectives: none -> 26.5 us  [on_device(): lax.all_to_all(partial_value.reshape(row_size, rows, width), 'row', 0, 0,...]
    gather x6 -> x0, local copies, waits for them, and re-layouts: 22.7 us -> none  [add_group(): feat_rows = source_tiles[src_group]]
    scatter-add x6 -> x0, other arithmetic: 13.1 us -> none  [add_group(): total = total.at[target_group].add(products)]
    dot_general x6 -> x0, matrix products: 10.8 us -> none  [add_group(): jnp.einsum('kij,kjf->kif', tile_group, feat_rows, preferred_element_type=...]
  transfers between devices with their start and end apart: 2 -> 10, of which waited for: 2 -> 4; matrix products, arithmetic and copies ran while one was open for 1% -> 2% of each run, Pallas kernels for 0% -> 0%
where the time goes in v1:
time: 130 us
  blocking collectives  71.9 us (55%)
  starting transfers between devices  31.3 us (24%)
  waiting for transfers between devices  10.5 us (8%)
  Pallas kernels  9.59 us (7%)
  local copies, waits for them, and re-layouts  4.84 us (4%)
    all_gather x1, blocking collectives, on_device(): own = lax.all_gather(features, 'z', axis=0, axis_index_groups=groups)  45.3 us
    ppermute x10, starting transfers between devices, ring_shift(): lax.ppermute(value, axis, [(i, (i + step) % size) for i in range(size)])  31.3 us
    all_to_all x1, blocking collectives, on_device(): lax.all_to_all(partial_value.reshape(row_size, rows, width), 'row', 0, 0,...  26.5 us
    ppermute x10, waiting for transfers between devices, ring_shift(): lax.ppermute(value, axis, [(i, (i + step) % size) for i in range(size)])  10.5 us
    pallas_call x1, Pallas kernels, on_device(): pl.pallas_call(functools.partial(aggregate_kernel, pieces=pieces, source_...  9.59 us
  transfers between devices with their start and end apart: 10, of which 4 were waited for; matrix products, arithmetic and copies ran while one was open for 2% of the time, Pallas kernels for 0%

profile of v1, /device:TPU:1, one launch (start us, length us, event | category | flops | bytes accessed | tf_op | source)
XLA Modules:
  0.0 129.8 jit_solution(6279208325079373593)
XLA Ops:
  0.0 0.0 copy-start
  0.0 0.0 copy-start.2
  0.0 45.3 %all-gather = bf16[1024,256]{1,0:T(8,128)(2,1)S(1)} all-gather(bf16[64,256]{1,0:T(8,128)(2,1)} %param.5), channel_id=2, replica_groups={{0,8,16,24,32,40,48,56,64,72,80,88,96,104,112,120},{4,12,20,28,36,44,52..., dimensions={0}, use_global_device_ids=true | all-gather | bytes 557056 | tf_op jit(solution)/shard_map/all_gather | solution.py:109
  45.4 2.6 %collective-permute-start = (bf16[8,64,256]{2,1,0:T(8,128)(2,1)S(1)}, bf16[8,64,256]{2,1,0:T(8,128)(2,1)S(1)}, u32[]{:S(2)}, u32[]{:S(2)}) collective-permute-start(bf16[8,64,256]{2,1,0:T(8,128)(2,1)S(1)} %bitcast.19), channel_id=1, source_target_pairs={{0,4},{4,8},{8,12},{12,16},{16,20},{20,24},{24,28},{28,32},{32,36}... | collective-permute-start | bytes 786440 | tf_op jit(solution)/shard_map/ppermute | solution.py:15
  48.0 3.9 %collective-permute-start.1 = (bf16[8,64,256]{2,1,0:T(8,128)(2,1)S(1)}, bf16[8,64,256]{2,1,0:T(8,128)(2,1)S(1)}, u32[]{:S(2)}, u32[]{:S(2)}) collective-permute-start(bf16[8,64,256]{2,1,0:T(8,128)(2,1)S(1)} %bitcast.18), channel_id=1, source_target_pairs={{0,124},{4,0},{8,4},{12,8},{16,12},{20,16},{24,20},{28,24},{32,28}... | collective-permute-start | bytes 786440 | tf_op jit(solution)/shard_map/ppermute | solution.py:15
  51.9 3.2 %collective-permute-start.2 = (bf16[16,64,256]{2,1,0:T(8,128)(2,1)S(1)}, bf16[16,64,256]{2,1,0:T(8,128)(2,1)S(1)}, u32[]{:S(2)}, u32[]{:S(2)}) collective-permute-start(bf16[16,64,256]{2,1,0:T(8,128)(2,1)S(1)} %bitcast.12), channel_id=1, source_target_pairs={{0,1},{1,2},{2,3},{3,0},{4,5},{5,6},{6,7},{7,4},{8,9},{9,10},{10,1... | collective-permute-start | bytes 1572872 | tf_op jit(solution)/shard_map/ppermute | solution.py:15
  55.0 3.4 %collective-permute-start.3 = (bf16[16,64,256]{2,1,0:T(8,128)(2,1)S(1)}, bf16[16,64,256]{2,1,0:T(8,128)(2,1)S(1)}, u32[]{:S(2)}, u32[]{:S(2)}) collective-permute-start(bf16[16,64,256]{2,1,0:T(8,128)(2,1)S(1)} %bitcast.13), channel_id=1, source_target_pairs={{0,3},{1,0},{2,1},{3,2},{4,7},{5,4},{6,5},{7,6},{8,11},{9,8},{10,9... | collective-permute-start | bytes 1572872 | tf_op jit(solution)/shard_map/ppermute | solution.py:15
  58.4 0.0 collective-permute-done
  58.5 0.0 collective-permute-done.1
  58.5 3.4 %collective-permute-start.7 = (bf16[16,64,256]{2,1,0:T(8,128)(2,1)S(1)}, bf16[16,64,256]{2,1,0:T(8,128)(2,1)S(1)}, u32[]{:S(2)}, u32[]{:S(2)}) collective-permute-start(bf16[16,64,256]{2,1,0:T(8,128)(2,1)S(1)} %constant_dynamic-update-slice_fusion.refs_1_), channel_id=1, source_target_pairs={{0,3},{1,0},{2,1},{3,2},{4,7},{5,4},{6,5},{7,6},{8,11},{9,8},{10,9... | collective-permute-start | bytes 1572872 | tf_op jit(solution)/shard_map/ppermute | solution.py:15
  61.9 1.9 %collective-permute-start.6 = (bf16[16,64,256]{2,1,0:T(8,128)(2,1)S(1)}, bf16[16,64,256]{2,1,0:T(8,128)(2,1)S(1)}, u32[]{:S(2)}, u32[]{:S(2)}) collective-permute-start(bf16[16,64,256]{2,1,0:T(8,128)(2,1)S(1)} %constant_dynamic-update-slice_fusion.refs_1_), channel_id=1, source_target_pairs={{0,1},{1,2},{2,3},{3,0},{4,5},{5,6},{6,7},{7,4},{8,9},{9,10},{10,1... | collective-permute-start | bytes 1572872 | tf_op jit(solution)/shard_map/ppermute | solution.py:15
  63.8 0.0 collective-permute-done.2.refs_2_
  63.8 0.7 slice.28
  64.5 1.9 %collective-permute-start.4 = (bf16[8,64,256]{2,1,0:T(8,128)(2,1)}, bf16[8,64,256]{2,1,0:T(8,128)(2,1)S(1)}, u32[]{:S(2)}, u32[]{:S(2)}) collective-permute-start(bf16[8,64,256]{2,1,0:T(8,128)(2,1)} %slice.28), channel_id=1, source_target_pairs={{0,1},{1,2},{2,3},{3,0},{4,5},{5,6},{6,7},{7,4},{8,9},{9,10},{10,1... | collective-permute-start | bytes 786440 | tf_op jit(solution)/shard_map/ppermute | solution.py:15
  66.4 0.0 collective-permute-done.3.refs_3_
  66.4 0.7 slice.29
  67.2 4.6 %collective-permute-start.5 = (bf16[8,64,256]{2,1,0:T(8,128)(2,1)}, bf16[8,64,256]{2,1,0:T(8,128)(2,1)}, u32[]{:S(2)}, u32[]{:S(2)}) collective-permute-start(bf16[8,64,256]{2,1,0:T(8,128)(2,1)} %slice.29), channel_id=1, source_target_pairs={{0,3},{1,0},{2,1},{3,2},{4,7},{5,4},{6,5},{7,6},{8,11},{9,8},{10,9... | collective-permute-start | bytes 786440 | tf_op jit(solution)/shard_map/ppermute | solution.py:15
  71.7 1.5 %collective-permute-done.7.refs_7_ = bf16[16,64,256]{2,1,0:T(8,128)(2,1)S(1)} collective-permute-done((bf16[16,64,256]{2,1,0:T(8,128)(2,1)S(1)}, bf16[16,64,256]{2,1,0:T(8,128)(2,1)S(1)}, u32[]{:S(2)}, u32[]{:S(2)}) %collective-permute-start.7) | collective-permute-done | bytes 524320 | tf_op jit(solution)/shard_map/ppermute | solution.py:15
  73.2 0.7 slice.31
  73.9 4.6 %collective-permute-start.9 = (bf16[8,64,256]{2,1,0:T(8,128)(2,1)}, bf16[8,64,256]{2,1,0:T(8,128)(2,1)}, u32[]{:S(2)}, u32[]{:S(2)}) collective-permute-start(bf16[8,64,256]{2,1,0:T(8,128)(2,1)} %slice.31), channel_id=1, source_target_pairs={{0,3},{1,0},{2,1},{3,2},{4,7},{5,4},{6,5},{7,6},{8,11},{9,8},{10,9... | collective-permute-start | bytes 786440 | tf_op jit(solution)/shard_map/ppermute | solution.py:15
  78.6 0.0 collective-permute-done.6.refs_6_
  78.6 0.7 slice.30
  79.3 1.9 %collective-permute-start.8 = (bf16[8,64,256]{2,1,0:T(8,128)(2,1)}, bf16[8,64,256]{2,1,0:T(8,128)(2,1)}, u32[]{:S(2)}, u32[]{:S(2)}) collective-permute-start(bf16[8,64,256]{2,1,0:T(8,128)(2,1)} %slice.30), channel_id=1, source_target_pairs={{0,1},{1,2},{2,3},{3,0},{4,5},{5,6},{6,7},{7,4},{8,9},{9,10},{10,1... | collective-permute-start | bytes 786440 | tf_op jit(solution)/shard_map/ppermute | solution.py:15
  81.9 0.1 pad_add_fusion.place_ref
  82.0 1.4 %collective-permute-done.4.refs_4_ = bf16[8,64,256]{2,1,0:T(8,128)(2,1)S(1)} collective-permute-done((bf16[8,64,256]{2,1,0:T(8,128)(2,1)}, bf16[8,64,256]{2,1,0:T(8,128)(2,1)S(1)}, u32[]{:S(2)}, u32[]{:S(2)}) %collective-permute-start.4) | collective-permute-done | bytes 262176 | tf_op jit(solution)/shard_map/ppermute | solution.py:15
  83.3 0.0 collective-permute-done.5.refs_5_
  83.3 1.7 %collective-permute-done.9.refs_9_ = bf16[8,64,256]{2,1,0:T(8,128)(2,1)} collective-permute-done((bf16[8,64,256]{2,1,0:T(8,128)(2,1)}, bf16[8,64,256]{2,1,0:T(8,128)(2,1)}, u32[]{:S(2)}, u32[]{:S(2)}) %collective-permute-start.9) | collective-permute-done | bytes 262176 | tf_op jit(solution)/shard_map/ppermute | solution.py:15
  85.1 5.9 %collective-permute-done.8.refs_8_ = bf16[8,64,256]{2,1,0:T(8,128)(2,1)} collective-permute-done((bf16[8,64,256]{2,1,0:T(8,128)(2,1)}, bf16[8,64,256]{2,1,0:T(8,128)(2,1)}, u32[]{:S(2)}, u32[]{:S(2)}) %collective-permute-start.8) | collective-permute-done | bytes 262176 | tf_op jit(solution)/shard_map/ppermute | solution.py:15
  91.0 0.0 copy-done.2
  91.0 0.0 copy-start.1
  91.0 1.9 %copy-done.1 = bf16[1,1,96,128,128]{4,3,2,1,0:T(8,128)(2,1)S(1)} copy-done((bf16[1,1,96,128,128]{4,3,2,1,0:T(8,128)(2,1)S(1)}, bf16[1,1,96,128,128]{4,3,2,1,0:T(8,128)(2,1)}, u32[]{:S(2)}) %copy-start.1) | copy-done | bytes 3145752
  92.9 9.6 %shard_map.55 = f32[512,256]{1,0:T(8,128)S(1)} custom-call(s32[2]{0:T(128)S(1)} %pad_add_fusion.place_ref, s32[96]{0:T(128)S(1)} %bitcast.17, s32[1]{0:T(128)} %bitcast.11.count_ref, bf16[96,128,128]{2,1,0:T(8,128)(2,1)S(1)} %bitcast.15, bf16[16,64,256]{2,1,0:T(8,128)(2,1)S(1)} %bitcast.14, ...), custom_call_target="tpu_custom_call" | custom-call | tf_op jit(solution)/shard_map/pallas_call | solution.py:122
  102.5 26.5 %all_to_all.5 = f32[8,64,256]{2,1,0:T(8,128)S(1)} all-to-all(f32[8,64,256]{2,1,0:T(8,128)S(1)} %bitcast.16), channel_id=1, replica_groups=mesh['row'=8,'z'=32,'y'=4] {'row'}, dimensions={0} | all-to-all | bytes 1048576 | tf_op jit(solution)/shard_map/all_to_all | solution.py:138
  129.1 0.0 copy-done
  129.1 0.8 fusion
  (4 shorter events, 0.1 us)
Async XLA Ops:
  0.0 129.1 %copy-start = (bf16[256,256]{1,0:T(8,128)(2,1)S(1)}, bf16[256,256]{1,0:T(8,128)(2,1)}, u32[]{:S(2)}) copy-start(bf16[256,256]{1,0:T(8,128)(2,1)} %param.9) | copy-start | bytes 393220
  0.0 91.0 %copy-start.2 = (s32[1,1,96]{2,1,0:T(1,128)S(1)}, s32[1,1,96]{2,1,0:T(1,128)}, u32[]{:S(2)}) copy-start(s32[1,1,96]{2,1,0:T(1,128)} %param.7) | copy-start | bytes 1156
  45.4 13.0 %collective-permute-start = (bf16[8,64,256]{2,1,0:T(8,128)(2,1)S(1)}, bf16[8,64,256]{2,1,0:T(8,128)(2,1)S(1)}, u32[]{:S(2)}, u32[]{:S(2)}) collective-permute-start(bf16[8,64,256]{2,1,0:T(8,128)(2,1)S(1)} %bitcast.19), channel_id=1, source_target_pairs={{0,4},{4,8},{8,12},{12,16},{16,20},{20,24},{24,28},{28,32},{32,36}... | collective-permute-start | bytes 786440 | tf_op jit(solution)/shard_map/ppermute | solution.py:15
  48.0 10.4 %collective-permute-start.1 = (bf16[8,64,256]{2,1,0:T(8,128)(2,1)S(1)}, bf16[8,64,256]{2,1,0:T(8,128)(2,1)S(1)}, u32[]{:S(2)}, u32[]{:S(2)}) collective-permute-start(bf16[8,64,256]{2,1,0:T(8,128)(2,1)S(1)} %bitcast.18), channel_id=1, source_target_pairs={{0,124},{4,0},{8,4},{12,8},{16,12},{20,16},{24,20},{28,24},{32,28}... | collective-permute-start | bytes 786440 | tf_op jit(solution)/shard_map/ppermute | solution.py:15
  51.9 11.9 %collective-permute-start.2 = (bf16[16,64,256]{2,1,0:T(8,128)(2,1)S(1)}, bf16[16,64,256]{2,1,0:T(8,128)(2,1)S(1)}, u32[]{:S(2)}, u32[]{:S(2)}) collective-permute-start(bf16[16,64,256]{2,1,0:T(8,128)(2,1)S(1)} %bitcast.12), channel_id=1, source_target_pairs={{0,1},{1,2},{2,3},{3,0},{4,5},{5,6},{6,7},{7,4},{8,9},{9,10},{10,1... | collective-permute-start | bytes 1572872 | tf_op jit(solution)/shard_map/ppermute | solution.py:15
  55.0 11.4 %collective-permute-start.3 = (bf16[16,64,256]{2,1,0:T(8,128)(2,1)S(1)}, bf16[16,64,256]{2,1,0:T(8,128)(2,1)S(1)}, u32[]{:S(2)}, u32[]{:S(2)}) collective-permute-start(bf16[16,64,256]{2,1,0:T(8,128)(2,1)S(1)} %bitcast.13), channel_id=1, source_target_pairs={{0,3},{1,0},{2,1},{3,2},{4,7},{5,4},{6,5},{7,6},{8,11},{9,8},{10,9... | collective-permute-start | bytes 1572872 | tf_op jit(solution)/shard_map/ppermute | solution.py:15
  58.5 14.7 %collective-permute-start.7 = (bf16[16,64,256]{2,1,0:T(8,128)(2,1)S(1)}, bf16[16,64,256]{2,1,0:T(8,128)(2,1)S(1)}, u32[]{:S(2)}, u32[]{:S(2)}) collective-permute-start(bf16[16,64,256]{2,1,0:T(8,128)(2,1)S(1)} %constant_dynamic-update-slice_fusion.refs_1_), channel_id=1, source_target_pairs={{0,3},{1,0},{2,1},{3,2},{4,7},{5,4},{6,5},{7,6},{8,11},{9,8},{10,9... | collective-permute-start | bytes 1572872 | tf_op jit(solution)/shard_map/ppermute | solution.py:15
  61.9 16.7 %collective-permute-start.6 = (bf16[16,64,256]{2,1,0:T(8,128)(2,1)S(1)}, bf16[16,64,256]{2,1,0:T(8,128)(2,1)S(1)}, u32[]{:S(2)}, u32[]{:S(2)}) collective-permute-start(bf16[16,64,256]{2,1,0:T(8,128)(2,1)S(1)} %constant_dynamic-update-slice_fusion.refs_1_), channel_id=1, source_target_pairs={{0,1},{1,2},{2,3},{3,0},{4,5},{5,6},{6,7},{7,4},{8,9},{9,10},{10,1... | collective-permute-start | bytes 1572872 | tf_op jit(solution)/shard_map/ppermute | solution.py:15
  64.5 18.8 %collective-permute-start.4 = (bf16[8,64,256]{2,1,0:T(8,128)(2,1)}, bf16[8,64,256]{2,1,0:T(8,128)(2,1)S(1)}, u32[]{:S(2)}, u32[]{:S(2)}) collective-permute-start(bf16[8,64,256]{2,1,0:T(8,128)(2,1)} %slice.28), channel_id=1, source_target_pairs={{0,1},{1,2},{2,3},{3,0},{4,5},{5,6},{6,7},{7,4},{8,9},{9,10},{10,1... | collective-permute-start | bytes 786440 | tf_op jit(solution)/shard_map/ppermute | solution.py:15
  67.2 16.2 %collective-permute-start.5 = (bf16[8,64,256]{2,1,0:T(8,128)(2,1)}, bf16[8,64,256]{2,1,0:T(8,128)(2,1)}, u32[]{:S(2)}, u32[]{:S(2)}) collective-permute-start(bf16[8,64,256]{2,1,0:T(8,128)(2,1)} %slice.29), channel_id=1, source_target_pairs={{0,3},{1,0},{2,1},{3,2},{4,7},{5,4},{6,5},{7,6},{8,11},{9,8},{10,9... | collective-permute-start | bytes 786440 | tf_op jit(solution)/shard_map/ppermute | solution.py:15
  73.9 11.1 %collective-permute-start.9 = (bf16[8,64,256]{2,1,0:T(8,128)(2,1)}, bf16[8,64,256]{2,1,0:T(8,128)(2,1)}, u32[]{:S(2)}, u32[]{:S(2)}) collective-permute-start(bf16[8,64,256]{2,1,0:T(8,128)(2,1)} %slice.31), channel_id=1, source_target_pairs={{0,3},{1,0},{2,1},{3,2},{4,7},{5,4},{6,5},{7,6},{8,11},{9,8},{10,9... | collective-permute-start | bytes 786440 | tf_op jit(solution)/shard_map/ppermute | solution.py:15
  79.3 11.7 %collective-permute-start.8 = (bf16[8,64,256]{2,1,0:T(8,128)(2,1)}, bf16[8,64,256]{2,1,0:T(8,128)(2,1)}, u32[]{:S(2)}, u32[]{:S(2)}) collective-permute-start(bf16[8,64,256]{2,1,0:T(8,128)(2,1)} %slice.30), channel_id=1, source_target_pairs={{0,1},{1,2},{2,3},{3,0},{4,5},{5,6},{6,7},{7,4},{8,9},{9,10},{10,1... | collective-permute-start | bytes 786440 | tf_op jit(solution)/shard_map/ppermute | solution.py:15
  91.0 1.9 %copy-start.1 = (bf16[1,1,96,128,128]{4,3,2,1,0:T(8,128)(2,1)S(1)}, bf16[1,1,96,128,128]{4,3,2,1,0:T(8,128)(2,1)}, u32[]{:S(2)}) copy-start(bf16[1,1,96,128,128]{4,3,2,1,0:T(8,128)(2,1)} %param.6) | copy-start | bytes 9437188

commit v2 on v1

v2 whole, which is shorter than its diff:
```python
import functools

import jax
import jax.numpy as jnp
from jax import lax
from jax.experimental import pallas as pl
from jax.experimental.pallas import tpu as pltpu
from jax.sharding import Mesh, PartitionSpec as P

Y_RING = 4


def ring_shift(value, axis, step):
    size = lax.axis_size(axis)
    return lax.ppermute(value, axis, [(i, (i + step) % size) for i in range(size)])


def spread_kernel(
    coord_ref, count_ref, adj_ref, dense_ref, dense, tile_sem, out_sem, *, source_count, tile
):
    def clear(index, carry):
        dense[index] = jnp.zeros(dense.shape[1:], dense.dtype)
        return carry

    lax.fori_loop(0, source_count, clear, 0)
    live = count_ref[0]

    def place(slot, carry):
        target = coord_ref[slot] // source_count
        source = coord_ref[slot] % source_count
        rows = pl.ds(pl.multiple_of(target * tile, tile), tile)
        pltpu.make_async_copy(adj_ref.at[slot], dense.at[source, rows], tile_sem).start()
        return carry

    lax.fori_loop(0, live, place, 0)

    def arrived(slot, carry):
        pltpu.make_async_copy(adj_ref.at[0], dense.at[0, pl.ds(0, tile)], tile_sem).wait()
        return carry

    lax.fori_loop(0, live, arrived, 0)
    out = pltpu.make_async_copy(dense, dense_ref, out_sem)
    out.start()
    out.wait()


def spread(adj_tiles, coord, count, target_count, source_count):
    tile = adj_tiles.shape[-1]
    shape = (source_count, target_count * tile, tile)
    return pl.pallas_call(
        functools.partial(spread_kernel, source_count=source_count, tile=tile),
        out_shape=jax.ShapeDtypeStruct(shape, jnp.bfloat16),
        in_specs=[pl.BlockSpec(memory_space=pltpu.SMEM)] * 2
        + [pl.BlockSpec(memory_space=pltpu.HBM)],
        out_specs=pl.BlockSpec(memory_space=pltpu.HBM),
        scratch_shapes=[
            pltpu.VMEM(shape, jnp.bfloat16),
            pltpu.SemaphoreType.DMA(()),
            pltpu.SemaphoreType.DMA(()),
        ],
        cost_estimate=pl.CostEstimate(
            flops=0, bytes_accessed=12 * 1024 * 1024, transcendentals=0
        ),
    )(coord, count, adj_tiles)


def multiply_kernel(dense_ref, *refs, spots, across, added):
    base_ref = refs[0] if added else None
    piece_refs = refs[added : added + len(spots)]
    out_ref, feats, dense, feat_sems, dense_sems = refs[added + len(spots) :]
    half = (lax.axis_index("z") + across) % 2
    own_y = lax.axis_index("y")
    y_size, z_count, rows, width = feats.shape
    tile = dense.shape[-1]
    per_z = y_size * rows // tile
    copies = []
    for index, (ref, offset) in enumerate(zip(piece_refs, spots)):
        into = feats if offset is None else feats.at[(own_y + offset) % Y_RING]
        copies.append(pltpu.make_async_copy(ref, into, feat_sems.at[index]))
    columns = []
    for z in range(z_count):
        source = dense_ref.at[pl.ds((2 * z + half) * per_z, per_z)]
        columns.append(pltpu.make_async_copy(source, dense.at[z], dense_sems.at[z]))
    for copy in copies + columns:
        copy.start()
    for copy in copies:
        copy.wait()
    per_step = 4
    for at in range(0, z_count, per_step):
        left, right = [], []
        for z in range(at, at + per_step):
            columns[z].wait()
            left += [dense[z, k] for k in range(per_z)]
            right += [feats[k, z] for k in range(y_size)]
        product = jnp.dot(
            jnp.concatenate(left, axis=1),
            jnp.concatenate(right, axis=0),
            preferred_element_type=jnp.float32,
        )
        if at > 0:
            out_ref[...] += product
        elif added:
            out_ref[...] = base_ref[...] + product
        else:
            out_ref[...] = product


def multiply(dense, pieces, spots, across, y_size, base=None):
    z_count, rows, width = pieces[0].shape[-3:]
    tile = dense.shape[-1]
    per_z = y_size * rows // tile
    out = jax.ShapeDtypeStruct((dense.shape[1], width), jnp.float32)
    added = 0 if base is None else 1
    return pl.pallas_call(
        functools.partial(multiply_kernel, spots=spots, across=across, added=added),
        out_shape=out,
        in_specs=[pl.BlockSpec(memory_space=pltpu.HBM)]
        + [pl.BlockSpec(memory_space=pltpu.VMEM)] * added
        + [pl.BlockSpec(memory_space=pltpu.HBM)] * len(pieces),
        out_specs=pl.BlockSpec(memory_space=pltpu.VMEM),
        scratch_shapes=[
            pltpu.VMEM((y_size, z_count, rows, width), jnp.bfloat16),
            pltpu.VMEM((z_count, per_z, dense.shape[1], tile), jnp.bfloat16),
            pltpu.SemaphoreType.DMA((len(pieces),)),
            pltpu.SemaphoreType.DMA((z_count,)),
        ],
        cost_estimate=pl.CostEstimate(
            flops=2 * dense.shape[1] * z_count * y_size * rows * width,
            bytes_accessed=6 * 1024 * 1024,
            transcendentals=0,
        ),
    )(dense, *([base] if added else []), *pieces)


def on_device(features, adj_tiles, tile_coord, tile_count, weight):
    tile = adj_tiles.shape[-1]
    rows, width = features.shape
    z_size, y_size = lax.axis_size("z"), lax.axis_size("y")
    row_size = lax.axis_size("row")
    target_count = rows * row_size // tile
    source_count = rows * z_size * y_size // tile
    half_z = z_size // 2
    groups = [[i + 2 * j for j in range(half_z)] for i in range(2)]
    own = lax.all_gather(features, "z", axis=0, axis_index_groups=groups)
    own_all = lax.all_gather(own, "y", axis=0)
    quarter = half_z // 2
    other = jnp.concatenate(
        [ring_shift(own[:quarter], "z", 1), ring_shift(own[quarter:], "z", -1)], axis=0
    )
    previous = ring_shift(other, "y", 1)
    following = ring_shift(other, "y", -1)
    opposite = ring_shift(following, "y", -1)

    dense = spread(adj_tiles[0, 0], tile_coord[0, 0], tile_count[0], target_count, source_count)
    first = multiply(dense, [own_all], [None], 0, y_size)
    partial_value = multiply(
        dense,
        [other, previous, following, opposite],
        [0, y_size - 1, 1, 2],
        1,
        y_size,
        first,
    )
    parts = lax.all_to_all(
        partial_value.reshape(row_size, rows, width), "row", 0, 0, tiled=True
    )
    hidden = jnp.sum(parts, axis=0).astype(jnp.bfloat16)
    mixed = jnp.dot(hidden, weight, preferred_element_type=jnp.float32)
    return jax.nn.relu(mixed).astype(jnp.bfloat16)


def solution(mesh):
    devices = mesh.devices
    split = Mesh(
        devices.reshape(devices.shape[0], devices.shape[1] // Y_RING, Y_RING),
        ("row", "z", "y"),
    )
    col = ("z", "y")
    return jax.shard_map(
        on_device,
        mesh=split,
        in_specs=(
            P(("row", "z", "y"), None),
            P("row", col, None, None, None),
            P("row", col, None),
            P("row", col),
            P(),
        ),
        out_specs=P(("z", "y", "row"), None),
        check_vma=False,
    )
```

time: 130 us -> 149 us (1.15)
  waiting for transfers between devices: 10.5 us -> 30.5 us
  between operations: 0.82 us -> 14.2 us
  starting transfers between devices: 31.3 us -> 18.1 us
  Pallas kernels: 9.59 us -> 20.5 us
  blocking collectives: 71.9 us -> 61.6 us
  local copies, waits for them, and re-layouts: 4.84 us -> 2.75 us
    all_gather x0 -> x1, waiting for transfers between devices: none -> 23 us  [on_device(): own_all = lax.all_gather(own, 'y', axis=0)]
    ppermute x10 -> x5, starting transfers between devices: 31.3 us -> 18.1 us  [ring_shift(): lax.ppermute(value, axis, [(i, (i + step) % size) for i in range(size)])]
    all_to_all x1, blocking collectives: 26.5 us -> 13.7 us  [on_device(): lax.all_to_all(partial_value.reshape(row_size, rows, width), 'row', 0, 0,...]
    pallas_call x1 -> x3, Pallas kernels: 9.59 us -> 20.5 us  [the longest x2 14.5 us: multiply(): pl.pallas_call(functools.partial(multiply_kernel, spots=spots, across=acr...]
    ppermute x10 -> x5, waiting for transfers between devices: 10.5 us -> 7.47 us  [ring_shift(): lax.ppermute(value, axis, [(i, (i + step) % size) for i in range(size)])]
    all_gather x1, blocking collectives: 45.3 us -> 47.9 us  [on_device(): own = lax.all_gather(features, 'z', axis=0, axis_index_groups=groups)]
    slice x5 -> x1, local copies, waits for them, and re-layouts: 2.9 us -> 1.07 us  [on_device(): own[quarter:]]
  transfers between devices with their start and end apart: 10 -> 6, of which waited for: 4 -> 4; matrix products, arithmetic and copies ran while one was open for 2% -> 1% of each run, Pallas kernels for 0% -> 9%
where the time goes in v2:
time: 149 us; the launch traced here: 148 us
  blocking collectives  61.6 us (41%)
  waiting for transfers between devices  30.5 us (20%)
  Pallas kernels  20.5 us (14%)
  starting transfers between devices  18.1 us (12%)
  between operations  14.2 us (10%)
  local copies, waits for them, and re-layouts  2.75 us (2%)
    all_gather x1, blocking collectives, on_device(): own = lax.all_gather(features, 'z', axis=0, axis_index_groups=groups)  47.9 us
    all_gather x1, waiting for transfers between devices, on_device(): own_all = lax.all_gather(own, 'y', axis=0)  23 us
    ppermute x5, starting transfers between devices, ring_shift(): lax.ppermute(value, axis, [(i, (i + step) % size) for i in range(size)])  18.1 us
    pallas_call x2, Pallas kernels, multiply(): pl.pallas_call(functools.partial(multiply_kernel, spots=spots, across=acr...  14.5 us
    all_to_all x1, blocking collectives, on_device(): lax.all_to_all(partial_value.reshape(row_size, rows, width), 'row', 0, 0,...  13.7 us
    ppermute x5, waiting for transfers between devices, ring_shift(): lax.ppermute(value, axis, [(i, (i + step) % size) for i in range(size)])  7.47 us
    pallas_call x1, Pallas kernels, spread(): pl.pallas_call(functools.partial(spread_kernel, source_count=source_count...  6 us
  transfers between devices with their start and end apart: 6, of which 4 were waited for; matrix products, arithmetic and copies ran while one was open for 1% of the time, Pallas kernels for 9%

profile of v2, /device:TPU:1, one launch (start us, length us, event | category | flops | bytes accessed | tf_op | source)
XLA Modules:
  0.0 148.4 jit_solution(17490832821967929614)
XLA Ops:
  6.5 0.0 copy-start
  6.5 0.0 all-gather.4.cloned.1.call-start
  6.5 47.9 %all-gather = bf16[1024,256]{1,0:T(8,128)(2,1)} all-gather(bf16[64,256]{1,0:T(8,128)(2,1)} %param.5), channel_id=2, replica_groups={{0,8,16,24,32,40,48,56,64,72,80,88,96,104,112,120},{4,12,20,28,36,44,52..., dimensions={0}, use_global_device_ids=true | all-gather | bytes 557056 | tf_op jit(solution)/shard_map/all_gather | solution.py:144
  54.4 0.0 all-gather.4.cloned.1.call-update
  54.4 1.1 fusion.2
  55.5 2.7 %collective-permute-start = (bf16[8,64,256]{2,1,0:T(8,128)(2,1)S(1)}, bf16[8,64,256]{2,1,0:T(8,128)(2,1)S(1)}, u32[]{:S(2)}, u32[]{:S(2)}) collective-permute-start(bf16[8,64,256]{2,1,0:T(8,128)(2,1)S(1)} %bitcast.16), channel_id=1, source_target_pairs={{0,4},{4,8},{8,12},{12,16},{16,20},{20,24},{24,28},{28,32},{32,36}... | collective-permute-start | bytes 786440 | tf_op jit(solution)/shard_map/ppermute | solution.py:15
  58.2 3.8 %collective-permute-start.1 = (bf16[8,64,256]{2,1,0:T(8,128)(2,1)S(1)}, bf16[8,64,256]{2,1,0:T(8,128)(2,1)S(1)}, u32[]{:S(2)}, u32[]{:S(2)}) collective-permute-start(bf16[8,64,256]{2,1,0:T(8,128)(2,1)S(1)} %bitcast.15), channel_id=1, source_target_pairs={{0,124},{4,0},{8,4},{12,8},{16,12},{20,16},{24,20},{28,24},{32,28}... | collective-permute-start | bytes 786440 | tf_op jit(solution)/shard_map/ppermute | solution.py:15
  62.0 2.0 %collective-permute-done = bf16[8,64,256]{2,1,0:T(8,128)(2,1)S(1)} collective-permute-done((bf16[8,64,256]{2,1,0:T(8,128)(2,1)S(1)}, bf16[8,64,256]{2,1,0:T(8,128)(2,1)S(1)}, u32[]{:S(2)}, u32[]{:S(2)}) %collective-permute-start) | collective-permute-done | bytes 262176 | tf_op jit(solution)/shard_map/ppermute | solution.py:15
  64.0 1.3 collective-permute-done.1
  65.4 0.0 copy-start.1
  65.4 4.6 %collective-permute-start.3 = (bf16[16,64,256]{2,1,0:T(8,128)(2,1)S(1)}, bf16[16,64,256]{2,1,0:T(8,128)(2,1)S(1)}, u32[]{:S(2)}, u32[]{:S(2)}) collective-permute-start(bf16[16,64,256]{2,1,0:T(8,128)(2,1)S(1)} %constant_dynamic-update-slice_fusion.refs_1_), channel_id=1, source_target_pairs={{0,3},{1,0},{2,1},{3,2},{4,7},{5,4},{6,5},{7,6},{8,11},{9,8},{10,9... | collective-permute-start | bytes 1572872 | tf_op jit(solution)/shard_map/ppermute | solution.py:15
  70.0 1.9 %collective-permute-start.2 = (bf16[16,64,256]{2,1,0:T(8,128)(2,1)S(1)}, bf16[16,64,256]{2,1,0:T(8,128)(2,1)S(1)}, u32[]{:S(2)}, u32[]{:S(2)}) collective-permute-start(bf16[16,64,256]{2,1,0:T(8,128)(2,1)S(1)} %constant_dynamic-update-slice_fusion.refs_1_), channel_id=1, source_target_pairs={{0,1},{1,2},{2,3},{3,0},{4,5},{5,6},{6,7},{7,4},{8,9},{9,10},{10,1... | collective-permute-start | bytes 1572872 | tf_op jit(solution)/shard_map/ppermute | solution.py:15
  71.9 4.2 %collective-permute-done.3.refs_3_ = bf16[16,64,256]{2,1,0:T(8,128)(2,1)S(1)} collective-permute-done((bf16[16,64,256]{2,1,0:T(8,128)(2,1)S(1)}, bf16[16,64,256]{2,1,0:T(8,128)(2,1)S(1)}, u32[]{:S(2)}, u32[]{:S(2)}) %collective-permute-start.3) | collective-permute-done | bytes 524320 | tf_op jit(solution)/shard_map/ppermute | solution.py:15
  76.1 0.0 copy-start.2
  76.1 5.0 %collective-permute-start.4 = (bf16[16,64,256]{2,1,0:T(8,128)(2,1)S(1)}, bf16[16,64,256]{2,1,0:T(8,128)(2,1)S(1)}, u32[]{:S(2)}, u32[]{:S(2)}) collective-permute-start(bf16[16,64,256]{2,1,0:T(8,128)(2,1)S(1)} %collective-permute-done.3.refs_3_), channel_id=1, source_target_pairs={{0,3},{1,0},{2,1},{3,2},{4,7},{5,4},{6,5},{7,6},{8,11},{9,8},{10,9... | collective-permute-start | bytes 1572872 | tf_op jit(solution)/shard_map/ppermute | solution.py:15
  81.8 6.0 %shard_map.55.dense_ref = bf16[64,512,128]{2,1,0:T(8,128)(2,1)} custom-call(s32[96]{0:T(128)} %bitcast.17, s32[1]{0:T(128)} %bitcast.10.count_ref, bf16[96,128,128]{2,1,0:T(8,128)(2,1)} %bitcast.12), custom_call_target="tpu_custom_call" | custom-call | bytes 12582912 | tf_op jit(solution)/shard_map/pallas_call | solution.py:50
  87.8 0.0 copy-done.1
  87.8 0.0 copy-done.2
  87.8 23.0 %all-gather.4.cloned.1.call-done = bf16[64,64,256]{2,1,0:T(8,128)(2,1)} async-done(((bf16[16,64,256]{2,1,0:T(8,128)(2,1)}), bf16[64,64,256]{2,1,0:T(8,128)(2,1)}) %all-gather.4.cloned.1.call-update) | async-done | bytes 2097168 | tf_op jit(solution)/shard_map/all_gather | solution.py:145
  110.8 6.8 %shard_map.56.refs_0_ = f32[512,256]{1,0:T(8,128)} custom-call(bf16[64,512,128]{2,1,0:T(8,128)(2,1)} %shard_map.55.dense_ref, bf16[4,16,64,256]{3,2,1,0:T(8,128)(2,1)} %bitcast.14), custom_call_target="tpu_custom_call" | custom-call | flops 1073741824 | bytes 6291456 | tf_op jit(solution)/shard_map/pallas_call | solution.py:114
  117.6 0.0 collective-permute-done.2.refs_2_
  117.6 0.0 copy-start.3
  117.6 0.0 collective-permute-done.4.refs_4_
  117.6 0.8 copy-done.3
  118.4 0.0 copy-start.4
  118.4 0.8 copy-done.4
  119.3 7.8 %shard_map.57 = f32[512,256]{1,0:T(8,128)} custom-call(bf16[64,512,128]{2,1,0:T(8,128)(2,1)} %shard_map.55.dense_ref, f32[512,256]{1,0:T(8,128)} %shard_map.56.refs_0_, bf16[16,64,256]{2,1,0:T(8,128)(2,1)} %copy-done.1, bf16[16,64,256]{2,1,0:T(8,128)(2,1)} %copy-done.3, bf16[16,64,256]{2,1,0:T(8,128)(2,1)} %copy-done.2, bf16[16,64,256]{2,1,0:T(8,128)(2,1)} %copy-done.4), custom_call_target="tpu_custom_call" | custom-call | flops 1073741824 | bytes 6291456 | tf_op jit(solution)/shard_map/pallas_call | solution.py:114
  127.0 13.7 %all_to_all.5 = f32[8,64,256]{2,1,0:T(8,128)S(1)} all-to-all(f32[8,64,256]{2,1,0:T(8,128)} %bitcast.13), channel_id=1, replica_groups=mesh['row'=8,'z'=32,'y'=4] {'row'}, dimensions={0} | all-to-all | bytes 1048576 | tf_op jit(solution)/shard_map/all_to_all | solution.py:164
  140.8 0.0 copy-done
  140.8 0.8 fusion
  (3 shorter events, 0.1 us)
Async XLA Ops:
  6.5 134.3 %copy-start = (bf16[256,256]{1,0:T(8,128)(2,1)S(1)}, bf16[256,256]{1,0:T(8,128)(2,1)}, u32[]{:S(2)}) copy-start(bf16[256,256]{1,0:T(8,128)(2,1)} %param.9) | copy-start | bytes 393220
  6.5 104.3 %all-gather.4.cloned.1.call-start = ((), (), s32[]{:S(2)}) async-start(), calls=%async_computation.1 | async-start | bytes 2621440 | tf_op jit(solution)/shard_map/all_gather | solution.py:145
  55.5 8.5 %collective-permute-start = (bf16[8,64,256]{2,1,0:T(8,128)(2,1)S(1)}, bf16[8,64,256]{2,1,0:T(8,128)(2,1)S(1)}, u32[]{:S(2)}, u32[]{:S(2)}) collective-permute-start(bf16[8,64,256]{2,1,0:T(8,128)(2,1)S(1)} %bitcast.16), channel_id=1, source_target_pairs={{0,4},{4,8},{8,12},{12,16},{16,20},{20,24},{24,28},{28,32},{32,36}... | collective-permute-start | bytes 786440 | tf_op jit(solution)/shard_map/ppermute | solution.py:15
  58.2 7.1 %collective-permute-start.1 = (bf16[8,64,256]{2,1,0:T(8,128)(2,1)S(1)}, bf16[8,64,256]{2,1,0:T(8,128)(2,1)S(1)}, u32[]{:S(2)}, u32[]{:S(2)}) collective-permute-start(bf16[8,64,256]{2,1,0:T(8,128)(2,1)S(1)} %bitcast.15), channel_id=1, source_target_pairs={{0,124},{4,0},{8,4},{12,8},{16,12},{20,16},{24,20},{28,24},{32,28}... | collective-permute-start | bytes 786440 | tf_op jit(solution)/shard_map/ppermute | solution.py:15
  65.4 22.4 %copy-start.1 = (bf16[16,64,256]{2,1,0:T(8,128)(2,1)}, bf16[16,64,256]{2,1,0:T(8,128)(2,1)S(1)}, u32[]{:S(2)}) copy-start(bf16[16,64,256]{2,1,0:T(8,128)(2,1)S(1)} %constant_dynamic-update-slice_fusion.refs_1_) | copy-start | bytes 1572868
  65.4 10.8 %collective-permute-start.3 = (bf16[16,64,256]{2,1,0:T(8,128)(2,1)S(1)}, bf16[16,64,256]{2,1,0:T(8,128)(2,1)S(1)}, u32[]{:S(2)}, u32[]{:S(2)}) collective-permute-start(bf16[16,64,256]{2,1,0:T(8,128)(2,1)S(1)} %constant_dynamic-update-slice_fusion.refs_1_), channel_id=1, source_target_pairs={{0,3},{1,0},{2,1},{3,2},{4,7},{5,4},{6,5},{7,6},{8,11},{9,8},{10,9... | collective-permute-start | bytes 1572872 | tf_op jit(solution)/shard_map/ppermute | solution.py:15
  70.0 47.6 %collective-permute-start.2 = (bf16[16,64,256]{2,1,0:T(8,128)(2,1)S(1)}, bf16[16,64,256]{2,1,0:T(8,128)(2,1)S(1)}, u32[]{:S(2)}, u32[]{:S(2)}) collective-permute-start(bf16[16,64,256]{2,1,0:T(8,128)(2,1)S(1)} %constant_dynamic-update-slice_fusion.refs_1_), channel_id=1, source_target_pairs={{0,1},{1,2},{2,3},{3,0},{4,5},{5,6},{6,7},{7,4},{8,9},{9,10},{10,1... | collective-permute-start | bytes 1572872 | tf_op jit(solution)/shard_map/ppermute | solution.py:15
  76.1 11.7 %copy-start.2 = (bf16[16,64,256]{2,1,0:T(8,128)(2,1)}, bf16[16,64,256]{2,1,0:T(8,128)(2,1)S(1)}, u32[]{:S(2)}) copy-start(bf16[16,64,256]{2,1,0:T(8,128)(2,1)S(1)} %collective-permute-done.3.refs_3_) | copy-start | bytes 1572868
  76.1 41.5 %collective-permute-start.4 = (bf16[16,64,256]{2,1,0:T(8,128)(2,1)S(1)}, bf16[16,64,256]{2,1,0:T(8,128)(2,1)S(1)}, u32[]{:S(2)}, u32[]{:S(2)}) collective-permute-start(bf16[16,64,256]{2,1,0:T(8,128)(2,1)S(1)} %collective-permute-done.3.refs_3_), channel_id=1, source_target_pairs={{0,3},{1,0},{2,1},{3,2},{4,7},{5,4},{6,5},{7,6},{8,11},{9,8},{10,9... | collective-permute-start | bytes 1572872 | tf_op jit(solution)/shard_map/ppermute | solution.py:15
  117.6 0.8 copy-start.3
  118.4 0.8 copy-start.4
Sparse Core Ops, SparseCore 0:
  54.6 56.2 all-gather.3

commit v3 on v2

v3 whole, which is shorter than its diff:
```python
import functools

import jax
import jax.numpy as jnp
from jax import lax
from jax.experimental import pallas as pl
from jax.experimental.pallas import tpu as pltpu
from jax.sharding import Mesh, PartitionSpec as P

Y_RING = 4
VMEM_GRANT = 24 * 1024 * 1024


def ring_shift(value, axis, step):
    size = lax.axis_size(axis)
    return lax.ppermute(value, axis, [(i, (i + step) % size) for i in range(size)])


def spread_kernel(coord_ref, count_ref, adj_ref, dense, sem, *, source_count, tile):
    def clear(index, carry):
        dense[index] = jnp.zeros(dense.shape[1:], dense.dtype)
        return carry

    lax.fori_loop(0, source_count, clear, 0)
    live = count_ref[0]

    def place(slot, carry):
        target = coord_ref[slot] // source_count
        source = coord_ref[slot] % source_count
        rows = pl.ds(pl.multiple_of(target * tile, tile), tile)
        pltpu.make_async_copy(adj_ref.at[slot], dense.at[source, rows], sem).start()
        return carry

    lax.fori_loop(0, live, place, 0)

    def arrived(slot, carry):
        pltpu.make_async_copy(adj_ref.at[0], dense.at[0, pl.ds(0, tile)], sem).wait()
        return carry

    lax.fori_loop(0, live, arrived, 0)


def spread(adj_tiles, coord, count, target_count, source_count):
    tile = adj_tiles.shape[-1]
    return pl.pallas_call(
        functools.partial(spread_kernel, source_count=source_count, tile=tile),
        out_shape=jax.ShapeDtypeStruct(
            (source_count, target_count * tile, tile), jnp.bfloat16
        ),
        in_specs=[pl.BlockSpec(memory_space=pltpu.SMEM)] * 2
        + [pl.BlockSpec(memory_space=pltpu.HBM)],
        out_specs=pl.BlockSpec(memory_space=pltpu.VMEM),
        scratch_shapes=[pltpu.SemaphoreType.DMA(())],
        compiler_params=pltpu.CompilerParams(vmem_limit_bytes=VMEM_GRANT),
        cost_estimate=pl.CostEstimate(
            flops=0, bytes_accessed=12 * 1024 * 1024, transcendentals=0
        ),
    )(coord, count, adj_tiles)


def multiply_kernel(dense, *refs, spots, across, added):
    base_ref = refs[0] if added else None
    piece_refs = refs[added : added + len(spots)]
    out_ref, feats = refs[added + len(spots) :]
    half = (lax.axis_index("z") + across) % 2
    own_y = lax.axis_index("y")
    y_size, z_count, rows, width = feats.shape
    tile = dense.shape[-1]
    per_z = y_size * rows // tile
    for ref, offset in zip(piece_refs, spots):
        feats[(own_y + offset) % y_size] = ref[...]
    per_step = 4
    for at in range(0, z_count, per_step):
        left, right = [], []
        for z in range(at, at + per_step):
            left += [dense[(2 * z + half) * per_z + k] for k in range(per_z)]
            right += [feats[k, z] for k in range(y_size)]
        product = jnp.dot(
            jnp.concatenate(left, axis=1),
            jnp.concatenate(right, axis=0),
            preferred_element_type=jnp.float32,
        )
        if at > 0:
            out_ref[...] += product
        elif added:
            out_ref[...] = base_ref[...] + product
        else:
            out_ref[...] = product


def multiply(dense, pieces, spots, across, base=None):
    z_count, rows, width = pieces[0].shape
    added = 0 if base is None else 1
    arrays = [dense] + ([base] if added else []) + pieces
    return pl.pallas_call(
        functools.partial(multiply_kernel, spots=spots, across=across, added=added),
        out_shape=jax.ShapeDtypeStruct((dense.shape[1], width), jnp.float32),
        in_specs=[pl.BlockSpec(memory_space=pltpu.VMEM)] * len(arrays),
        out_specs=pl.BlockSpec(memory_space=pltpu.VMEM),
        scratch_shapes=[pltpu.VMEM((len(spots), z_count, rows, width), jnp.bfloat16)],
        compiler_params=pltpu.CompilerParams(vmem_limit_bytes=VMEM_GRANT),
        cost_estimate=pl.CostEstimate(
            flops=2 * dense.shape[1] * z_count * len(spots) * rows * width,
            bytes_accessed=6 * 1024 * 1024,
            transcendentals=0,
        ),
    )(*arrays)


def on_device(features, adj_tiles, tile_coord, tile_count, weight):
    tile = adj_tiles.shape[-1]
    rows, width = features.shape
    z_size, y_size = lax.axis_size("z"), lax.axis_size("y")
    row_size = lax.axis_size("row")
    target_count = rows * row_size // tile
    source_count = rows * z_size * y_size // tile
    half_z = z_size // 2
    groups = [[i + 2 * j for j in range(half_z)] for i in range(2)]
    own = lax.all_gather(features, "z", axis=0, axis_index_groups=groups)
    spots = [2, 1, y_size - 1, 0]
    near = [ring_shift(own, "y", -spot) for spot in spots[:-1]] + [own]
    far = [ring_shift(piece, "z", (-1) ** at) for at, piece in enumerate(near)]

    dense = spread(adj_tiles[0, 0], tile_coord[0, 0], tile_count[0], target_count, source_count)
    first = multiply(dense, near, spots, 0)
    partial_value = multiply(dense, far, spots, 1, first)
    parts = lax.all_to_all(
        partial_value.reshape(row_size, rows, width), "row", 0, 0, tiled=True
    )
    hidden = jnp.sum(parts, axis=0).astype(jnp.bfloat16)
    mixed = jnp.dot(hidden, weight, preferred_element_type=jnp.float32)
    return jax.nn.relu(mixed).astype(jnp.bfloat16)


def solution(mesh):
    devices = mesh.devices
    split = Mesh(
        devices.reshape(devices.shape[0], devices.shape[1] // Y_RING, Y_RING),
        ("row", "z", "y"),
    )
    col = ("z", "y")
    return jax.shard_map(
        on_device,
        mesh=split,
        in_specs=(
            P(("row", "z", "y"), None),
            P("row", col, None, None, None),
            P("row", col, None),
            P("row", col),
            P(),
        ),
        out_specs=P(("z", "y", "row"), None),
        check_vma=False,
    )
```

time: 149 us -> 109 us (0.73)
  waiting for transfers between devices: 30.5 us -> 13.8 us
  between operations: 14.2 us -> 0.79 us
  Pallas kernels: 20.5 us -> 7.28 us
  starting transfers between devices: 18.1 us -> 20.6 us
    all_gather x1 -> x0, waiting for transfers between devices: 23 us -> none  [on_device(): own_all = lax.all_gather(own, 'y', axis=0)]
    pallas_call x2, Pallas kernels: 14.5 us -> 2.8 us  [multiply(): pl.pallas_call(functools.partial(multiply_kernel, spots=spots, across=acr...]
    ppermute x5 -> x7, waiting for transfers between devices: 7.47 us -> 13.8 us  [ring_shift(): lax.ppermute(value, axis, [(i, (i + step) % size) for i in range(size)])]
    all_to_all x1, blocking collectives: 13.7 us -> 17.5 us  [on_device(): lax.all_to_all(partial_value.reshape(row_size, rows, width), 'row', 0, 0,...]
    all_gather x1, blocking collectives: 47.9 us -> 45.3 us  [on_device(): own = lax.all_gather(features, 'z', axis=0, axis_index_groups=groups)]
    ppermute x5 -> x7, starting transfers between devices: 18.1 us -> 20.6 us  [ring_shift(): lax.ppermute(value, axis, [(i, (i + step) % size) for i in range(size)])]
    pallas_call x1, Pallas kernels: 6 us -> 4.49 us  [spread(): pl.pallas_call(functools.partial(spread_kernel, source_count=source_count...]
  transfers between devices with their start and end apart: 6 -> 7, of which waited for: 4 -> 2; matrix products, arithmetic and copies ran while one was open for 1% -> 0% of each run, Pallas kernels for 9% -> 5%
where the time goes in v3:
time: 109 us
  blocking collectives  62.9 us (58%)
  starting transfers between devices  20.6 us (19%)
  waiting for transfers between devices  13.8 us (13%)
  Pallas kernels  7.28 us (7%)
  local copies, waits for them, and re-layouts  2.54 us (2%)
    all_gather x1, blocking collectives, on_device(): own = lax.all_gather(features, 'z', axis=0, axis_index_groups=groups)  45.3 us
    ppermute x7, starting transfers between devices, ring_shift(): lax.ppermute(value, axis, [(i, (i + step) % size) for i in range(size)])  20.6 us
    all_to_all x1, blocking collectives, on_device(): lax.all_to_all(partial_value.reshape(row_size, rows, width), 'row', 0, 0,...  17.5 us
    ppermute x7, waiting for transfers between devices, ring_shift(): lax.ppermute(value, axis, [(i, (i + step) % size) for i in range(size)])  13.8 us
    pallas_call x1, Pallas kernels, spread(): pl.pallas_call(functools.partial(spread_kernel, source_count=source_count...  4.49 us
    pallas_call x2, Pallas kernels, multiply(): pl.pallas_call(functools.partial(multiply_kernel, spots=spots, across=acr...  2.8 us
    unnamed x6, local copies, waits for them, and re-layouts  2.54 us
  transfers between devices with their start and end apart: 7, of which 2 were waited for; matrix products, arithmetic and copies ran while one was open for 0% of the time, Pallas kernels for 5%

profile of v3, /device:TPU:1, one launch (start us, length us, event | category | flops | bytes accessed | tf_op | source)
XLA Modules:
  0.0 108.7 jit_solution(864719165441488699)
XLA Ops:
  0.0 0.0 copy-start
  0.0 45.3 %all-gather = bf16[1024,256]{1,0:T(8,128)(2,1)S(1)} all-gather(bf16[64,256]{1,0:T(8,128)(2,1)} %param.5), channel_id=2, replica_groups={{0,8,16,24,32,40,48,56,64,72,80,88,96,104,112,120},{4,12,20,28,36,44,52..., dimensions={0}, use_global_device_ids=true | all-gather | bytes 557056 | tf_op jit(solution)/shard_map/all_gather | solution.py:119
  45.3 4.8 %collective-permute-start = (bf16[16,64,256]{2,1,0:T(8,128)(2,1)S(1)}, bf16[16,64,256]{2,1,0:T(8,128)(2,1)S(1)}, u32[]{:S(2)}, u32[]{:S(2)}) collective-permute-start(bf16[16,64,256]{2,1,0:T(8,128)(2,1)S(1)} %bitcast.10), channel_id=1, source_target_pairs={{0,2},{1,3},{2,0},{3,1},{4,6},{5,7},{6,4},{7,5},{8,10},{9,11},{10,... | collective-permute-start | bytes 1572872 | tf_op jit(solution)/shard_map/ppermute | solution.py:16
  50.1 2.7 %collective-permute-start.1 = (bf16[16,64,256]{2,1,0:T(8,128)(2,1)S(1)}, bf16[16,64,256]{2,1,0:T(8,128)(2,1)S(1)}, u32[]{:S(2)}, u32[]{:S(2)}) collective-permute-start(bf16[16,64,256]{2,1,0:T(8,128)(2,1)S(1)} %bitcast.11), channel_id=1, source_target_pairs={{0,3},{1,0},{2,1},{3,2},{4,7},{5,4},{6,5},{7,6},{8,11},{9,8},{10,9... | collective-permute-start | bytes 1572872 | tf_op jit(solution)/shard_map/ppermute | solution.py:16
  52.8 2.6 %collective-permute-start.2 = (bf16[16,64,256]{2,1,0:T(8,128)(2,1)S(1)}, bf16[16,64,256]{2,1,0:T(8,128)(2,1)S(1)}, u32[]{:S(2)}, u32[]{:S(2)}) collective-permute-start(bf16[16,64,256]{2,1,0:T(8,128)(2,1)S(1)} %bitcast.12), channel_id=1, source_target_pairs={{0,1},{1,2},{2,3},{3,0},{4,5},{5,6},{6,7},{7,4},{8,9},{9,10},{10,1... | collective-permute-start | bytes 1572872 | tf_op jit(solution)/shard_map/ppermute | solution.py:16
  55.4 2.9 %collective-permute-start.6 = (bf16[16,64,256]{2,1,0:T(8,128)(2,1)S(1)}, bf16[16,64,256]{2,1,0:T(8,128)(2,1)S(1)}, u32[]{:S(2)}, u32[]{:S(2)}) collective-permute-start(bf16[16,64,256]{2,1,0:T(8,128)(2,1)S(1)} %bitcast.13), channel_id=1, source_target_pairs={{0,124},{4,0},{8,4},{12,8},{16,12},{20,16},{24,20},{28,24},{32,28}... | collective-permute-start | bytes 1572872 | tf_op jit(solution)/shard_map/ppermute | solution.py:16
  58.4 0.0 collective-permute-done.refs_0_
  58.4 2.3 %collective-permute-start.3 = (bf16[16,64,256]{2,1,0:T(8,128)(2,1)S(1)}, bf16[16,64,256]{2,1,0:T(8,128)(2,1)S(1)}, u32[]{:S(2)}, u32[]{:S(2)}) collective-permute-start(bf16[16,64,256]{2,1,0:T(8,128)(2,1)S(1)} %collective-permute-done.refs_0_), channel_id=1, source_target_pairs={{0,4},{4,8},{8,12},{12,16},{16,20},{20,24},{24,28},{28,32},{32,36}... | collective-permute-start | bytes 1572872 | tf_op jit(solution)/shard_map/ppermute | solution.py:16
  60.7 8.9 %collective-permute-done.1.refs_1_ = bf16[16,64,256]{2,1,0:T(8,128)(2,1)S(1)} collective-permute-done((bf16[16,64,256]{2,1,0:T(8,128)(2,1)S(1)}, bf16[16,64,256]{2,1,0:T(8,128)(2,1)S(1)}, u32[]{:S(2)}, u32[]{:S(2)}) %collective-permute-start.1) | collective-permute-done | bytes 524320 | tf_op jit(solution)/shard_map/ppermute | solution.py:16
  69.6 2.6 %collective-permute-start.4 = (bf16[16,64,256]{2,1,0:T(8,128)(2,1)S(1)}, bf16[16,64,256]{2,1,0:T(8,128)(2,1)S(1)}, u32[]{:S(2)}, u32[]{:S(2)}) collective-permute-start(bf16[16,64,256]{2,1,0:T(8,128)(2,1)S(1)} %collective-permute-done.1.refs_1_), channel_id=1, source_target_pairs={{0,124},{4,0},{8,4},{12,8},{16,12},{20,16},{24,20},{28,24},{32,28}... | collective-permute-start | bytes 1572872 | tf_op jit(solution)/shard_map/ppermute | solution.py:16
  72.2 0.0 collective-permute-done.2.refs_2_
  72.2 2.7 %collective-permute-start.5 = (bf16[16,64,256]{2,1,0:T(8,128)(2,1)S(1)}, bf16[16,64,256]{2,1,0:T(8,128)(2,1)S(1)}, u32[]{:S(2)}, u32[]{:S(2)}) collective-permute-start(bf16[16,64,256]{2,1,0:T(8,128)(2,1)S(1)} %collective-permute-done.2.refs_2_), channel_id=1, source_target_pairs={{0,4},{4,8},{8,12},{12,16},{16,20},{20,24},{24,28},{28,32},{32,36}... | collective-permute-start | bytes 1572872 | tf_op jit(solution)/shard_map/ppermute | solution.py:16
  75.6 0.0 copy-start.1
  75.6 1.9 %copy-done.1 = bf16[1,1,96,128,128]{4,3,2,1,0:T(8,128)(2,1)S(1)} copy-done((bf16[1,1,96,128,128]{4,3,2,1,0:T(8,128)(2,1)S(1)}, bf16[1,1,96,128,128]{4,3,2,1,0:T(8,128)(2,1)}, u32[]{:S(2)}) %copy-start.1) | copy-done | bytes 3145752
  77.5 0.0 copy-start.2
  77.5 0.7 copy-done.2
  78.1 4.5 %shard_map.55.dense = bf16[64,512,128]{2,1,0:T(8,128)(2,1)S(1)} custom-call(s32[96]{0:T(128)S(1)} %bitcast.15, s32[1]{0:T(128)} %bitcast.7.count_ref, bf16[96,128,128]{2,1,0:T(8,128)(2,1)S(1)} %bitcast.8), custom_call_target="tpu_custom_call" | custom-call | bytes 12582912 | tf_op jit(solution)/shard_map/pallas_call | solution.py:45
  82.6 1.4 %shard_map.56.refs_0_ = f32[512,256]{1,0:T(8,128)S(1)} custom-call(bf16[64,512,128]{2,1,0:T(8,128)(2,1)S(1)} %shard_map.55.dense, bf16[16,64,256]{2,1,0:T(8,128)(2,1)S(1)} %collective-permute-done.refs_0_, bf16[16,64,256]{2,1,0:T(8,128)(2,1)S(1)} %collective-permute-done.1.refs_1_, bf16[16,64,256]{2,1,0:T(8,128)(2,1)S(1)} %collective-permute-done.2.refs_2_, ...), custom_call_target="tpu_custom_call" | custom-call | flops 1073741824 | bytes 6291456 | tf_op jit(solution)/shard_map/pallas_call | solution.py:95
  84.0 0.0 collective-permute-done.6.refs_4_
  84.0 0.0 collective-permute-done.3.refs_1_
  84.0 0.0 collective-permute-done.4.refs_2_
  84.1 4.9 %collective-permute-done.5.refs_3_ = bf16[16,64,256]{2,1,0:T(8,128)(2,1)S(1)} collective-permute-done((bf16[16,64,256]{2,1,0:T(8,128)(2,1)S(1)}, bf16[16,64,256]{2,1,0:T(8,128)(2,1)S(1)}, u32[]{:S(2)}, u32[]{:S(2)}) %collective-permute-start.5) | collective-permute-done | bytes 524320 | tf_op jit(solution)/shard_map/ppermute | solution.py:16
  88.9 1.4 %shard_map.57 = f32[512,256]{1,0:T(8,128)S(1)} custom-call(bf16[64,512,128]{2,1,0:T(8,128)(2,1)S(1)} %shard_map.55.dense, f32[512,256]{1,0:T(8,128)S(1)} %shard_map.56.refs_0_, bf16[16,64,256]{2,1,0:T(8,128)(2,1)S(1)} %collective-permute-done.3.refs_1_, bf16[16,64,256]{2,1,0:T(8,128)(2,1)S(1)} %collective-permute-done.4.refs_2_, ...), custom_call_target="tpu_custom_call" | custom-call | flops 1073741824 | bytes 6291456 | tf_op jit(solution)/shard_map/pallas_call | solution.py:95
  90.3 17.5 %all_to_all.5 = f32[8,64,256]{2,1,0:T(8,128)S(1)} all-to-all(f32[8,64,256]{2,1,0:T(8,128)S(1)} %bitcast.9), channel_id=1, replica_groups=mesh['row'=8,'z'=32,'y'=4] {'row'}, dimensions={0} | all-to-all | bytes 1048576 | tf_op jit(solution)/shard_map/all_to_all | solution.py:127
  107.9 0.0 copy-done
  107.9 0.8 fusion
  (1 shorter events, 0.0 us)
Async XLA Ops:
  0.0 107.9 %copy-start = (bf16[256,256]{1,0:T(8,128)(2,1)S(1)}, bf16[256,256]{1,0:T(8,128)(2,1)}, u32[]{:S(2)}) copy-start(bf16[256,256]{1,0:T(8,128)(2,1)} %param.9) | copy-start | bytes 393220
  45.3 13.0 %collective-permute-start = (bf16[16,64,256]{2,1,0:T(8,128)(2,1)S(1)}, bf16[16,64,256]{2,1,0:T(8,128)(2,1)S(1)}, u32[]{:S(2)}, u32[]{:S(2)}) collective-permute-start(bf16[16,64,256]{2,1,0:T(8,128)(2,1)S(1)} %bitcast.10), channel_id=1, source_target_pairs={{0,2},{1,3},{2,0},{3,1},{4,6},{5,7},{6,4},{7,5},{8,10},{9,11},{10,... | collective-permute-start | bytes 1572872 | tf_op jit(solution)/shard_map/ppermute | solution.py:16
  50.1 19.5 %collective-permute-start.1 = (bf16[16,64,256]{2,1,0:T(8,128)(2,1)S(1)}, bf16[16,64,256]{2,1,0:T(8,128)(2,1)S(1)}, u32[]{:S(2)}, u32[]{:S(2)}) collective-permute-start(bf16[16,64,256]{2,1,0:T(8,128)(2,1)S(1)} %bitcast.11), channel_id=1, source_target_pairs={{0,3},{1,0},{2,1},{3,2},{4,7},{5,4},{6,5},{7,6},{8,11},{9,8},{10,9... | collective-permute-start | bytes 1572872 | tf_op jit(solution)/shard_map/ppermute | solution.py:16
  52.8 19.4 %collective-permute-start.2 = (bf16[16,64,256]{2,1,0:T(8,128)(2,1)S(1)}, bf16[16,64,256]{2,1,0:T(8,128)(2,1)S(1)}, u32[]{:S(2)}, u32[]{:S(2)}) collective-permute-start(bf16[16,64,256]{2,1,0:T(8,128)(2,1)S(1)} %bitcast.12), channel_id=1, source_target_pairs={{0,1},{1,2},{2,3},{3,0},{4,5},{5,6},{6,7},{7,4},{8,9},{9,10},{10,1... | collective-permute-start | bytes 1572872 | tf_op jit(solution)/shard_map/ppermute | solution.py:16
  55.4 28.6 %collective-permute-start.6 = (bf16[16,64,256]{2,1,0:T(8,128)(2,1)S(1)}, bf16[16,64,256]{2,1,0:T(8,128)(2,1)S(1)}, u32[]{:S(2)}, u32[]{:S(2)}) collective-permute-start(bf16[16,64,256]{2,1,0:T(8,128)(2,1)S(1)} %bitcast.13), channel_id=1, source_target_pairs={{0,124},{4,0},{8,4},{12,8},{16,12},{20,16},{24,20},{28,24},{32,28}... | collective-permute-start | bytes 1572872 | tf_op jit(solution)/shard_map/ppermute | solution.py:16
  58.4 25.7 %collective-permute-start.3 = (bf16[16,64,256]{2,1,0:T(8,128)(2,1)S(1)}, bf16[16,64,256]{2,1,0:T(8,128)(2,1)S(1)}, u32[]{:S(2)}, u32[]{:S(2)}) collective-permute-start(bf16[16,64,256]{2,1,0:T(8,128)(2,1)S(1)} %collective-permute-done.refs_0_), channel_id=1, source_target_pairs={{0,4},{4,8},{8,12},{12,16},{16,20},{20,24},{24,28},{28,32},{32,36}... | collective-permute-start | bytes 1572872 | tf_op jit(solution)/shard_map/ppermute | solution.py:16
  69.6 14.4 %collective-permute-start.4 = (bf16[16,64,256]{2,1,0:T(8,128)(2,1)S(1)}, bf16[16,64,256]{2,1,0:T(8,128)(2,1)S(1)}, u32[]{:S(2)}, u32[]{:S(2)}) collective-permute-start(bf16[16,64,256]{2,1,0:T(8,128)(2,1)S(1)} %collective-permute-done.1.refs_1_), channel_id=1, source_target_pairs={{0,124},{4,0},{8,4},{12,8},{16,12},{20,16},{24,20},{28,24},{32,28}... | collective-permute-start | bytes 1572872 | tf_op jit(solution)/shard_map/ppermute | solution.py:16
  72.2 16.7 %collective-permute-start.5 = (bf16[16,64,256]{2,1,0:T(8,128)(2,1)S(1)}, bf16[16,64,256]{2,1,0:T(8,128)(2,1)S(1)}, u32[]{:S(2)}, u32[]{:S(2)}) collective-permute-start(bf16[16,64,256]{2,1,0:T(8,128)(2,1)S(1)} %collective-permute-done.2.refs_2_), channel_id=1, source_target_pairs={{0,4},{4,8},{8,12},{12,16},{16,20},{20,24},{24,28},{28,32},{32,36}... | collective-permute-start | bytes 1572872 | tf_op jit(solution)/shard_map/ppermute | solution.py:16
  75.6 1.9 %copy-start.1 = (bf16[1,1,96,128,128]{4,3,2,1,0:T(8,128)(2,1)S(1)}, bf16[1,1,96,128,128]{4,3,2,1,0:T(8,128)(2,1)}, u32[]{:S(2)}) copy-start(bf16[1,1,96,128,128]{4,3,2,1,0:T(8,128)(2,1)} %param.6) | copy-start | bytes 9437188
  77.5 0.7 copy-start.2

commit v4 on v3

--- a/solution.py
+++ b/solution.py
@@ -17,36 +17,52 @@
 
 
 def spread_kernel(coord_ref, count_ref, adj_ref, dense, sem, *, source_count, tile):
+    slots = adj_ref.shape[2]
+    group = 8
+
     def clear(index, carry):
         dense[index] = jnp.zeros(dense.shape[1:], dense.dtype)
         return carry
 
     lax.fori_loop(0, source_count, clear, 0)
-    live = count_ref[0]
+    live = count_ref[0, 0]
 
-    def place(slot, carry):
-        target = coord_ref[slot] // source_count
-        source = coord_ref[slot] % source_count
+    def place(slot):
+        spot = coord_ref[0, 0, slot]
+        target = lax.div(spot, source_count)
+        source = lax.rem(spot, source_count)
         rows = pl.ds(pl.multiple_of(target * tile, tile), tile)
-        pltpu.make_async_copy(adj_ref.at[slot], dense.at[source, rows], sem).start()
+        pltpu.make_async_copy(adj_ref.at[0, 0, slot], dense.at[source, rows], sem).start()
+
+    def place_group(at, carry):
+        for i in range(group):
+            place(at * group + i)
         return carry
 
-    lax.fori_loop(0, live, place, 0)
-
-    def arrived(slot, carry):
-        pltpu.make_async_copy(adj_ref.at[0], dense.at[0, pl.ds(0, tile)], sem).wait()
+    def place_one(slot, carry):
+        place(slot)
         return carry
 
-    lax.fori_loop(0, live, arrived, 0)
+    whole = lax.div(live, group)
+    lax.fori_loop(0, whole, place_group, 0)
+    lax.fori_loop(whole * group, live, place_one, 0)
+    amount = 1
+    while amount <= slots:
+
+        @pl.when(lax.rem(lax.div(live, amount), 2) == 1)
+        def arrived():
+            some = adj_ref.at[0, 0, pl.ds(0, amount)]
+            pltpu.make_async_copy(some, some, sem).wait()
+
+        amount *= 2
 
 
 def spread(adj_tiles, coord, count, target_count, source_count):
     tile = adj_tiles.shape[-1]
+    shape = (source_count, target_count * tile, tile)
     return pl.pallas_call(
         functools.partial(spread_kernel, source_count=source_count, tile=tile),
-        out_shape=jax.ShapeDtypeStruct(
-            (source_count, target_count * tile, tile), jnp.bfloat16
-        ),
+        out_shape=jax.ShapeDtypeStruct(shape, jnp.bfloat16),
         in_specs=[pl.BlockSpec(memory_space=pltpu.SMEM)] * 2
         + [pl.BlockSpec(memory_space=pltpu.HBM)],
         out_specs=pl.BlockSpec(memory_space=pltpu.VMEM),
@@ -55,7 +71,11 @@
         cost_estimate=pl.CostEstimate(
             flops=0, bytes_accessed=12 * 1024 * 1024, transcendentals=0
         ),
-    )(coord, count, adj_tiles)
+    )(
+        pltpu.with_memory_space_constraint(coord, pltpu.HBM),
+        count,
+        pltpu.with_memory_space_constraint(adj_tiles, pltpu.HBM),
+    )
 
 
 def multiply_kernel(dense, *refs, spots, across, added):
@@ -121,7 +141,7 @@
     near = [ring_shift(own, "y", -spot) for spot in spots[:-1]] + [own]
     far = [ring_shift(piece, "z", (-1) ** at) for at, piece in enumerate(near)]
 
-    dense = spread(adj_tiles[0, 0], tile_coord[0, 0], tile_count[0], target_count, source_count)
+    dense = spread(adj_tiles, tile_coord, tile_count, target_count, source_count)
     first = multiply(dense, near, spots, 0)
     partial_value = multiply(dense, far, spots, 1, first)
     parts = lax.all_to_all(

time: 109 us -> 109 us (level)
  waiting for transfers between devices: 13.8 us -> 17.8 us
  local copies, waits for them, and re-layouts: 2.54 us -> 0.01 us
  Pallas kernels: 7.28 us -> 5.89 us
    ppermute x7, waiting for transfers between devices: 13.8 us -> 17.8 us  [ring_shift(): lax.ppermute(value, axis, [(i, (i + step) % size) for i in range(size)])]
    unnamed x6 -> x2, local copies, waits for them, and re-layouts: 2.54 us -> 0.01 us
    pallas_call x1, Pallas kernels: 4.49 us -> 3.09 us  [spread(): pl.pallas_call(functools.partial(spread_kernel, source_count=source_count...]
  transfers between devices with their start and end apart: 7 -> 7, of which waited for: 2 -> 2; matrix products, arithmetic and copies ran while one was open for 0% -> 0% of each run, Pallas kernels for 5% -> 4%
where the time goes in v4:
time: 109 us; the launch traced here: 108 us
  blocking collectives  62.4 us (57%)
  starting transfers between devices  20.6 us (19%)
  waiting for transfers between devices  17.8 us (16%)
  Pallas kernels  5.89 us (5%)
    all_gather x1, blocking collectives, on_device(): own = lax.all_gather(features, 'z', axis=0, axis_index_groups=groups)  45.3 us
    ppermute x7, starting transfers between devices, ring_shift(): lax.ppermute(value, axis, [(i, (i + step) % size) for i in range(size)])  20.6 us
    ppermute x7, waiting for transfers between devices, ring_shift(): lax.ppermute(value, axis, [(i, (i + step) % size) for i in range(size)])  17.8 us
    all_to_all x1, blocking collectives, on_device(): lax.all_to_all(partial_value.reshape(row_size, rows, width), 'row', 0, 0,...  17.1 us
    pallas_call x1, Pallas kernels, spread(): pl.pallas_call(functools.partial(spread_kernel, source_count=source_count...  3.09 us
    pallas_call x2, Pallas kernels, multiply(): pl.pallas_call(functools.partial(multiply_kernel, spots=spots, across=acr...  2.8 us
  transfers between devices with their start and end apart: 7, of which 2 were waited for; matrix products, arithmetic and copies ran while one was open for 0% of the time, Pallas kernels for 4%

profile of v4, /device:TPU:1, one launch (start us, length us, event | category | flops | bytes accessed | tf_op | source)
XLA Modules:
  0.0 108.3 jit_solution(3270909906247749160)
XLA Ops:
  0.0 0.0 copy-start
  0.0 45.3 %all-gather = bf16[1024,256]{1,0:T(8,128)(2,1)S(1)} all-gather(bf16[64,256]{1,0:T(8,128)(2,1)} %param.5), channel_id=2, replica_groups={{0,8,16,24,32,40,48,56,64,72,80,88,96,104,112,120},{4,12,20,28,36,44,52..., dimensions={0}, use_global_device_ids=true | all-gather | bytes 557056 | tf_op jit(solution)/shard_map/all_gather | solution.py:139
  45.3 4.8 %collective-permute-start = (bf16[16,64,256]{2,1,0:T(8,128)(2,1)S(1)}, bf16[16,64,256]{2,1,0:T(8,128)(2,1)S(1)}, u32[]{:S(2)}, u32[]{:S(2)}) collective-permute-start(bf16[16,64,256]{2,1,0:T(8,128)(2,1)S(1)} %bitcast.5), channel_id=1, source_target_pairs={{0,2},{1,3},{2,0},{3,1},{4,6},{5,7},{6,4},{7,5},{8,10},{9,11},{10,... | collective-permute-start | bytes 1572872 | tf_op jit(solution)/shard_map/ppermute | solution.py:16
  50.1 2.7 %collective-permute-start.1 = (bf16[16,64,256]{2,1,0:T(8,128)(2,1)S(1)}, bf16[16,64,256]{2,1,0:T(8,128)(2,1)S(1)}, u32[]{:S(2)}, u32[]{:S(2)}) collective-permute-start(bf16[16,64,256]{2,1,0:T(8,128)(2,1)S(1)} %bitcast.6), channel_id=1, source_target_pairs={{0,3},{1,0},{2,1},{3,2},{4,7},{5,4},{6,5},{7,6},{8,11},{9,8},{10,9... | collective-permute-start | bytes 1572872 | tf_op jit(solution)/shard_map/ppermute | solution.py:16
  52.8 2.6 %collective-permute-start.2 = (bf16[16,64,256]{2,1,0:T(8,128)(2,1)S(1)}, bf16[16,64,256]{2,1,0:T(8,128)(2,1)S(1)}, u32[]{:S(2)}, u32[]{:S(2)}) collective-permute-start(bf16[16,64,256]{2,1,0:T(8,128)(2,1)S(1)} %bitcast.7), channel_id=1, source_target_pairs={{0,1},{1,2},{2,3},{3,0},{4,5},{5,6},{6,7},{7,4},{8,9},{9,10},{10,1... | collective-permute-start | bytes 1572872 | tf_op jit(solution)/shard_map/ppermute | solution.py:16
  55.4 2.9 %collective-permute-start.6 = (bf16[16,64,256]{2,1,0:T(8,128)(2,1)S(1)}, bf16[16,64,256]{2,1,0:T(8,128)(2,1)S(1)}, u32[]{:S(2)}, u32[]{:S(2)}) collective-permute-start(bf16[16,64,256]{2,1,0:T(8,128)(2,1)S(1)} %bitcast.8), channel_id=1, source_target_pairs={{0,124},{4,0},{8,4},{12,8},{16,12},{20,16},{24,20},{28,24},{32,28}... | collective-permute-start | bytes 1572872 | tf_op jit(solution)/shard_map/ppermute | solution.py:16
  58.4 0.0 collective-permute-done.refs_0_
  58.4 2.3 %collective-permute-start.3 = (bf16[16,64,256]{2,1,0:T(8,128)(2,1)S(1)}, bf16[16,64,256]{2,1,0:T(8,128)(2,1)S(1)}, u32[]{:S(2)}, u32[]{:S(2)}) collective-permute-start(bf16[16,64,256]{2,1,0:T(8,128)(2,1)S(1)} %collective-permute-done.refs_0_), channel_id=1, source_target_pairs={{0,4},{4,8},{8,12},{12,16},{16,20},{20,24},{24,28},{28,32},{32,36}... | collective-permute-start | bytes 1572872 | tf_op jit(solution)/shard_map/ppermute | solution.py:16
  60.7 8.9 %collective-permute-done.1.refs_1_ = bf16[16,64,256]{2,1,0:T(8,128)(2,1)S(1)} collective-permute-done((bf16[16,64,256]{2,1,0:T(8,128)(2,1)S(1)}, bf16[16,64,256]{2,1,0:T(8,128)(2,1)S(1)}, u32[]{:S(2)}, u32[]{:S(2)}) %collective-permute-start.1) | collective-permute-done | bytes 524320 | tf_op jit(solution)/shard_map/ppermute | solution.py:16
  69.6 2.6 %collective-permute-start.4 = (bf16[16,64,256]{2,1,0:T(8,128)(2,1)S(1)}, bf16[16,64,256]{2,1,0:T(8,128)(2,1)S(1)}, u32[]{:S(2)}, u32[]{:S(2)}) collective-permute-start(bf16[16,64,256]{2,1,0:T(8,128)(2,1)S(1)} %collective-permute-done.1.refs_1_), channel_id=1, source_target_pairs={{0,124},{4,0},{8,4},{12,8},{16,12},{20,16},{24,20},{28,24},{32,28}... | collective-permute-start | bytes 1572872 | tf_op jit(solution)/shard_map/ppermute | solution.py:16
  72.2 0.0 collective-permute-done.2.refs_2_
  72.2 2.7 %collective-permute-start.5 = (bf16[16,64,256]{2,1,0:T(8,128)(2,1)S(1)}, bf16[16,64,256]{2,1,0:T(8,128)(2,1)S(1)}, u32[]{:S(2)}, u32[]{:S(2)}) collective-permute-start(bf16[16,64,256]{2,1,0:T(8,128)(2,1)S(1)} %collective-permute-done.2.refs_2_), channel_id=1, source_target_pairs={{0,4},{4,8},{8,12},{12,16},{16,20},{20,24},{24,28},{28,32},{32,36}... | collective-permute-start | bytes 1572872 | tf_op jit(solution)/shard_map/ppermute | solution.py:16
  75.6 3.1 %shard_map.55.dense = bf16[64,512,128]{2,1,0:T(8,128)(2,1)S(1)} custom-call(s32[1,1,96]{2,1,0:T(1,128)} %coord_ref.1, s32[1,1]{1,0:T(1,128)S(6)} %copy.6.count_ref, bf16[1,1,96,128,128]{4,3,2,1,0:T(8,128)(2,1)} %adj_ref.1), custom_call_target="tpu_custom_call" | custom-call | bytes 12582912 | tf_op jit(solution)/shard_map/pallas_call | solution.py:63
  78.7 1.4 %shard_map.56.refs_0_ = f32[512,256]{1,0:T(8,128)S(1)} custom-call(bf16[64,512,128]{2,1,0:T(8,128)(2,1)S(1)} %shard_map.55.dense, bf16[16,64,256]{2,1,0:T(8,128)(2,1)S(1)} %collective-permute-done.refs_0_, bf16[16,64,256]{2,1,0:T(8,128)(2,1)S(1)} %collective-permute-done.1.refs_1_, bf16[16,64,256]{2,1,0:T(8,128)(2,1)S(1)} %collective-permute-done.2.refs_2_, ...), custom_call_target="tpu_custom_call" | custom-call | flops 1073741824 | bytes 6291456 | tf_op jit(solution)/shard_map/pallas_call | solution.py:115
  80.1 0.0 collective-permute-done.6.refs_4_
  80.1 0.0 collective-permute-done.3.refs_1_
  80.1 0.0 collective-permute-done.4.refs_2_
  80.1 8.8 %collective-permute-done.5.refs_3_ = bf16[16,64,256]{2,1,0:T(8,128)(2,1)S(1)} collective-permute-done((bf16[16,64,256]{2,1,0:T(8,128)(2,1)S(1)}, bf16[16,64,256]{2,1,0:T(8,128)(2,1)S(1)}, u32[]{:S(2)}, u32[]{:S(2)}) %collective-permute-start.5) | collective-permute-done | bytes 524320 | tf_op jit(solution)/shard_map/ppermute | solution.py:16
  88.9 1.4 %shard_map.57 = f32[512,256]{1,0:T(8,128)S(1)} custom-call(bf16[64,512,128]{2,1,0:T(8,128)(2,1)S(1)} %shard_map.55.dense, f32[512,256]{1,0:T(8,128)S(1)} %shard_map.56.refs_0_, bf16[16,64,256]{2,1,0:T(8,128)(2,1)S(1)} %collective-permute-done.3.refs_1_, bf16[16,64,256]{2,1,0:T(8,128)(2,1)S(1)} %collective-permute-done.4.refs_2_, ...), custom_call_target="tpu_custom_call" | custom-call | flops 1073741824 | bytes 6291456 | tf_op jit(solution)/shard_map/pallas_call | solution.py:115
  90.3 17.1 %all_to_all.5 = f32[8,64,256]{2,1,0:T(8,128)S(1)} all-to-all(f32[8,64,256]{2,1,0:T(8,128)S(1)} %bitcast.4), channel_id=1, replica_groups=mesh['row'=8,'z'=32,'y'=4] {'row'}, dimensions={0} | all-to-all | bytes 1048576 | tf_op jit(solution)/shard_map/all_to_all | solution.py:147
  107.5 0.0 copy-done
  107.5 0.8 fusion
  (1 shorter events, 0.0 us)
Async XLA Ops:
  0.0 107.5 %copy-start = (bf16[256,256]{1,0:T(8,128)(2,1)S(1)}, bf16[256,256]{1,0:T(8,128)(2,1)}, u32[]{:S(2)}) copy-start(bf16[256,256]{1,0:T(8,128)(2,1)} %param.9) | copy-start | bytes 393220
  45.3 13.0 %collective-permute-start = (bf16[16,64,256]{2,1,0:T(8,128)(2,1)S(1)}, bf16[16,64,256]{2,1,0:T(8,128)(2,1)S(1)}, u32[]{:S(2)}, u32[]{:S(2)}) collective-permute-start(bf16[16,64,256]{2,1,0:T(8,128)(2,1)S(1)} %bitcast.5), channel_id=1, source_target_pairs={{0,2},{1,3},{2,0},{3,1},{4,6},{5,7},{6,4},{7,5},{8,10},{9,11},{10,... | collective-permute-start | bytes 1572872 | tf_op jit(solution)/shard_map/ppermute | solution.py:16
  50.1 19.5 %collective-permute-start.1 = (bf16[16,64,256]{2,1,0:T(8,128)(2,1)S(1)}, bf16[16,64,256]{2,1,0:T(8,128)(2,1)S(1)}, u32[]{:S(2)}, u32[]{:S(2)}) collective-permute-start(bf16[16,64,256]{2,1,0:T(8,128)(2,1)S(1)} %bitcast.6), channel_id=1, source_target_pairs={{0,3},{1,0},{2,1},{3,2},{4,7},{5,4},{6,5},{7,6},{8,11},{9,8},{10,9... | collective-permute-start | bytes 1572872 | tf_op jit(solution)/shard_map/ppermute | solution.py:16
  52.8 19.4 %collective-permute-start.2 = (bf16[16,64,256]{2,1,0:T(8,128)(2,1)S(1)}, bf16[16,64,256]{2,1,0:T(8,128)(2,1)S(1)}, u32[]{:S(2)}, u32[]{:S(2)}) collective-permute-start(bf16[16,64,256]{2,1,0:T(8,128)(2,1)S(1)} %bitcast.7), channel_id=1, source_target_pairs={{0,1},{1,2},{2,3},{3,0},{4,5},{5,6},{6,7},{7,4},{8,9},{9,10},{10,1... | collective-permute-start | bytes 1572872 | tf_op jit(solution)/shard_map/ppermute | solution.py:16
  55.4 24.7 %collective-permute-start.6 = (bf16[16,64,256]{2,1,0:T(8,128)(2,1)S(1)}, bf16[16,64,256]{2,1,0:T(8,128)(2,1)S(1)}, u32[]{:S(2)}, u32[]{:S(2)}) collective-permute-start(bf16[16,64,256]{2,1,0:T(8,128)(2,1)S(1)} %bitcast.8), channel_id=1, source_target_pairs={{0,124},{4,0},{8,4},{12,8},{16,12},{20,16},{24,20},{28,24},{32,28}... | collective-permute-start | bytes 1572872 | tf_op jit(solution)/shard_map/ppermute | solution.py:16
  58.4 21.7 %collective-permute-start.3 = (bf16[16,64,256]{2,1,0:T(8,128)(2,1)S(1)}, bf16[16,64,256]{2,1,0:T(8,128)(2,1)S(1)}, u32[]{:S(2)}, u32[]{:S(2)}) collective-permute-start(bf16[16,64,256]{2,1,0:T(8,128)(2,1)S(1)} %collective-permute-done.refs_0_), channel_id=1, source_target_pairs={{0,4},{4,8},{8,12},{12,16},{16,20},{20,24},{24,28},{28,32},{32,36}... | collective-permute-start | bytes 1572872 | tf_op jit(solution)/shard_map/ppermute | solution.py:16
  69.6 10.5 %collective-permute-start.4 = (bf16[16,64,256]{2,1,0:T(8,128)(2,1)S(1)}, bf16[16,64,256]{2,1,0:T(8,128)(2,1)S(1)}, u32[]{:S(2)}, u32[]{:S(2)}) collective-permute-start(bf16[16,64,256]{2,1,0:T(8,128)(2,1)S(1)} %collective-permute-done.1.refs_1_), channel_id=1, source_target_pairs={{0,124},{4,0},{8,4},{12,8},{16,12},{20,16},{24,20},{28,24},{32,28}... | collective-permute-start | bytes 1572872 | tf_op jit(solution)/shard_map/ppermute | solution.py:16
  72.2 16.7 %collective-permute-start.5 = (bf16[16,64,256]{2,1,0:T(8,128)(2,1)S(1)}, bf16[16,64,256]{2,1,0:T(8,128)(2,1)S(1)}, u32[]{:S(2)}, u32[]{:S(2)}) collective-permute-start(bf16[16,64,256]{2,1,0:T(8,128)(2,1)S(1)} %collective-permute-done.2.refs_2_), channel_id=1, source_target_pairs={{0,4},{4,8},{8,12},{12,16},{16,20},{20,24},{24,28},{28,32},{32,36}... | collective-permute-start | bytes 1572872 | tf_op jit(solution)/shard_map/ppermute | solution.py:16

commit v5 on v4

--- a/solution.py
+++ b/solution.py
@@ -137,7 +137,7 @@
     half_z = z_size // 2
     groups = [[i + 2 * j for j in range(half_z)] for i in range(2)]
     own = lax.all_gather(features, "z", axis=0, axis_index_groups=groups)
-    spots = [2, 1, y_size - 1, 0]
+    spots = [1, y_size - 1, 2, 0]
     near = [ring_shift(own, "y", -spot) for spot in spots[:-1]] + [own]
     far = [ring_shift(piece, "z", (-1) ** at) for at, piece in enumerate(near)]
 

time: 109 us -> 111 us (1.018)
  blocking collectives: 62.4 us -> 72.9 us
  waiting for transfers between devices: 17.8 us -> 8.05 us
    all_to_all x1, blocking collectives: 17.1 us -> 27.6 us  [on_device(): lax.all_to_all(partial_value.reshape(row_size, rows, width), 'row', 0, 0,...]
    ppermute x7, waiting for transfers between devices: 17.8 us -> 8.05 us  [ring_shift(): lax.ppermute(value, axis, [(i, (i + step) % size) for i in range(size)])]
  transfers between devices with their start and end apart: 7 -> 7, of which waited for: 2 -> 4; matrix products, arithmetic and copies ran while one was open for 0% -> 0% of each run, Pallas kernels for 4% -> 4%
where the time goes in v5:
time: 111 us; the launch traced here: 110 us
  blocking collectives  72.9 us (66%)
  starting transfers between devices  21.4 us (19%)
  waiting for transfers between devices  8.05 us (7%)
  Pallas kernels  6.02 us (5%)
    all_gather x1, blocking collectives, on_device(): own = lax.all_gather(features, 'z', axis=0, axis_index_groups=groups)  45.3 us
    all_to_all x1, blocking collectives, on_device(): lax.all_to_all(partial_value.reshape(row_size, rows, width), 'row', 0, 0,...  27.6 us
    ppermute x7, starting transfers between devices, ring_shift(): lax.ppermute(value, axis, [(i, (i + step) % size) for i in range(size)])  21.4 us
    ppermute x7, waiting for transfers between devices, ring_shift(): lax.ppermute(value, axis, [(i, (i + step) % size) for i in range(size)])  8.05 us
    pallas_call x1, Pallas kernels, spread(): pl.pallas_call(functools.partial(spread_kernel, source_count=source_count...  3.22 us
    pallas_call x2, Pallas kernels, multiply(): pl.pallas_call(functools.partial(multiply_kernel, spots=spots, across=acr...  2.8 us
  transfers between devices with their start and end apart: 7, of which 4 were waited for; matrix products, arithmetic and copies ran while one was open for 0% of the time, Pallas kernels for 4%

profile of v5, /device:TPU:1, one launch (start us, length us, event | category | flops | bytes accessed | tf_op | source)
XLA Modules:
  0.0 109.9 jit_solution(6950528480895596106)
XLA Ops:
  0.0 0.0 copy-start
  0.0 45.3 %all-gather = bf16[1024,256]{1,0:T(8,128)(2,1)S(1)} all-gather(bf16[64,256]{1,0:T(8,128)(2,1)} %param.5), channel_id=2, replica_groups={{0,8,16,24,32,40,48,56,64,72,80,88,96,104,112,120},{4,12,20,28,36,44,52..., dimensions={0}, use_global_device_ids=true | all-gather | bytes 557056 | tf_op jit(solution)/shard_map/all_gather | solution.py:139
  45.3 4.6 %collective-permute-start = (bf16[16,64,256]{2,1,0:T(8,128)(2,1)S(1)}, bf16[16,64,256]{2,1,0:T(8,128)(2,1)S(1)}, u32[]{:S(2)}, u32[]{:S(2)}) collective-permute-start(bf16[16,64,256]{2,1,0:T(8,128)(2,1)S(1)} %bitcast.5), channel_id=1, source_target_pairs={{0,3},{1,0},{2,1},{3,2},{4,7},{5,4},{6,5},{7,6},{8,11},{9,8},{10,9... | collective-permute-start | bytes 1572872 | tf_op jit(solution)/shard_map/ppermute | solution.py:16
  49.9 1.9 %collective-permute-start.1 = (bf16[16,64,256]{2,1,0:T(8,128)(2,1)S(1)}, bf16[16,64,256]{2,1,0:T(8,128)(2,1)S(1)}, u32[]{:S(2)}, u32[]{:S(2)}) collective-permute-start(bf16[16,64,256]{2,1,0:T(8,128)(2,1)S(1)} %bitcast.6), channel_id=1, source_target_pairs={{0,1},{1,2},{2,3},{3,0},{4,5},{5,6},{6,7},{7,4},{8,9},{9,10},{10,1... | collective-permute-start | bytes 1572872 | tf_op jit(solution)/shard_map/ppermute | solution.py:16
  51.9 3.5 %collective-permute-start.2 = (bf16[16,64,256]{2,1,0:T(8,128)(2,1)S(1)}, bf16[16,64,256]{2,1,0:T(8,128)(2,1)S(1)}, u32[]{:S(2)}, u32[]{:S(2)}) collective-permute-start(bf16[16,64,256]{2,1,0:T(8,128)(2,1)S(1)} %bitcast.7), channel_id=1, source_target_pairs={{0,2},{1,3},{2,0},{3,1},{4,6},{5,7},{6,4},{7,5},{8,10},{9,11},{10,... | collective-permute-start | bytes 1572872 | tf_op jit(solution)/shard_map/ppermute | solution.py:16
  55.4 2.9 %collective-permute-start.6 = (bf16[16,64,256]{2,1,0:T(8,128)(2,1)S(1)}, bf16[16,64,256]{2,1,0:T(8,128)(2,1)S(1)}, u32[]{:S(2)}, u32[]{:S(2)}) collective-permute-start(bf16[16,64,256]{2,1,0:T(8,128)(2,1)S(1)} %bitcast.8), channel_id=1, source_target_pairs={{0,124},{4,0},{8,4},{12,8},{16,12},{20,16},{24,20},{28,24},{32,28}... | collective-permute-start | bytes 1572872 | tf_op jit(solution)/shard_map/ppermute | solution.py:16
  58.4 0.0 collective-permute-done.refs_0_
  58.4 2.3 %collective-permute-start.3 = (bf16[16,64,256]{2,1,0:T(8,128)(2,1)S(1)}, bf16[16,64,256]{2,1,0:T(8,128)(2,1)S(1)}, u32[]{:S(2)}, u32[]{:S(2)}) collective-permute-start(bf16[16,64,256]{2,1,0:T(8,128)(2,1)S(1)} %collective-permute-done.refs_0_), channel_id=1, source_target_pairs={{0,4},{4,8},{8,12},{12,16},{16,20},{20,24},{24,28},{28,32},{32,36}... | collective-permute-start | bytes 1572872 | tf_op jit(solution)/shard_map/ppermute | solution.py:16
  60.7 4.8 %collective-permute-done.1.refs_1_ = bf16[16,64,256]{2,1,0:T(8,128)(2,1)S(1)} collective-permute-done((bf16[16,64,256]{2,1,0:T(8,128)(2,1)S(1)}, bf16[16,64,256]{2,1,0:T(8,128)(2,1)S(1)}, u32[]{:S(2)}, u32[]{:S(2)}) %collective-permute-start.1) | collective-permute-done | bytes 524320 | tf_op jit(solution)/shard_map/ppermute | solution.py:16
  65.5 3.3 %collective-permute-start.4 = (bf16[16,64,256]{2,1,0:T(8,128)(2,1)S(1)}, bf16[16,64,256]{2,1,0:T(8,128)(2,1)S(1)}, u32[]{:S(2)}, u32[]{:S(2)}) collective-permute-start(bf16[16,64,256]{2,1,0:T(8,128)(2,1)S(1)} %collective-permute-done.1.refs_1_), channel_id=1, source_target_pairs={{0,124},{4,0},{8,4},{12,8},{16,12},{20,16},{24,20},{28,24},{32,28}... | collective-permute-start | bytes 1572872 | tf_op jit(solution)/shard_map/ppermute | solution.py:16
  68.8 0.2 collective-permute-done.2.refs_2_
  69.0 2.8 %collective-permute-start.5 = (bf16[16,64,256]{2,1,0:T(8,128)(2,1)S(1)}, bf16[16,64,256]{2,1,0:T(8,128)(2,1)S(1)}, u32[]{:S(2)}, u32[]{:S(2)}) collective-permute-start(bf16[16,64,256]{2,1,0:T(8,128)(2,1)S(1)} %collective-permute-done.2.refs_2_), channel_id=1, source_target_pairs={{0,4},{4,8},{8,12},{12,16},{16,20},{20,24},{24,28},{28,32},{32,36}... | collective-permute-start | bytes 1572872 | tf_op jit(solution)/shard_map/ppermute | solution.py:16
  72.4 3.2 %shard_map.55.dense = bf16[64,512,128]{2,1,0:T(8,128)(2,1)S(1)} custom-call(s32[1,1,96]{2,1,0:T(1,128)} %coord_ref.1, s32[1,1]{1,0:T(1,128)S(6)} %copy.6.count_ref, bf16[1,1,96,128,128]{4,3,2,1,0:T(8,128)(2,1)} %adj_ref.1), custom_call_target="tpu_custom_call" | custom-call | bytes 12582912 | tf_op jit(solution)/shard_map/pallas_call | solution.py:63
  75.7 1.4 %shard_map.56.refs_0_ = f32[512,256]{1,0:T(8,128)S(1)} custom-call(bf16[64,512,128]{2,1,0:T(8,128)(2,1)S(1)} %shard_map.55.dense, bf16[16,64,256]{2,1,0:T(8,128)(2,1)S(1)} %collective-permute-done.refs_0_, bf16[16,64,256]{2,1,0:T(8,128)(2,1)S(1)} %collective-permute-done.1.refs_1_, bf16[16,64,256]{2,1,0:T(8,128)(2,1)S(1)} %collective-permute-done.2.refs_2_, ...), custom_call_target="tpu_custom_call" | custom-call | flops 1073741824 | bytes 6291456 | tf_op jit(solution)/shard_map/pallas_call | solution.py:115
  77.1 0.0 collective-permute-done.6.refs_4_
  77.1 0.0 collective-permute-done.3.refs_1_
  77.1 2.3 %collective-permute-done.4.refs_2_ = bf16[16,64,256]{2,1,0:T(8,128)(2,1)S(1)} collective-permute-done((bf16[16,64,256]{2,1,0:T(8,128)(2,1)S(1)}, bf16[16,64,256]{2,1,0:T(8,128)(2,1)S(1)}, u32[]{:S(2)}, u32[]{:S(2)}) %collective-permute-start.4) | collective-permute-done | bytes 524320 | tf_op jit(solution)/shard_map/ppermute | solution.py:16
  79.4 0.7 collective-permute-done.5.refs_3_
  80.1 1.4 %shard_map.57 = f32[512,256]{1,0:T(8,128)S(1)} custom-call(bf16[64,512,128]{2,1,0:T(8,128)(2,1)S(1)} %shard_map.55.dense, f32[512,256]{1,0:T(8,128)S(1)} %shard_map.56.refs_0_, bf16[16,64,256]{2,1,0:T(8,128)(2,1)S(1)} %collective-permute-done.3.refs_1_, bf16[16,64,256]{2,1,0:T(8,128)(2,1)S(1)} %collective-permute-done.4.refs_2_, ...), custom_call_target="tpu_custom_call" | custom-call | flops 1073741824 | bytes 6291456 | tf_op jit(solution)/shard_map/pallas_call | solution.py:115
  81.5 27.6 %all_to_all.5 = f32[8,64,256]{2,1,0:T(8,128)S(1)} all-to-all(f32[8,64,256]{2,1,0:T(8,128)S(1)} %bitcast.4), channel_id=1, replica_groups=mesh['row'=8,'z'=32,'y'=4] {'row'}, dimensions={0} | all-to-all | bytes 1048576 | tf_op jit(solution)/shard_map/all_to_all | solution.py:147
  109.1 0.0 copy-done
  109.2 0.8 fusion
  (1 shorter events, 0.0 us)
Async XLA Ops:
  0.0 109.1 %copy-start = (bf16[256,256]{1,0:T(8,128)(2,1)S(1)}, bf16[256,256]{1,0:T(8,128)(2,1)}, u32[]{:S(2)}) copy-start(bf16[256,256]{1,0:T(8,128)(2,1)} %param.9) | copy-start | bytes 393220
  45.3 13.0 %collective-permute-start = (bf16[16,64,256]{2,1,0:T(8,128)(2,1)S(1)}, bf16[16,64,256]{2,1,0:T(8,128)(2,1)S(1)}, u32[]{:S(2)}, u32[]{:S(2)}) collective-permute-start(bf16[16,64,256]{2,1,0:T(8,128)(2,1)S(1)} %bitcast.5), channel_id=1, source_target_pairs={{0,3},{1,0},{2,1},{3,2},{4,7},{5,4},{6,5},{7,6},{8,11},{9,8},{10,9... | collective-permute-start | bytes 1572872 | tf_op jit(solution)/shard_map/ppermute | solution.py:16
  49.9 15.6 %collective-permute-start.1 = (bf16[16,64,256]{2,1,0:T(8,128)(2,1)S(1)}, bf16[16,64,256]{2,1,0:T(8,128)(2,1)S(1)}, u32[]{:S(2)}, u32[]{:S(2)}) collective-permute-start(bf16[16,64,256]{2,1,0:T(8,128)(2,1)S(1)} %bitcast.6), channel_id=1, source_target_pairs={{0,1},{1,2},{2,3},{3,0},{4,5},{5,6},{6,7},{7,4},{8,9},{9,10},{10,1... | collective-permute-start | bytes 1572872 | tf_op jit(solution)/shard_map/ppermute | solution.py:16
  51.9 17.1 %collective-permute-start.2 = (bf16[16,64,256]{2,1,0:T(8,128)(2,1)S(1)}, bf16[16,64,256]{2,1,0:T(8,128)(2,1)S(1)}, u32[]{:S(2)}, u32[]{:S(2)}) collective-permute-start(bf16[16,64,256]{2,1,0:T(8,128)(2,1)S(1)} %bitcast.7), channel_id=1, source_target_pairs={{0,2},{1,3},{2,0},{3,1},{4,6},{5,7},{6,4},{7,5},{8,10},{9,11},{10,... | collective-permute-start | bytes 1572872 | tf_op jit(solution)/shard_map/ppermute | solution.py:16
  55.4 21.7 %collective-permute-start.6 = (bf16[16,64,256]{2,1,0:T(8,128)(2,1)S(1)}, bf16[16,64,256]{2,1,0:T(8,128)(2,1)S(1)}, u32[]{:S(2)}, u32[]{:S(2)}) collective-permute-start(bf16[16,64,256]{2,1,0:T(8,128)(2,1)S(1)} %bitcast.8), channel_id=1, source_target_pairs={{0,124},{4,0},{8,4},{12,8},{16,12},{20,16},{24,20},{28,24},{32,28}... | collective-permute-start | bytes 1572872 | tf_op jit(solution)/shard_map/ppermute | solution.py:16
  58.4 18.7 %collective-permute-start.3 = (bf16[16,64,256]{2,1,0:T(8,128)(2,1)S(1)}, bf16[16,64,256]{2,1,0:T(8,128)(2,1)S(1)}, u32[]{:S(2)}, u32[]{:S(2)}) collective-permute-start(bf16[16,64,256]{2,1,0:T(8,128)(2,1)S(1)} %collective-permute-done.refs_0_), channel_id=1, source_target_pairs={{0,4},{4,8},{8,12},{12,16},{16,20},{20,24},{24,28},{28,32},{32,36}... | collective-permute-start | bytes 1572872 | tf_op jit(solution)/shard_map/ppermute | solution.py:16
  65.5 13.9 %collective-permute-start.4 = (bf16[16,64,256]{2,1,0:T(8,128)(2,1)S(1)}, bf16[16,64,256]{2,1,0:T(8,128)(2,1)S(1)}, u32[]{:S(2)}, u32[]{:S(2)}) collective-permute-start(bf16[16,64,256]{2,1,0:T(8,128)(2,1)S(1)} %collective-permute-done.1.refs_1_), channel_id=1, source_target_pairs={{0,124},{4,0},{8,4},{12,8},{16,12},{20,16},{24,20},{28,24},{32,28}... | collective-permute-start | bytes 1572872 | tf_op jit(solution)/shard_map/ppermute | solution.py:16
  69.0 11.1 %collective-permute-start.5 = (bf16[16,64,256]{2,1,0:T(8,128)(2,1)S(1)}, bf16[16,64,256]{2,1,0:T(8,128)(2,1)S(1)}, u32[]{:S(2)}, u32[]{:S(2)}) collective-permute-start(bf16[16,64,256]{2,1,0:T(8,128)(2,1)S(1)} %collective-permute-done.2.refs_2_), channel_id=1, source_target_pairs={{0,4},{4,8},{8,12},{12,16},{16,20},{20,24},{24,28},{28,32},{32,36}... | collective-permute-start | bytes 1572872 | tf_op jit(solution)/shard_map/ppermute | solution.py:16

commit v6 on v4

--- a/solution.py
+++ b/solution.py
@@ -81,7 +81,7 @@
 def multiply_kernel(dense, *refs, spots, across, added):
     base_ref = refs[0] if added else None
     piece_refs = refs[added : added + len(spots)]
-    out_ref, feats = refs[added + len(spots) :]
+    out_ref, feats, total = refs[added + len(spots) :]
     half = (lax.axis_index("z") + across) % 2
     own_y = lax.axis_index("y")
     y_size, z_count, rows, width = feats.shape
@@ -101,23 +101,29 @@
             preferred_element_type=jnp.float32,
         )
         if at > 0:
-            out_ref[...] += product
+            product += total[...]
         elif added:
-            out_ref[...] = base_ref[...] + product
+            product += base_ref[...]
+        if at + per_step < z_count:
+            total[...] = product
         else:
-            out_ref[...] = product
+            out_ref[...] = product.astype(out_ref.dtype)
 
 
-def multiply(dense, pieces, spots, across, base=None):
+def multiply(dense, pieces, spots, across, kind, base=None):
     z_count, rows, width = pieces[0].shape
     added = 0 if base is None else 1
     arrays = [dense] + ([base] if added else []) + pieces
+    shape = (dense.shape[1], width)
     return pl.pallas_call(
         functools.partial(multiply_kernel, spots=spots, across=across, added=added),
-        out_shape=jax.ShapeDtypeStruct((dense.shape[1], width), jnp.float32),
+        out_shape=jax.ShapeDtypeStruct(shape, kind),
         in_specs=[pl.BlockSpec(memory_space=pltpu.VMEM)] * len(arrays),
         out_specs=pl.BlockSpec(memory_space=pltpu.VMEM),
-        scratch_shapes=[pltpu.VMEM((len(spots), z_count, rows, width), jnp.bfloat16)],
+        scratch_shapes=[
+            pltpu.VMEM((len(spots), z_count, rows, width), jnp.bfloat16),
+            pltpu.VMEM(shape, jnp.float32),
+        ],
         compiler_params=pltpu.CompilerParams(vmem_limit_bytes=VMEM_GRANT),
         cost_estimate=pl.CostEstimate(
             flops=2 * dense.shape[1] * z_count * len(spots) * rows * width,
@@ -142,12 +148,12 @@
     far = [ring_shift(piece, "z", (-1) ** at) for at, piece in enumerate(near)]
 
     dense = spread(adj_tiles, tile_coord, tile_count, target_count, source_count)
-    first = multiply(dense, near, spots, 0)
-    partial_value = multiply(dense, far, spots, 1, first)
+    first = multiply(dense, near, spots, 0, jnp.float32)
+    partial_value = multiply(dense, far, spots, 1, jnp.bfloat16, first)
     parts = lax.all_to_all(
         partial_value.reshape(row_size, rows, width), "row", 0, 0, tiled=True
     )
-    hidden = jnp.sum(parts, axis=0).astype(jnp.bfloat16)
+    hidden = jnp.sum(parts.astype(jnp.float32), axis=0).astype(jnp.bfloat16)
     mixed = jnp.dot(hidden, weight, preferred_element_type=jnp.float32)
     return jax.nn.relu(mixed).astype(jnp.bfloat16)
 

time: 109 us -> 106 us (0.972)
  blocking collectives: 62.4 us -> 59.6 us
    all_to_all x1, blocking collectives: 17.1 us -> 14.3 us  [on_device(): lax.all_to_all(partial_value.reshape(row_size, rows, width), 'row', 0, 0,...]
  transfers between devices with their start and end apart: 7 -> 7, of which waited for: 2 -> 2; matrix products, arithmetic and copies ran while one was open for 0% -> 0% of each run, Pallas kernels for 4% -> 5%
where the time goes in v6:
time: 106 us; the launch traced here: 105 us
  blocking collectives  59.6 us (56%)
  starting transfers between devices  20.6 us (19%)
  waiting for transfers between devices  17.2 us (16%)
  Pallas kernels  6.43 us (6%)
    all_gather x1, blocking collectives, on_device(): own = lax.all_gather(features, 'z', axis=0, axis_index_groups=groups)  45.3 us
    ppermute x7, starting transfers between devices, ring_shift(): lax.ppermute(value, axis, [(i, (i + step) % size) for i in range(size)])  20.6 us
    ppermute x7, waiting for transfers between devices, ring_shift(): lax.ppermute(value, axis, [(i, (i + step) % size) for i in range(size)])  17.2 us
    all_to_all x1, blocking collectives, on_device(): lax.all_to_all(partial_value.reshape(row_size, rows, width), 'row', 0, 0,...  14.3 us
    pallas_call x1, Pallas kernels, spread(): pl.pallas_call(functools.partial(spread_kernel, source_count=source_count...  3.63 us
    pallas_call x2, Pallas kernels, multiply(): pl.pallas_call(functools.partial(multiply_kernel, spots=spots, across=acr...  2.8 us
  transfers between devices with their start and end apart: 7, of which 2 were waited for; matrix products, arithmetic and copies ran while one was open for 0% of the time, Pallas kernels for 5%

profile of v6, /device:TPU:1, one launch (start us, length us, event | category | flops | bytes accessed | tf_op | source)
XLA Modules:
  0.0 105.4 jit_solution(18336619657739828833)
XLA Ops:
  0.0 0.0 copy-start
  0.0 45.3 %all-gather = bf16[1024,256]{1,0:T(8,128)(2,1)S(1)} all-gather(bf16[64,256]{1,0:T(8,128)(2,1)} %param.5), channel_id=2, replica_groups={{0,8,16,24,32,40,48,56,64,72,80,88,96,104,112,120},{4,12,20,28,36,44,52..., dimensions={0}, use_global_device_ids=true | all-gather | bytes 557056 | tf_op jit(solution)/shard_map/all_gather | solution.py:145
  45.3 4.8 %collective-permute-start = (bf16[16,64,256]{2,1,0:T(8,128)(2,1)S(1)}, bf16[16,64,256]{2,1,0:T(8,128)(2,1)S(1)}, u32[]{:S(2)}, u32[]{:S(2)}) collective-permute-start(bf16[16,64,256]{2,1,0:T(8,128)(2,1)S(1)} %bitcast.4), channel_id=1, source_target_pairs={{0,2},{1,3},{2,0},{3,1},{4,6},{5,7},{6,4},{7,5},{8,10},{9,11},{10,... | collective-permute-start | bytes 1572872 | tf_op jit(solution)/shard_map/ppermute | solution.py:16
  50.1 2.7 %collective-permute-start.1 = (bf16[16,64,256]{2,1,0:T(8,128)(2,1)S(1)}, bf16[16,64,256]{2,1,0:T(8,128)(2,1)S(1)}, u32[]{:S(2)}, u32[]{:S(2)}) collective-permute-start(bf16[16,64,256]{2,1,0:T(8,128)(2,1)S(1)} %bitcast.5), channel_id=1, source_target_pairs={{0,3},{1,0},{2,1},{3,2},{4,7},{5,4},{6,5},{7,6},{8,11},{9,8},{10,9... | collective-permute-start | bytes 1572872 | tf_op jit(solution)/shard_map/ppermute | solution.py:16
  52.8 2.6 %collective-permute-start.2 = (bf16[16,64,256]{2,1,0:T(8,128)(2,1)S(1)}, bf16[16,64,256]{2,1,0:T(8,128)(2,1)S(1)}, u32[]{:S(2)}, u32[]{:S(2)}) collective-permute-start(bf16[16,64,256]{2,1,0:T(8,128)(2,1)S(1)} %bitcast.6), channel_id=1, source_target_pairs={{0,1},{1,2},{2,3},{3,0},{4,5},{5,6},{6,7},{7,4},{8,9},{9,10},{10,1... | collective-permute-start | bytes 1572872 | tf_op jit(solution)/shard_map/ppermute | solution.py:16
  55.4 2.9 %collective-permute-start.6 = (bf16[16,64,256]{2,1,0:T(8,128)(2,1)S(1)}, bf16[16,64,256]{2,1,0:T(8,128)(2,1)S(1)}, u32[]{:S(2)}, u32[]{:S(2)}) collective-permute-start(bf16[16,64,256]{2,1,0:T(8,128)(2,1)S(1)} %bitcast.7), channel_id=1, source_target_pairs={{0,124},{4,0},{8,4},{12,8},{16,12},{20,16},{24,20},{28,24},{32,28}... | collective-permute-start | bytes 1572872 | tf_op jit(solution)/shard_map/ppermute | solution.py:16
  58.4 0.0 collective-permute-done.refs_0_
  58.4 2.3 %collective-permute-start.3 = (bf16[16,64,256]{2,1,0:T(8,128)(2,1)S(1)}, bf16[16,64,256]{2,1,0:T(8,128)(2,1)S(1)}, u32[]{:S(2)}, u32[]{:S(2)}) collective-permute-start(bf16[16,64,256]{2,1,0:T(8,128)(2,1)S(1)} %collective-permute-done.refs_0_), channel_id=1, source_target_pairs={{0,4},{4,8},{8,12},{12,16},{16,20},{20,24},{24,28},{28,32},{32,36}... | collective-permute-start | bytes 1572872 | tf_op jit(solution)/shard_map/ppermute | solution.py:16
  60.7 8.9 %collective-permute-done.1.refs_1_ = bf16[16,64,256]{2,1,0:T(8,128)(2,1)S(1)} collective-permute-done((bf16[16,64,256]{2,1,0:T(8,128)(2,1)S(1)}, bf16[16,64,256]{2,1,0:T(8,128)(2,1)S(1)}, u32[]{:S(2)}, u32[]{:S(2)}) %collective-permute-start.1) | collective-permute-done | bytes 524320 | tf_op jit(solution)/shard_map/ppermute | solution.py:16
  69.6 2.6 %collective-permute-start.4 = (bf16[16,64,256]{2,1,0:T(8,128)(2,1)S(1)}, bf16[16,64,256]{2,1,0:T(8,128)(2,1)S(1)}, u32[]{:S(2)}, u32[]{:S(2)}) collective-permute-start(bf16[16,64,256]{2,1,0:T(8,128)(2,1)S(1)} %collective-permute-done.1.refs_1_), channel_id=1, source_target_pairs={{0,124},{4,0},{8,4},{12,8},{16,12},{20,16},{24,20},{28,24},{32,28}... | collective-permute-start | bytes 1572872 | tf_op jit(solution)/shard_map/ppermute | solution.py:16
  72.2 0.0 collective-permute-done.2.refs_2_
  72.2 2.7 %collective-permute-start.5 = (bf16[16,64,256]{2,1,0:T(8,128)(2,1)S(1)}, bf16[16,64,256]{2,1,0:T(8,128)(2,1)S(1)}, u32[]{:S(2)}, u32[]{:S(2)}) collective-permute-start(bf16[16,64,256]{2,1,0:T(8,128)(2,1)S(1)} %collective-permute-done.2.refs_2_), channel_id=1, source_target_pairs={{0,4},{4,8},{8,12},{12,16},{16,20},{20,24},{24,28},{28,32},{32,36}... | collective-permute-start | bytes 1572872 | tf_op jit(solution)/shard_map/ppermute | solution.py:16
  75.6 3.6 %shard_map.55.dense = bf16[64,512,128]{2,1,0:T(8,128)(2,1)S(1)} custom-call(s32[1,1,96]{2,1,0:T(1,128)} %coord_ref.1, s32[1,1]{1,0:T(1,128)S(6)} %copy.6.count_ref, bf16[1,1,96,128,128]{4,3,2,1,0:T(8,128)(2,1)} %adj_ref.1), custom_call_target="tpu_custom_call" | custom-call | bytes 12582912 | tf_op jit(solution)/shard_map/pallas_call | solution.py:63
  79.2 1.4 %shard_map.56.refs_0_ = f32[512,256]{1,0:T(8,128)S(1)} custom-call(bf16[64,512,128]{2,1,0:T(8,128)(2,1)S(1)} %shard_map.55.dense, bf16[16,64,256]{2,1,0:T(8,128)(2,1)S(1)} %collective-permute-done.refs_0_, bf16[16,64,256]{2,1,0:T(8,128)(2,1)S(1)} %collective-permute-done.1.refs_1_, bf16[16,64,256]{2,1,0:T(8,128)(2,1)S(1)} %collective-permute-done.2.refs_2_, ...), custom_call_target="tpu_custom_call" | custom-call | flops 1073741824 | bytes 6291456 | tf_op jit(solution)/shard_map/pallas_call | solution.py:118
  80.6 0.0 collective-permute-done.6.refs_4_
  80.6 0.0 collective-permute-done.3.refs_1_
  80.6 0.0 collective-permute-done.4.refs_2_
  80.7 8.3 %collective-permute-done.5.refs_3_ = bf16[16,64,256]{2,1,0:T(8,128)(2,1)S(1)} collective-permute-done((bf16[16,64,256]{2,1,0:T(8,128)(2,1)S(1)}, bf16[16,64,256]{2,1,0:T(8,128)(2,1)S(1)}, u32[]{:S(2)}, u32[]{:S(2)}) %collective-permute-start.5) | collective-permute-done | bytes 524320 | tf_op jit(solution)/shard_map/ppermute | solution.py:16
  88.9 1.4 %shard_map.57 = bf16[512,256]{1,0:T(8,128)(2,1)S(1)} custom-call(bf16[64,512,128]{2,1,0:T(8,128)(2,1)S(1)} %shard_map.55.dense, f32[512,256]{1,0:T(8,128)S(1)} %shard_map.56.refs_0_, bf16[16,64,256]{2,1,0:T(8,128)(2,1)S(1)} %collective-permute-done.3.refs_1_, bf16[16,64,256]{2,1,0:T(8,128)(2,1)S(1)} %collective-permute-done.4.refs_2_, ...), custom_call_target="tpu_custom_call" | custom-call | flops 1073741824 | bytes 6291456 | tf_op jit(solution)/shard_map/pallas_call | solution.py:118
  90.3 14.3 %all_to_all.5 = bf16[8,64,256]{2,1,0:T(8,128)(2,1)S(1)} all-to-all(bf16[8,64,256]{2,1,0:T(8,128)(2,1)S(1)} %bitcast.9), channel_id=1, replica_groups=mesh['row'=8,'z'=32,'y'=4] {'row'}, dimensions={0} | all-to-all | bytes 524288 | tf_op jit(solution)/shard_map/all_to_all | solution.py:153
  104.6 0.0 copy-done
  104.7 0.8 fusion
  (1 shorter events, 0.0 us)
Async XLA Ops:
  0.0 104.6 %copy-start = (bf16[256,256]{1,0:T(8,128)(2,1)S(1)}, bf16[256,256]{1,0:T(8,128)(2,1)}, u32[]{:S(2)}) copy-start(bf16[256,256]{1,0:T(8,128)(2,1)} %param.9) | copy-start | bytes 393220
  45.3 13.0 %collective-permute-start = (bf16[16,64,256]{2,1,0:T(8,128)(2,1)S(1)}, bf16[16,64,256]{2,1,0:T(8,128)(2,1)S(1)}, u32[]{:S(2)}, u32[]{:S(2)}) collective-permute-start(bf16[16,64,256]{2,1,0:T(8,128)(2,1)S(1)} %bitcast.4), channel_id=1, source_target_pairs={{0,2},{1,3},{2,0},{3,1},{4,6},{5,7},{6,4},{7,5},{8,10},{9,11},{10,... | collective-permute-start | bytes 1572872 | tf_op jit(solution)/shard_map/ppermute | solution.py:16
  50.1 19.5 %collective-permute-start.1 = (bf16[16,64,256]{2,1,0:T(8,128)(2,1)S(1)}, bf16[16,64,256]{2,1,0:T(8,128)(2,1)S(1)}, u32[]{:S(2)}, u32[]{:S(2)}) collective-permute-start(bf16[16,64,256]{2,1,0:T(8,128)(2,1)S(1)} %bitcast.5), channel_id=1, source_target_pairs={{0,3},{1,0},{2,1},{3,2},{4,7},{5,4},{6,5},{7,6},{8,11},{9,8},{10,9... | collective-permute-start | bytes 1572872 | tf_op jit(solution)/shard_map/ppermute | solution.py:16
  52.8 19.4 %collective-permute-start.2 = (bf16[16,64,256]{2,1,0:T(8,128)(2,1)S(1)}, bf16[16,64,256]{2,1,0:T(8,128)(2,1)S(1)}, u32[]{:S(2)}, u32[]{:S(2)}) collective-permute-start(bf16[16,64,256]{2,1,0:T(8,128)(2,1)S(1)} %bitcast.6), channel_id=1, source_target_pairs={{0,1},{1,2},{2,3},{3,0},{4,5},{5,6},{6,7},{7,4},{8,9},{9,10},{10,1... | collective-permute-start | bytes 1572872 | tf_op jit(solution)/shard_map/ppermute | solution.py:16
  55.4 25.2 %collective-permute-start.6 = (bf16[16,64,256]{2,1,0:T(8,128)(2,1)S(1)}, bf16[16,64,256]{2,1,0:T(8,128)(2,1)S(1)}, u32[]{:S(2)}, u32[]{:S(2)}) collective-permute-start(bf16[16,64,256]{2,1,0:T(8,128)(2,1)S(1)} %bitcast.7), channel_id=1, source_target_pairs={{0,124},{4,0},{8,4},{12,8},{16,12},{20,16},{24,20},{28,24},{32,28}... | collective-permute-start | bytes 1572872 | tf_op jit(solution)/shard_map/ppermute | solution.py:16
  58.4 22.3 %collective-permute-start.3 = (bf16[16,64,256]{2,1,0:T(8,128)(2,1)S(1)}, bf16[16,64,256]{2,1,0:T(8,128)(2,1)S(1)}, u32[]{:S(2)}, u32[]{:S(2)}) collective-permute-start(bf16[16,64,256]{2,1,0:T(8,128)(2,1)S(1)} %collective-permute-done.refs_0_), channel_id=1, source_target_pairs={{0,4},{4,8},{8,12},{12,16},{16,20},{20,24},{24,28},{28,32},{32,36}... | collective-permute-start | bytes 1572872 | tf_op jit(solution)/shard_map/ppermute | solution.py:16
  69.6 11.0 %collective-permute-start.4 = (bf16[16,64,256]{2,1,0:T(8,128)(2,1)S(1)}, bf16[16,64,256]{2,1,0:T(8,128)(2,1)S(1)}, u32[]{:S(2)}, u32[]{:S(2)}) collective-permute-start(bf16[16,64,256]{2,1,0:T(8,128)(2,1)S(1)} %collective-permute-done.1.refs_1_), channel_id=1, source_target_pairs={{0,124},{4,0},{8,4},{12,8},{16,12},{20,16},{24,20},{28,24},{32,28}... | collective-permute-start | bytes 1572872 | tf_op jit(solution)/shard_map/ppermute | solution.py:16
  72.2 16.7 %collective-permute-start.5 = (bf16[16,64,256]{2,1,0:T(8,128)(2,1)S(1)}, bf16[16,64,256]{2,1,0:T(8,128)(2,1)S(1)}, u32[]{:S(2)}, u32[]{:S(2)}) collective-permute-start(bf16[16,64,256]{2,1,0:T(8,128)(2,1)S(1)} %collective-permute-done.2.refs_2_), channel_id=1, source_target_pairs={{0,4},{4,8},{8,12},{12,16},{16,20},{20,24},{24,28},{28,32},{32,36}... | collective-permute-start | bytes 1572872 | tf_op jit(solution)/shard_map/ppermute | solution.py:16

commit v7 on v6

--- a/solution.py
+++ b/solution.py
@@ -9,6 +9,7 @@
 
 Y_RING = 4
 VMEM_GRANT = 24 * 1024 * 1024
+SENT_SCALE = 16.0
 
 
 def ring_shift(value, axis, step):
@@ -78,7 +79,7 @@
     )
 
 
-def multiply_kernel(dense, *refs, spots, across, added):
+def multiply_kernel(dense, *refs, spots, across, scale, added):
     base_ref = refs[0] if added else None
     piece_refs = refs[added : added + len(spots)]
     out_ref, feats, total = refs[added + len(spots) :]
@@ -107,16 +108,18 @@
         if at + per_step < z_count:
             total[...] = product
         else:
-            out_ref[...] = product.astype(out_ref.dtype)
+            out_ref[...] = (product * scale).astype(out_ref.dtype)
 
 
-def multiply(dense, pieces, spots, across, kind, base=None):
+def multiply(dense, pieces, spots, across, kind, scale=1.0, base=None):
     z_count, rows, width = pieces[0].shape
     added = 0 if base is None else 1
     arrays = [dense] + ([base] if added else []) + pieces
     shape = (dense.shape[1], width)
     return pl.pallas_call(
-        functools.partial(multiply_kernel, spots=spots, across=across, added=added),
+        functools.partial(
+            multiply_kernel, spots=spots, across=across, scale=scale, added=added
+        ),
         out_shape=jax.ShapeDtypeStruct(shape, kind),
         in_specs=[pl.BlockSpec(memory_space=pltpu.VMEM)] * len(arrays),
         out_specs=pl.BlockSpec(memory_space=pltpu.VMEM),
@@ -149,11 +152,12 @@
 
     dense = spread(adj_tiles, tile_coord, tile_count, target_count, source_count)
     first = multiply(dense, near, spots, 0, jnp.float32)
-    partial_value = multiply(dense, far, spots, 1, jnp.bfloat16, first)
+    partial_value = multiply(dense, far, spots, 1, jnp.float32, SENT_SCALE, first)
     parts = lax.all_to_all(
-        partial_value.reshape(row_size, rows, width), "row", 0, 0, tiled=True
+        partial_value.astype(jnp.float16).reshape(row_size, rows, width), "row", 0, 0, tiled=True
     )
-    hidden = jnp.sum(parts.astype(jnp.float32), axis=0).astype(jnp.bfloat16)
+    hidden = jnp.sum(parts.astype(jnp.float32), axis=0) / SENT_SCALE
+    hidden = hidden.astype(jnp.bfloat16)
     mixed = jnp.dot(hidden, weight, preferred_element_type=jnp.float32)
     return jax.nn.relu(mixed).astype(jnp.bfloat16)
 

time: 106 us -> 106 us (level)
  transfers between devices with their start and end apart: 7 -> 7, of which waited for: 2 -> 2; matrix products, arithmetic and copies ran while one was open for 0% -> 0% of each run, Pallas kernels for 5% -> 4%
where the time goes in v7:
time: 106 us; the launch traced here: 105 us
  blocking collectives  59.6 us (56%)
  starting transfers between devices  20.6 us (19%)
  waiting for transfers between devices  17.9 us (17%)
  Pallas kernels  5.71 us (5%)
    all_gather x1, blocking collectives, on_device(): own = lax.all_gather(features, 'z', axis=0, axis_index_groups=groups)  45.3 us
    ppermute x7, starting transfers between devices, ring_shift(): lax.ppermute(value, axis, [(i, (i + step) % size) for i in range(size)])  20.6 us
    ppermute x7, waiting for transfers between devices, ring_shift(): lax.ppermute(value, axis, [(i, (i + step) % size) for i in range(size)])  17.9 us
    all_to_all x1, blocking collectives, on_device(): lax.all_to_all(partial_value.astype(jnp.float16).reshape(row_size, rows,...  14.3 us
    pallas_call x1, Pallas kernels, spread(): pl.pallas_call(functools.partial(spread_kernel, source_count=source_count...  2.91 us
    pallas_call x2, Pallas kernels, multiply(): pl.pallas_call(functools.partial(multiply_kernel, spots=spots, across=acr...  2.8 us
  transfers between devices with their start and end apart: 7, of which 2 were waited for; matrix products, arithmetic and copies ran while one was open for 0% of the time, Pallas kernels for 4%

profile of v7, /device:TPU:1, one launch (start us, length us, event | category | flops | bytes accessed | tf_op | source)
XLA Modules:
  0.0 105.5 jit_solution(16333169032030653515)
XLA Ops:
  0.0 0.0 copy-start
  0.0 45.3 %all-gather = bf16[1024,256]{1,0:T(8,128)(2,1)S(1)} all-gather(bf16[64,256]{1,0:T(8,128)(2,1)} %param.5), channel_id=2, replica_groups={{0,8,16,24,32,40,48,56,64,72,80,88,96,104,112,120},{4,12,20,28,36,44,52..., dimensions={0}, use_global_device_ids=true | all-gather | bytes 557056 | tf_op jit(solution)/shard_map/all_gather | solution.py:148
  45.3 4.8 %collective-permute-start = (bf16[16,64,256]{2,1,0:T(8,128)(2,1)S(1)}, bf16[16,64,256]{2,1,0:T(8,128)(2,1)S(1)}, u32[]{:S(2)}, u32[]{:S(2)}) collective-permute-start(bf16[16,64,256]{2,1,0:T(8,128)(2,1)S(1)} %bitcast.3), channel_id=1, source_target_pairs={{0,2},{1,3},{2,0},{3,1},{4,6},{5,7},{6,4},{7,5},{8,10},{9,11},{10,... | collective-permute-start | bytes 1572872 | tf_op jit(solution)/shard_map/ppermute | solution.py:17
  50.1 2.7 %collective-permute-start.1 = (bf16[16,64,256]{2,1,0:T(8,128)(2,1)S(1)}, bf16[16,64,256]{2,1,0:T(8,128)(2,1)S(1)}, u32[]{:S(2)}, u32[]{:S(2)}) collective-permute-start(bf16[16,64,256]{2,1,0:T(8,128)(2,1)S(1)} %bitcast.4), channel_id=1, source_target_pairs={{0,3},{1,0},{2,1},{3,2},{4,7},{5,4},{6,5},{7,6},{8,11},{9,8},{10,9... | collective-permute-start | bytes 1572872 | tf_op jit(solution)/shard_map/ppermute | solution.py:17
  52.8 2.6 %collective-permute-start.2 = (bf16[16,64,256]{2,1,0:T(8,128)(2,1)S(1)}, bf16[16,64,256]{2,1,0:T(8,128)(2,1)S(1)}, u32[]{:S(2)}, u32[]{:S(2)}) collective-permute-start(bf16[16,64,256]{2,1,0:T(8,128)(2,1)S(1)} %bitcast.5), channel_id=1, source_target_pairs={{0,1},{1,2},{2,3},{3,0},{4,5},{5,6},{6,7},{7,4},{8,9},{9,10},{10,1... | collective-permute-start | bytes 1572872 | tf_op jit(solution)/shard_map/ppermute | solution.py:17
  55.4 2.9 %collective-permute-start.6 = (bf16[16,64,256]{2,1,0:T(8,128)(2,1)S(1)}, bf16[16,64,256]{2,1,0:T(8,128)(2,1)S(1)}, u32[]{:S(2)}, u32[]{:S(2)}) collective-permute-start(bf16[16,64,256]{2,1,0:T(8,128)(2,1)S(1)} %bitcast.6), channel_id=1, source_target_pairs={{0,124},{4,0},{8,4},{12,8},{16,12},{20,16},{24,20},{28,24},{32,28}... | collective-permute-start | bytes 1572872 | tf_op jit(solution)/shard_map/ppermute | solution.py:17
  58.4 0.0 collective-permute-done.refs_0_
  58.4 2.3 %collective-permute-start.3 = (bf16[16,64,256]{2,1,0:T(8,128)(2,1)S(1)}, bf16[16,64,256]{2,1,0:T(8,128)(2,1)S(1)}, u32[]{:S(2)}, u32[]{:S(2)}) collective-permute-start(bf16[16,64,256]{2,1,0:T(8,128)(2,1)S(1)} %collective-permute-done.refs_0_), channel_id=1, source_target_pairs={{0,4},{4,8},{8,12},{12,16},{16,20},{20,24},{24,28},{28,32},{32,36}... | collective-permute-start | bytes 1572872 | tf_op jit(solution)/shard_map/ppermute | solution.py:17
  60.7 8.9 %collective-permute-done.1.refs_1_ = bf16[16,64,256]{2,1,0:T(8,128)(2,1)S(1)} collective-permute-done((bf16[16,64,256]{2,1,0:T(8,128)(2,1)S(1)}, bf16[16,64,256]{2,1,0:T(8,128)(2,1)S(1)}, u32[]{:S(2)}, u32[]{:S(2)}) %collective-permute-start.1) | collective-permute-done | bytes 524320 | tf_op jit(solution)/shard_map/ppermute | solution.py:17
  69.6 2.6 %collective-permute-start.4 = (bf16[16,64,256]{2,1,0:T(8,128)(2,1)S(1)}, bf16[16,64,256]{2,1,0:T(8,128)(2,1)S(1)}, u32[]{:S(2)}, u32[]{:S(2)}) collective-permute-start(bf16[16,64,256]{2,1,0:T(8,128)(2,1)S(1)} %collective-permute-done.1.refs_1_), channel_id=1, source_target_pairs={{0,124},{4,0},{8,4},{12,8},{16,12},{20,16},{24,20},{28,24},{32,28}... | collective-permute-start | bytes 1572872 | tf_op jit(solution)/shard_map/ppermute | solution.py:17
  72.2 0.0 collective-permute-done.2.refs_2_
  72.2 2.7 %collective-permute-start.5 = (bf16[16,64,256]{2,1,0:T(8,128)(2,1)S(1)}, bf16[16,64,256]{2,1,0:T(8,128)(2,1)S(1)}, u32[]{:S(2)}, u32[]{:S(2)}) collective-permute-start(bf16[16,64,256]{2,1,0:T(8,128)(2,1)S(1)} %collective-permute-done.2.refs_2_), channel_id=1, source_target_pairs={{0,4},{4,8},{8,12},{12,16},{16,20},{20,24},{24,28},{28,32},{32,36}... | collective-permute-start | bytes 1572872 | tf_op jit(solution)/shard_map/ppermute | solution.py:17
  75.6 2.9 %shard_map.55.dense = bf16[64,512,128]{2,1,0:T(8,128)(2,1)S(1)} custom-call(s32[1,1,96]{2,1,0:T(1,128)} %coord_ref.1, s32[1,1]{1,0:T(1,128)S(6)} %copy.6.count_ref, bf16[1,1,96,128,128]{4,3,2,1,0:T(8,128)(2,1)} %adj_ref.1), custom_call_target="tpu_custom_call" | custom-call | bytes 12582912 | tf_op jit(solution)/shard_map/pallas_call | solution.py:64
  78.5 1.4 %shard_map.56.refs_0_ = f32[512,256]{1,0:T(8,128)S(1)} custom-call(bf16[64,512,128]{2,1,0:T(8,128)(2,1)S(1)} %shard_map.55.dense, bf16[16,64,256]{2,1,0:T(8,128)(2,1)S(1)} %collective-permute-done.refs_0_, bf16[16,64,256]{2,1,0:T(8,128)(2,1)S(1)} %collective-permute-done.1.refs_1_, bf16[16,64,256]{2,1,0:T(8,128)(2,1)S(1)} %collective-permute-done.2.refs_2_, ...), custom_call_target="tpu_custom_call" | custom-call | flops 1073741824 | bytes 6291456 | tf_op jit(solution)/shard_map/pallas_call | solution.py:119
  79.9 0.0 collective-permute-done.6.refs_4_
  79.9 0.0 collective-permute-done.3.refs_1_
  79.9 0.0 collective-permute-done.4.refs_2_
  79.9 9.0 %collective-permute-done.5.refs_3_ = bf16[16,64,256]{2,1,0:T(8,128)(2,1)S(1)} collective-permute-done((bf16[16,64,256]{2,1,0:T(8,128)(2,1)S(1)}, bf16[16,64,256]{2,1,0:T(8,128)(2,1)S(1)}, u32[]{:S(2)}, u32[]{:S(2)}) %collective-permute-start.5) | collective-permute-done | bytes 524320 | tf_op jit(solution)/shard_map/ppermute | solution.py:17
  88.9 1.4 %shard_map.57 = f32[512,256]{1,0:T(8,128)S(1)} custom-call(bf16[64,512,128]{2,1,0:T(8,128)(2,1)S(1)} %shard_map.55.dense, f32[512,256]{1,0:T(8,128)S(1)} %shard_map.56.refs_0_, bf16[16,64,256]{2,1,0:T(8,128)(2,1)S(1)} %collective-permute-done.3.refs_1_, bf16[16,64,256]{2,1,0:T(8,128)(2,1)S(1)} %collective-permute-done.4.refs_2_, ...), custom_call_target="tpu_custom_call" | custom-call | flops 1073741824 | bytes 6291456 | tf_op jit(solution)/shard_map/pallas_call | solution.py:119
  90.4 14.3 %all_to_all.5 = f16[8,64,256]{2,1,0:T(8,128)(2,1)S(1)} all-to-all(f16[8,64,256]{2,1,0:T(8,128)(2,1)S(1)} %bitcast.8), channel_id=1, replica_groups=mesh['row'=8,'z'=32,'y'=4] {'row'}, dimensions={0} | all-to-all | bytes 524288 | tf_op jit(solution)/shard_map/all_to_all | solution.py:156
  104.7 0.0 copy-done
  104.7 0.8 fusion
  (2 shorter events, 0.1 us)
Async XLA Ops:
  0.0 104.7 %copy-start = (bf16[256,256]{1,0:T(8,128)(2,1)S(1)}, bf16[256,256]{1,0:T(8,128)(2,1)}, u32[]{:S(2)}) copy-start(bf16[256,256]{1,0:T(8,128)(2,1)} %param.9) | copy-start | bytes 393220
  45.3 13.0 %collective-permute-start = (bf16[16,64,256]{2,1,0:T(8,128)(2,1)S(1)}, bf16[16,64,256]{2,1,0:T(8,128)(2,1)S(1)}, u32[]{:S(2)}, u32[]{:S(2)}) collective-permute-start(bf16[16,64,256]{2,1,0:T(8,128)(2,1)S(1)} %bitcast.3), channel_id=1, source_target_pairs={{0,2},{1,3},{2,0},{3,1},{4,6},{5,7},{6,4},{7,5},{8,10},{9,11},{10,... | collective-permute-start | bytes 1572872 | tf_op jit(solution)/shard_map/ppermute | solution.py:17
  50.1 19.5 %collective-permute-start.1 = (bf16[16,64,256]{2,1,0:T(8,128)(2,1)S(1)}, bf16[16,64,256]{2,1,0:T(8,128)(2,1)S(1)}, u32[]{:S(2)}, u32[]{:S(2)}) collective-permute-start(bf16[16,64,256]{2,1,0:T(8,128)(2,1)S(1)} %bitcast.4), channel_id=1, source_target_pairs={{0,3},{1,0},{2,1},{3,2},{4,7},{5,4},{6,5},{7,6},{8,11},{9,8},{10,9... | collective-permute-start | bytes 1572872 | tf_op jit(solution)/shard_map/ppermute | solution.py:17
  52.8 19.4 %collective-permute-start.2 = (bf16[16,64,256]{2,1,0:T(8,128)(2,1)S(1)}, bf16[16,64,256]{2,1,0:T(8,128)(2,1)S(1)}, u32[]{:S(2)}, u32[]{:S(2)}) collective-permute-start(bf16[16,64,256]{2,1,0:T(8,128)(2,1)S(1)} %bitcast.5), channel_id=1, source_target_pairs={{0,1},{1,2},{2,3},{3,0},{4,5},{5,6},{6,7},{7,4},{8,9},{9,10},{10,1... | collective-permute-start | bytes 1572872 | tf_op jit(solution)/shard_map/ppermute | solution.py:17
  55.4 24.5 %collective-permute-start.6 = (bf16[16,64,256]{2,1,0:T(8,128)(2,1)S(1)}, bf16[16,64,256]{2,1,0:T(8,128)(2,1)S(1)}, u32[]{:S(2)}, u32[]{:S(2)}) collective-permute-start(bf16[16,64,256]{2,1,0:T(8,128)(2,1)S(1)} %bitcast.6), channel_id=1, source_target_pairs={{0,124},{4,0},{8,4},{12,8},{16,12},{20,16},{24,20},{28,24},{32,28}... | collective-permute-start | bytes 1572872 | tf_op jit(solution)/shard_map/ppermute | solution.py:17
  58.4 21.6 %collective-permute-start.3 = (bf16[16,64,256]{2,1,0:T(8,128)(2,1)S(1)}, bf16[16,64,256]{2,1,0:T(8,128)(2,1)S(1)}, u32[]{:S(2)}, u32[]{:S(2)}) collective-permute-start(bf16[16,64,256]{2,1,0:T(8,128)(2,1)S(1)} %collective-permute-done.refs_0_), channel_id=1, source_target_pairs={{0,4},{4,8},{8,12},{12,16},{16,20},{20,24},{24,28},{28,32},{32,36}... | collective-permute-start | bytes 1572872 | tf_op jit(solution)/shard_map/ppermute | solution.py:17
  69.6 10.3 %collective-permute-start.4 = (bf16[16,64,256]{2,1,0:T(8,128)(2,1)S(1)}, bf16[16,64,256]{2,1,0:T(8,128)(2,1)S(1)}, u32[]{:S(2)}, u32[]{:S(2)}) collective-permute-start(bf16[16,64,256]{2,1,0:T(8,128)(2,1)S(1)} %collective-permute-done.1.refs_1_), channel_id=1, source_target_pairs={{0,124},{4,0},{8,4},{12,8},{16,12},{20,16},{24,20},{28,24},{32,28}... | collective-permute-start | bytes 1572872 | tf_op jit(solution)/shard_map/ppermute | solution.py:17
  72.2 16.7 %collective-permute-start.5 = (bf16[16,64,256]{2,1,0:T(8,128)(2,1)S(1)}, bf16[16,64,256]{2,1,0:T(8,128)(2,1)S(1)}, u32[]{:S(2)}, u32[]{:S(2)}) collective-permute-start(bf16[16,64,256]{2,1,0:T(8,128)(2,1)S(1)} %collective-permute-done.2.refs_2_), channel_id=1, source_target_pairs={{0,4},{4,8},{8,12},{12,16},{16,20},{20,24},{24,28},{28,32},{32,36}... | collective-permute-start | bytes 1572872 | tf_op jit(solution)/shard_map/ppermute | solution.py:17

commit v8 on v7

--- a/solution.py
+++ b/solution.py
@@ -13,8 +13,13 @@
 
 
 def ring_shift(value, axis, step):
-    size = lax.axis_size(axis)
-    return lax.ppermute(value, axis, [(i, (i + step) % size) for i in range(size)])
+    rows, size = lax.axis_size("row"), lax.axis_size(axis)
+    pairs = [
+        (row * size + i, row * size + (i + (-1) ** row * step) % size)
+        for row in range(rows)
+        for i in range(size)
+    ]
+    return lax.ppermute(value, ("row", axis), pairs)
 
 
 def spread_kernel(coord_ref, count_ref, adj_ref, dense, sem, *, source_count, tile):
@@ -85,11 +90,12 @@
     out_ref, feats, total = refs[added + len(spots) :]
     half = (lax.axis_index("z") + across) % 2
     own_y = lax.axis_index("y")
+    turn = 1 - 2 * (lax.axis_index("row") % 2)
     y_size, z_count, rows, width = feats.shape
     tile = dense.shape[-1]
     per_z = y_size * rows // tile
     for ref, offset in zip(piece_refs, spots):
-        feats[(own_y + offset) % y_size] = ref[...]
+        feats[(own_y + turn * offset + y_size) % y_size] = ref[...]
     per_step = 4
     for at in range(0, z_count, per_step):
         left, right = [], []

time: 106 us -> 105 us (level)
  the two profiles are of different devices: /device:TPU:1 before, /device:TPU:16 now
where the time goes in v8:
time: 105 us
  blocking collectives  62.6 us (60%)
  starting transfers between devices  20.8 us (20%)
  waiting for transfers between devices  13.8 us (13%)
  Pallas kernels  5.86 us (6%)
    all_gather x1, blocking collectives, on_device(): own = lax.all_gather(features, 'z', axis=0, axis_index_groups=groups)  51 us
    ppermute x7, starting transfers between devices, ring_shift(): return lax.ppermute(value, ('row', axis), pairs)  20.8 us
    ppermute x7, waiting for transfers between devices, ring_shift(): return lax.ppermute(value, ('row', axis), pairs)  13.8 us
    all_to_all x1, blocking collectives, on_device(): lax.all_to_all(partial_value.astype(jnp.float16).reshape(row_size, rows,...  11.6 us
    pallas_call x1, Pallas kernels, spread(): pl.pallas_call(functools.partial(spread_kernel, source_count=source_count...  3.03 us
    pallas_call x2, Pallas kernels, multiply(): pl.pallas_call(functools.partial(multiply_kernel, spots=spots, across=acr...  2.84 us
  transfers between devices with their start and end apart: 7, of which 5 were waited for; matrix products, arithmetic and copies ran while one was open for 0% of the time, Pallas kernels for 4%

profile of v8, /device:TPU:16, one launch (start us, length us, event | category | flops | bytes accessed | tf_op | source)
XLA Modules:
  0.0 104.7 jit_solution(15629849065317683244)
XLA Ops:
  0.0 0.0 copy-start
  0.0 51.0 %all-gather = bf16[1024,256]{1,0:T(8,128)(2,1)S(1)} all-gather(bf16[64,256]{1,0:T(8,128)(2,1)} %param.5), channel_id=2, replica_groups={{0,8,16,24,32,40,48,56,64,72,80,88,96,104,112,120},{4,12,20,28,36,44,52..., dimensions={0}, use_global_device_ids=true | all-gather | bytes 557056 | tf_op jit(solution)/shard_map/all_gather | solution.py:154
  51.0 2.2 %collective-permute-start = (bf16[16,64,256]{2,1,0:T(8,128)(2,1)S(1)}, bf16[16,64,256]{2,1,0:T(8,128)(2,1)S(1)}, u32[]{:S(2)}, u32[]{:S(2)}) collective-permute-start(bf16[16,64,256]{2,1,0:T(8,128)(2,1)S(1)} %bitcast.3), channel_id=1, source_target_pairs={{0,2},{1,3},{2,0},{3,1},{128,130},{129,131},{130,128},{131,129},{2... | collective-permute-start | bytes 1572872 | tf_op jit(solution)/shard_map/ppermute | solution.py:22
  53.2 4.3 %collective-permute-start.1 = (bf16[16,64,256]{2,1,0:T(8,128)(2,1)S(1)}, bf16[16,64,256]{2,1,0:T(8,128)(2,1)S(1)}, u32[]{:S(2)}, u32[]{:S(2)}) collective-permute-start(bf16[16,64,256]{2,1,0:T(8,128)(2,1)S(1)} %bitcast.4), channel_id=1, source_target_pairs={{0,3},{1,0},{2,1},{3,2},{128,129},{129,130},{130,131},{131,128},{2... | collective-permute-start | bytes 1572872 | tf_op jit(solution)/shard_map/ppermute | solution.py:22
  57.5 1.9 %collective-permute-start.2 = (bf16[16,64,256]{2,1,0:T(8,128)(2,1)S(1)}, bf16[16,64,256]{2,1,0:T(8,128)(2,1)S(1)}, u32[]{:S(2)}, u32[]{:S(2)}) collective-permute-start(bf16[16,64,256]{2,1,0:T(8,128)(2,1)S(1)} %bitcast.5), channel_id=1, source_target_pairs={{0,1},{1,2},{2,3},{3,0},{128,131},{129,128},{130,129},{131,130},{2... | collective-permute-start | bytes 1572872 | tf_op jit(solution)/shard_map/ppermute | solution.py:22
  59.5 3.6 %collective-permute-start.6 = (bf16[16,64,256]{2,1,0:T(8,128)(2,1)S(1)}, bf16[16,64,256]{2,1,0:T(8,128)(2,1)S(1)}, u32[]{:S(2)}, u32[]{:S(2)}) collective-permute-start(bf16[16,64,256]{2,1,0:T(8,128)(2,1)S(1)} %bitcast.6), channel_id=1, source_target_pairs={{0,124},{4,0},{8,4},{12,8},{16,12},{20,16},{24,20},{28,24},{32,28}... | collective-permute-start | bytes 1572872 | tf_op jit(solution)/shard_map/ppermute | solution.py:22
  63.0 4.2 %collective-permute-done.refs_0_ = bf16[16,64,256]{2,1,0:T(8,128)(2,1)S(1)} collective-permute-done((bf16[16,64,256]{2,1,0:T(8,128)(2,1)S(1)}, bf16[16,64,256]{2,1,0:T(8,128)(2,1)S(1)}, u32[]{:S(2)}, u32[]{:S(2)}) %collective-permute-start) | collective-permute-done | bytes 524320 | tf_op jit(solution)/shard_map/ppermute | solution.py:22
  67.3 3.0 %collective-permute-start.3 = (bf16[16,64,256]{2,1,0:T(8,128)(2,1)S(1)}, bf16[16,64,256]{2,1,0:T(8,128)(2,1)S(1)}, u32[]{:S(2)}, u32[]{:S(2)}) collective-permute-start(bf16[16,64,256]{2,1,0:T(8,128)(2,1)S(1)} %collective-permute-done.refs_0_), channel_id=1, source_target_pairs={{0,4},{4,8},{8,12},{12,16},{16,20},{20,24},{24,28},{28,32},{32,36}... | collective-permute-start | bytes 1572872 | tf_op jit(solution)/shard_map/ppermute | solution.py:22
  70.2 1.7 %collective-permute-done.1.refs_1_ = bf16[16,64,256]{2,1,0:T(8,128)(2,1)S(1)} collective-permute-done((bf16[16,64,256]{2,1,0:T(8,128)(2,1)S(1)}, bf16[16,64,256]{2,1,0:T(8,128)(2,1)S(1)}, u32[]{:S(2)}, u32[]{:S(2)}) %collective-permute-start.1) | collective-permute-done | bytes 524320 | tf_op jit(solution)/shard_map/ppermute | solution.py:22
  71.9 3.2 %collective-permute-start.4 = (bf16[16,64,256]{2,1,0:T(8,128)(2,1)S(1)}, bf16[16,64,256]{2,1,0:T(8,128)(2,1)S(1)}, u32[]{:S(2)}, u32[]{:S(2)}) collective-permute-start(bf16[16,64,256]{2,1,0:T(8,128)(2,1)S(1)} %collective-permute-done.1.refs_1_), channel_id=1, source_target_pairs={{0,124},{4,0},{8,4},{12,8},{16,12},{20,16},{24,20},{28,24},{32,28}... | collective-permute-start | bytes 1572872 | tf_op jit(solution)/shard_map/ppermute | solution.py:22
  75.1 0.0 collective-permute-done.2.refs_2_
  75.1 2.6 %collective-permute-start.5 = (bf16[16,64,256]{2,1,0:T(8,128)(2,1)S(1)}, bf16[16,64,256]{2,1,0:T(8,128)(2,1)S(1)}, u32[]{:S(2)}, u32[]{:S(2)}) collective-permute-start(bf16[16,64,256]{2,1,0:T(8,128)(2,1)S(1)} %collective-permute-done.2.refs_2_), channel_id=1, source_target_pairs={{0,4},{4,8},{8,12},{12,16},{16,20},{20,24},{24,28},{28,32},{32,36}... | collective-permute-start | bytes 1572872 | tf_op jit(solution)/shard_map/ppermute | solution.py:22
  78.4 3.0 %shard_map.55.dense = bf16[64,512,128]{2,1,0:T(8,128)(2,1)S(1)} custom-call(s32[1,1,96]{2,1,0:T(1,128)} %coord_ref.1, s32[1,1]{1,0:T(1,128)S(6)} %copy.6.count_ref, bf16[1,1,96,128,128]{4,3,2,1,0:T(8,128)(2,1)} %adj_ref.1), custom_call_target="tpu_custom_call" | custom-call | bytes 12582912 | tf_op jit(solution)/shard_map/pallas_call | solution.py:69
  81.4 1.4 %shard_map.56.refs_0_ = f32[512,256]{1,0:T(8,128)S(1)} custom-call(bf16[64,512,128]{2,1,0:T(8,128)(2,1)S(1)} %shard_map.55.dense, bf16[16,64,256]{2,1,0:T(8,128)(2,1)S(1)} %collective-permute-done.refs_0_, bf16[16,64,256]{2,1,0:T(8,128)(2,1)S(1)} %collective-permute-done.1.refs_1_, bf16[16,64,256]{2,1,0:T(8,128)(2,1)S(1)} %collective-permute-done.2.refs_2_, ...), custom_call_target="tpu_custom_call" | custom-call | flops 1073741824 | bytes 6291456 | tf_op jit(solution)/shard_map/pallas_call | solution.py:125
  82.9 0.0 collective-permute-done.6.refs_4_
  82.9 2.2 %collective-permute-done.3.refs_1_ = bf16[16,64,256]{2,1,0:T(8,128)(2,1)S(1)} collective-permute-done((bf16[16,64,256]{2,1,0:T(8,128)(2,1)S(1)}, bf16[16,64,256]{2,1,0:T(8,128)(2,1)S(1)}, u32[]{:S(2)}, u32[]{:S(2)}) %collective-permute-start.3) | collective-permute-done | bytes 524320 | tf_op jit(solution)/shard_map/ppermute | solution.py:22
  85.1 1.6 %collective-permute-done.4.refs_2_ = bf16[16,64,256]{2,1,0:T(8,128)(2,1)S(1)} collective-permute-done((bf16[16,64,256]{2,1,0:T(8,128)(2,1)S(1)}, bf16[16,64,256]{2,1,0:T(8,128)(2,1)S(1)}, u32[]{:S(2)}, u32[]{:S(2)}) %collective-permute-start.4) | collective-permute-done | bytes 524320 | tf_op jit(solution)/shard_map/ppermute | solution.py:22
  86.7 4.0 %collective-permute-done.5.refs_3_ = bf16[16,64,256]{2,1,0:T(8,128)(2,1)S(1)} collective-permute-done((bf16[16,64,256]{2,1,0:T(8,128)(2,1)S(1)}, bf16[16,64,256]{2,1,0:T(8,128)(2,1)S(1)}, u32[]{:S(2)}, u32[]{:S(2)}) %collective-permute-start.5) | collective-permute-done | bytes 524320 | tf_op jit(solution)/shard_map/ppermute | solution.py:22
  90.7 1.4 %shard_map.57 = f32[512,256]{1,0:T(8,128)S(1)} custom-call(bf16[64,512,128]{2,1,0:T(8,128)(2,1)S(1)} %shard_map.55.dense, f32[512,256]{1,0:T(8,128)S(1)} %shard_map.56.refs_0_, bf16[16,64,256]{2,1,0:T(8,128)(2,1)S(1)} %collective-permute-done.3.refs_1_, bf16[16,64,256]{2,1,0:T(8,128)(2,1)S(1)} %collective-permute-done.4.refs_2_, ...), custom_call_target="tpu_custom_call" | custom-call | flops 1073741824 | bytes 6291456 | tf_op jit(solution)/shard_map/pallas_call | solution.py:125
  92.2 11.6 %all_to_all.5 = f16[8,64,256]{2,1,0:T(8,128)(2,1)S(1)} all-to-all(f16[8,64,256]{2,1,0:T(8,128)(2,1)S(1)} %bitcast.8), channel_id=1, replica_groups=mesh['row'=8,'z'=32,'y'=4] {'row'}, dimensions={0} | all-to-all | bytes 524288 | tf_op jit(solution)/shard_map/all_to_all | solution.py:162
  103.9 0.0 copy-done
  103.9 0.8 fusion
  (2 shorter events, 0.1 us)
Async XLA Ops:
  0.0 103.9 %copy-start = (bf16[256,256]{1,0:T(8,128)(2,1)S(1)}, bf16[256,256]{1,0:T(8,128)(2,1)}, u32[]{:S(2)}) copy-start(bf16[256,256]{1,0:T(8,128)(2,1)} %param.9) | copy-start | bytes 393220
  51.0 16.3 %collective-permute-start = (bf16[16,64,256]{2,1,0:T(8,128)(2,1)S(1)}, bf16[16,64,256]{2,1,0:T(8,128)(2,1)S(1)}, u32[]{:S(2)}, u32[]{:S(2)}) collective-permute-start(bf16[16,64,256]{2,1,0:T(8,128)(2,1)S(1)} %bitcast.3), channel_id=1, source_target_pairs={{0,2},{1,3},{2,0},{3,1},{128,130},{129,131},{130,128},{131,129},{2... | collective-permute-start | bytes 1572872 | tf_op jit(solution)/shard_map/ppermute | solution.py:22
  53.2 18.7 %collective-permute-start.1 = (bf16[16,64,256]{2,1,0:T(8,128)(2,1)S(1)}, bf16[16,64,256]{2,1,0:T(8,128)(2,1)S(1)}, u32[]{:S(2)}, u32[]{:S(2)}) collective-permute-start(bf16[16,64,256]{2,1,0:T(8,128)(2,1)S(1)} %bitcast.4), channel_id=1, source_target_pairs={{0,3},{1,0},{2,1},{3,2},{128,129},{129,130},{130,131},{131,128},{2... | collective-permute-start | bytes 1572872 | tf_op jit(solution)/shard_map/ppermute | solution.py:22
  57.5 17.6 %collective-permute-start.2 = (bf16[16,64,256]{2,1,0:T(8,128)(2,1)S(1)}, bf16[16,64,256]{2,1,0:T(8,128)(2,1)S(1)}, u32[]{:S(2)}, u32[]{:S(2)}) collective-permute-start(bf16[16,64,256]{2,1,0:T(8,128)(2,1)S(1)} %bitcast.5), channel_id=1, source_target_pairs={{0,1},{1,2},{2,3},{3,0},{128,131},{129,128},{130,129},{131,130},{2... | collective-permute-start | bytes 1572872 | tf_op jit(solution)/shard_map/ppermute | solution.py:22
  59.5 23.4 %collective-permute-start.6 = (bf16[16,64,256]{2,1,0:T(8,128)(2,1)S(1)}, bf16[16,64,256]{2,1,0:T(8,128)(2,1)S(1)}, u32[]{:S(2)}, u32[]{:S(2)}) collective-permute-start(bf16[16,64,256]{2,1,0:T(8,128)(2,1)S(1)} %bitcast.6), channel_id=1, source_target_pairs={{0,124},{4,0},{8,4},{12,8},{16,12},{20,16},{24,20},{28,24},{32,28}... | collective-permute-start | bytes 1572872 | tf_op jit(solution)/shard_map/ppermute | solution.py:22
  67.3 17.9 %collective-permute-start.3 = (bf16[16,64,256]{2,1,0:T(8,128)(2,1)S(1)}, bf16[16,64,256]{2,1,0:T(8,128)(2,1)S(1)}, u32[]{:S(2)}, u32[]{:S(2)}) collective-permute-start(bf16[16,64,256]{2,1,0:T(8,128)(2,1)S(1)} %collective-permute-done.refs_0_), channel_id=1, source_target_pairs={{0,4},{4,8},{8,12},{12,16},{16,20},{20,24},{24,28},{28,32},{32,36}... | collective-permute-start | bytes 1572872 | tf_op jit(solution)/shard_map/ppermute | solution.py:22
  71.9 14.8 %collective-permute-start.4 = (bf16[16,64,256]{2,1,0:T(8,128)(2,1)S(1)}, bf16[16,64,256]{2,1,0:T(8,128)(2,1)S(1)}, u32[]{:S(2)}, u32[]{:S(2)}) collective-permute-start(bf16[16,64,256]{2,1,0:T(8,128)(2,1)S(1)} %collective-permute-done.1.refs_1_), channel_id=1, source_target_pairs={{0,124},{4,0},{8,4},{12,8},{16,12},{20,16},{24,20},{28,24},{32,28}... | collective-permute-start | bytes 1572872 | tf_op jit(solution)/shard_map/ppermute | solution.py:22
  75.1 15.6 %collective-permute-start.5 = (bf16[16,64,256]{2,1,0:T(8,128)(2,1)S(1)}, bf16[16,64,256]{2,1,0:T(8,128)(2,1)S(1)}, u32[]{:S(2)}, u32[]{:S(2)}) collective-permute-start(bf16[16,64,256]{2,1,0:T(8,128)(2,1)S(1)} %collective-permute-done.2.refs_2_), channel_id=1, source_target_pairs={{0,4},{4,8},{8,12},{12,16},{16,20},{20,24},{24,28},{28,32},{32,36}... | collective-permute-start | bytes 1572872 | tf_op jit(solution)/shard_map/ppermute | solution.py:22

commit v9 on v8

--- a/solution.py
+++ b/solution.py
@@ -152,7 +152,7 @@
     half_z = z_size // 2
     groups = [[i + 2 * j for j in range(half_z)] for i in range(2)]
     own = lax.all_gather(features, "z", axis=0, axis_index_groups=groups)
-    spots = [2, 1, y_size - 1, 0]
+    spots = [1, y_size - 1, 2, 0]
     near = [ring_shift(own, "y", -spot) for spot in spots[:-1]] + [own]
     far = [ring_shift(piece, "z", (-1) ** at) for at, piece in enumerate(near)]
 

time: 105 us -> 108 us (1.029)
  the two profiles are of different devices: /device:TPU:16 before, /device:TPU:1 now
where the time goes in v9:
time: 108 us
  blocking collectives  71.2 us (66%)
  starting transfers between devices  22.7 us (21%)
  Pallas kernels  6.25 us (6%)
  waiting for transfers between devices  5.77 us (5%)
    all_gather x1, blocking collectives, on_device(): own = lax.all_gather(features, 'z', axis=0, axis_index_groups=groups)  45.3 us
    all_to_all x1, blocking collectives, on_device(): lax.all_to_all(partial_value.astype(jnp.float16).reshape(row_size, rows,...  25.9 us
    ppermute x7, starting transfers between devices, ring_shift(): return lax.ppermute(value, ('row', axis), pairs)  22.7 us
    ppermute x7, waiting for transfers between devices, ring_shift(): return lax.ppermute(value, ('row', axis), pairs)  5.77 us
    pallas_call x1, Pallas kernels, spread(): pl.pallas_call(functools.partial(spread_kernel, source_count=source_count...  3.42 us
    pallas_call x2, Pallas kernels, multiply(): pl.pallas_call(functools.partial(multiply_kernel, spots=spots, across=acr...  2.82 us
  transfers between devices with their start and end apart: 7, of which 2 were waited for; matrix products, arithmetic and copies ran while one was open for 0% of the time, Pallas kernels for 4%

profile of v9, /device:TPU:1, one launch (start us, length us, event | category | flops | bytes accessed | tf_op | source)
XLA Modules:
  0.0 107.6 jit_solution(5139816370896673980)
XLA Ops:
  0.0 0.0 copy-start
  0.0 45.3 %all-gather = bf16[1024,256]{1,0:T(8,128)(2,1)S(1)} all-gather(bf16[64,256]{1,0:T(8,128)(2,1)} %param.5), channel_id=2, replica_groups={{0,8,16,24,32,40,48,56,64,72,80,88,96,104,112,120},{4,12,20,28,36,44,52..., dimensions={0}, use_global_device_ids=true | all-gather | bytes 557056 | tf_op jit(solution)/shard_map/all_gather | solution.py:154
  45.3 3.1 %collective-permute-start = (bf16[16,64,256]{2,1,0:T(8,128)(2,1)S(1)}, bf16[16,64,256]{2,1,0:T(8,128)(2,1)S(1)}, u32[]{:S(2)}, u32[]{:S(2)}) collective-permute-start(bf16[16,64,256]{2,1,0:T(8,128)(2,1)S(1)} %bitcast.3), channel_id=1, source_target_pairs={{0,3},{1,0},{2,1},{3,2},{128,129},{129,130},{130,131},{131,128},{2... | collective-permute-start | bytes 1572872 | tf_op jit(solution)/shard_map/ppermute | solution.py:22
  48.5 3.4 %collective-permute-start.1 = (bf16[16,64,256]{2,1,0:T(8,128)(2,1)S(1)}, bf16[16,64,256]{2,1,0:T(8,128)(2,1)S(1)}, u32[]{:S(2)}, u32[]{:S(2)}) collective-permute-start(bf16[16,64,256]{2,1,0:T(8,128)(2,1)S(1)} %bitcast.4), channel_id=1, source_target_pairs={{0,1},{1,2},{2,3},{3,0},{128,131},{129,128},{130,129},{131,130},{2... | collective-permute-start | bytes 1572872 | tf_op jit(solution)/shard_map/ppermute | solution.py:22
  51.9 3.5 %collective-permute-start.2 = (bf16[16,64,256]{2,1,0:T(8,128)(2,1)S(1)}, bf16[16,64,256]{2,1,0:T(8,128)(2,1)S(1)}, u32[]{:S(2)}, u32[]{:S(2)}) collective-permute-start(bf16[16,64,256]{2,1,0:T(8,128)(2,1)S(1)} %bitcast.5), channel_id=1, source_target_pairs={{0,2},{1,3},{2,0},{3,1},{128,130},{129,131},{130,128},{131,129},{2... | collective-permute-start | bytes 1572872 | tf_op jit(solution)/shard_map/ppermute | solution.py:22
  55.4 2.7 %collective-permute-start.6 = (bf16[16,64,256]{2,1,0:T(8,128)(2,1)S(1)}, bf16[16,64,256]{2,1,0:T(8,128)(2,1)S(1)}, u32[]{:S(2)}, u32[]{:S(2)}) collective-permute-start(bf16[16,64,256]{2,1,0:T(8,128)(2,1)S(1)} %bitcast.6), channel_id=1, source_target_pairs={{0,124},{4,0},{8,4},{12,8},{16,12},{20,16},{24,20},{28,24},{32,28}... | collective-permute-start | bytes 1572872 | tf_op jit(solution)/shard_map/ppermute | solution.py:22
  58.1 0.0 collective-permute-done.refs_0_
  58.1 3.8 %collective-permute-start.3 = (bf16[16,64,256]{2,1,0:T(8,128)(2,1)S(1)}, bf16[16,64,256]{2,1,0:T(8,128)(2,1)S(1)}, u32[]{:S(2)}, u32[]{:S(2)}) collective-permute-start(bf16[16,64,256]{2,1,0:T(8,128)(2,1)S(1)} %collective-permute-done.refs_0_), channel_id=1, source_target_pairs={{0,4},{4,8},{8,12},{12,16},{16,20},{20,24},{24,28},{28,32},{32,36}... | collective-permute-start | bytes 1572872 | tf_op jit(solution)/shard_map/ppermute | solution.py:22
  61.9 0.0 collective-permute-done.1.refs_1_
  61.9 1.9 %collective-permute-start.4 = (bf16[16,64,256]{2,1,0:T(8,128)(2,1)S(1)}, bf16[16,64,256]{2,1,0:T(8,128)(2,1)S(1)}, u32[]{:S(2)}, u32[]{:S(2)}) collective-permute-start(bf16[16,64,256]{2,1,0:T(8,128)(2,1)S(1)} %collective-permute-done.1.refs_1_), channel_id=1, source_target_pairs={{0,124},{4,0},{8,4},{12,8},{16,12},{20,16},{24,20},{28,24},{32,28}... | collective-permute-start | bytes 1572872 | tf_op jit(solution)/shard_map/ppermute | solution.py:22
  63.9 0.3 collective-permute-done.2.refs_2_
  64.2 4.3 %collective-permute-start.5 = (bf16[16,64,256]{2,1,0:T(8,128)(2,1)S(1)}, bf16[16,64,256]{2,1,0:T(8,128)(2,1)S(1)}, u32[]{:S(2)}, u32[]{:S(2)}) collective-permute-start(bf16[16,64,256]{2,1,0:T(8,128)(2,1)S(1)} %collective-permute-done.2.refs_2_), channel_id=1, source_target_pairs={{0,4},{4,8},{8,12},{12,16},{16,20},{20,24},{24,28},{28,32},{32,36}... | collective-permute-start | bytes 1572872 | tf_op jit(solution)/shard_map/ppermute | solution.py:22
  69.1 3.4 %shard_map.55.dense = bf16[64,512,128]{2,1,0:T(8,128)(2,1)S(1)} custom-call(s32[1,1,96]{2,1,0:T(1,128)} %coord_ref.1, s32[1,1]{1,0:T(1,128)S(6)} %copy.6.count_ref, bf16[1,1,96,128,128]{4,3,2,1,0:T(8,128)(2,1)} %adj_ref.1), custom_call_target="tpu_custom_call" | custom-call | bytes 12582912 | tf_op jit(solution)/shard_map/pallas_call | solution.py:69
  72.5 1.4 %shard_map.56.refs_0_ = f32[512,256]{1,0:T(8,128)S(1)} custom-call(bf16[64,512,128]{2,1,0:T(8,128)(2,1)S(1)} %shard_map.55.dense, bf16[16,64,256]{2,1,0:T(8,128)(2,1)S(1)} %collective-permute-done.refs_0_, bf16[16,64,256]{2,1,0:T(8,128)(2,1)S(1)} %collective-permute-done.1.refs_1_, bf16[16,64,256]{2,1,0:T(8,128)(2,1)S(1)} %collective-permute-done.2.refs_2_, ...), custom_call_target="tpu_custom_call" | custom-call | flops 1073741824 | bytes 6291456 | tf_op jit(solution)/shard_map/pallas_call | solution.py:125
  74.0 0.0 collective-permute-done.6.refs_4_
  74.0 0.0 collective-permute-done.3.refs_1_
  74.0 0.0 collective-permute-done.4.refs_2_
  74.0 5.4 %collective-permute-done.5.refs_3_ = bf16[16,64,256]{2,1,0:T(8,128)(2,1)S(1)} collective-permute-done((bf16[16,64,256]{2,1,0:T(8,128)(2,1)S(1)}, bf16[16,64,256]{2,1,0:T(8,128)(2,1)S(1)}, u32[]{:S(2)}, u32[]{:S(2)}) %collective-permute-start.5) | collective-permute-done | bytes 524320 | tf_op jit(solution)/shard_map/ppermute | solution.py:22
  79.4 1.4 %shard_map.57 = f32[512,256]{1,0:T(8,128)S(1)} custom-call(bf16[64,512,128]{2,1,0:T(8,128)(2,1)S(1)} %shard_map.55.dense, f32[512,256]{1,0:T(8,128)S(1)} %shard_map.56.refs_0_, bf16[16,64,256]{2,1,0:T(8,128)(2,1)S(1)} %collective-permute-done.3.refs_1_, bf16[16,64,256]{2,1,0:T(8,128)(2,1)S(1)} %collective-permute-done.4.refs_2_, ...), custom_call_target="tpu_custom_call" | custom-call | flops 1073741824 | bytes 6291456 | tf_op jit(solution)/shard_map/pallas_call | solution.py:125
  80.9 25.9 %all_to_all.5 = f16[8,64,256]{2,1,0:T(8,128)(2,1)S(1)} all-to-all(f16[8,64,256]{2,1,0:T(8,128)(2,1)S(1)} %bitcast.8), channel_id=1, replica_groups=mesh['row'=8,'z'=32,'y'=4] {'row'}, dimensions={0} | all-to-all | bytes 524288 | tf_op jit(solution)/shard_map/all_to_all | solution.py:162
  106.8 0.0 copy-done
  106.8 0.8 fusion
  (2 shorter events, 0.1 us)
Async XLA Ops:
  0.0 106.8 %copy-start = (bf16[256,256]{1,0:T(8,128)(2,1)S(1)}, bf16[256,256]{1,0:T(8,128)(2,1)}, u32[]{:S(2)}) copy-start(bf16[256,256]{1,0:T(8,128)(2,1)} %param.9) | copy-start | bytes 393220
  45.3 12.8 %collective-permute-start = (bf16[16,64,256]{2,1,0:T(8,128)(2,1)S(1)}, bf16[16,64,256]{2,1,0:T(8,128)(2,1)S(1)}, u32[]{:S(2)}, u32[]{:S(2)}) collective-permute-start(bf16[16,64,256]{2,1,0:T(8,128)(2,1)S(1)} %bitcast.3), channel_id=1, source_target_pairs={{0,3},{1,0},{2,1},{3,2},{128,129},{129,130},{130,131},{131,128},{2... | collective-permute-start | bytes 1572872 | tf_op jit(solution)/shard_map/ppermute | solution.py:22
  48.5 13.4 %collective-permute-start.1 = (bf16[16,64,256]{2,1,0:T(8,128)(2,1)S(1)}, bf16[16,64,256]{2,1,0:T(8,128)(2,1)S(1)}, u32[]{:S(2)}, u32[]{:S(2)}) collective-permute-start(bf16[16,64,256]{2,1,0:T(8,128)(2,1)S(1)} %bitcast.4), channel_id=1, source_target_pairs={{0,1},{1,2},{2,3},{3,0},{128,131},{129,128},{130,129},{131,130},{2... | collective-permute-start | bytes 1572872 | tf_op jit(solution)/shard_map/ppermute | solution.py:22
  51.9 12.3 %collective-permute-start.2 = (bf16[16,64,256]{2,1,0:T(8,128)(2,1)S(1)}, bf16[16,64,256]{2,1,0:T(8,128)(2,1)S(1)}, u32[]{:S(2)}, u32[]{:S(2)}) collective-permute-start(bf16[16,64,256]{2,1,0:T(8,128)(2,1)S(1)} %bitcast.5), channel_id=1, source_target_pairs={{0,2},{1,3},{2,0},{3,1},{128,130},{129,131},{130,128},{131,129},{2... | collective-permute-start | bytes 1572872 | tf_op jit(solution)/shard_map/ppermute | solution.py:22
  55.4 18.6 %collective-permute-start.6 = (bf16[16,64,256]{2,1,0:T(8,128)(2,1)S(1)}, bf16[16,64,256]{2,1,0:T(8,128)(2,1)S(1)}, u32[]{:S(2)}, u32[]{:S(2)}) collective-permute-start(bf16[16,64,256]{2,1,0:T(8,128)(2,1)S(1)} %bitcast.6), channel_id=1, source_target_pairs={{0,124},{4,0},{8,4},{12,8},{16,12},{20,16},{24,20},{28,24},{32,28}... | collective-permute-start | bytes 1572872 | tf_op jit(solution)/shard_map/ppermute | solution.py:22
  58.1 15.9 %collective-permute-start.3 = (bf16[16,64,256]{2,1,0:T(8,128)(2,1)S(1)}, bf16[16,64,256]{2,1,0:T(8,128)(2,1)S(1)}, u32[]{:S(2)}, u32[]{:S(2)}) collective-permute-start(bf16[16,64,256]{2,1,0:T(8,128)(2,1)S(1)} %collective-permute-done.refs_0_), channel_id=1, source_target_pairs={{0,4},{4,8},{8,12},{12,16},{16,20},{20,24},{24,28},{28,32},{32,36}... | collective-permute-start | bytes 1572872 | tf_op jit(solution)/shard_map/ppermute | solution.py:22
  61.9 12.0 %collective-permute-start.4 = (bf16[16,64,256]{2,1,0:T(8,128)(2,1)S(1)}, bf16[16,64,256]{2,1,0:T(8,128)(2,1)S(1)}, u32[]{:S(2)}, u32[]{:S(2)}) collective-permute-start(bf16[16,64,256]{2,1,0:T(8,128)(2,1)S(1)} %collective-permute-done.1.refs_1_), channel_id=1, source_target_pairs={{0,124},{4,0},{8,4},{12,8},{16,12},{20,16},{24,20},{28,24},{32,28}... | collective-permute-start | bytes 1572872 | tf_op jit(solution)/shard_map/ppermute | solution.py:22
  64.2 15.3 %collective-permute-start.5 = (bf16[16,64,256]{2,1,0:T(8,128)(2,1)S(1)}, bf16[16,64,256]{2,1,0:T(8,128)(2,1)S(1)}, u32[]{:S(2)}, u32[]{:S(2)}) collective-permute-start(bf16[16,64,256]{2,1,0:T(8,128)(2,1)S(1)} %collective-permute-done.2.refs_2_), channel_id=1, source_target_pairs={{0,4},{4,8},{8,12},{12,16},{16,20},{20,24},{24,28},{28,32},{32,36}... | collective-permute-start | bytes 1572872 | tf_op jit(solution)/shard_map/ppermute | solution.py:22

commit v10 on v7

--- a/solution.py
+++ b/solution.py
@@ -12,9 +12,19 @@
 SENT_SCALE = 16.0
 
 
-def ring_shift(value, axis, step):
-    size = lax.axis_size(axis)
-    return lax.ppermute(value, axis, [(i, (i + step) % size) for i in range(size)])
+def shift(value, z_step, y_step):
+    axes = ("row", "z", "y")
+    rows, z_size, y_size = (lax.axis_size(axis) for axis in axes)
+    pairs = []
+    for row in range(rows):
+        turn = (-1) ** row
+        for z in range(z_size):
+            for y in range(y_size):
+                to_z, to_y = (z + turn * z_step) % z_size, (y + turn * y_step) % y_size
+                pairs.append(
+                    ((row * z_size + z) * y_size + y, (row * z_size + to_z) * y_size + to_y)
+                )
+    return lax.ppermute(value, axes, pairs)
 
 
 def spread_kernel(coord_ref, count_ref, adj_ref, dense, sem, *, source_count, tile):
@@ -85,11 +95,12 @@
     out_ref, feats, total = refs[added + len(spots) :]
     half = (lax.axis_index("z") + across) % 2
     own_y = lax.axis_index("y")
+    turn = 1 - 2 * (lax.axis_index("row") % 2)
     y_size, z_count, rows, width = feats.shape
     tile = dense.shape[-1]
     per_z = y_size * rows // tile
     for ref, offset in zip(piece_refs, spots):
-        feats[(own_y + offset) % y_size] = ref[...]
+        feats[(own_y + turn * offset + y_size) % y_size] = ref[...]
     per_step = 4
     for at in range(0, z_count, per_step):
         left, right = [], []
@@ -147,8 +158,14 @@
     groups = [[i + 2 * j for j in range(half_z)] for i in range(2)]
     own = lax.all_gather(features, "z", axis=0, axis_index_groups=groups)
     spots = [2, 1, y_size - 1, 0]
-    near = [ring_shift(own, "y", -spot) for spot in spots[:-1]] + [own]
-    far = [ring_shift(piece, "z", (-1) ** at) for at, piece in enumerate(near)]
+    opposite, one, other = (shift(own, 0, -spot) for spot in spots[:-1])
+    near = [opposite, one, other, own]
+    far = [
+        shift(opposite, 1, 0),
+        shift(one, -1, 0),
+        shift(own, 1, -spots[2]),
+        shift(own, -1, 0),
+    ]
 
     dense = spread(adj_tiles, tile_coord, tile_count, target_count, source_count)
     first = multiply(dense, near, spots, 0, jnp.float32)

time: 106 us -> 105 us (level)
  waiting for transfers between devices: 17.9 us -> 9.13 us
  blocking collectives: 59.6 us -> 63.9 us
  starting transfers between devices: 20.6 us -> 23.1 us
    ppermute x7, waiting for transfers between devices: 17.9 us -> 9.13 us  [shift(): return lax.ppermute(value, axes, pairs)]
    all_to_all x1, blocking collectives: 14.3 us -> 18.5 us  [on_device(): lax.all_to_all(partial_value.astype(jnp.float16).reshape(row_size, rows,...]
    ppermute x7, starting transfers between devices: 20.6 us -> 23.1 us  [shift(): return lax.ppermute(value, axes, pairs)]
  transfers between devices with their start and end apart: 7 -> 7, of which waited for: 2 -> 3; matrix products, arithmetic and copies ran while one was open for 0% -> 0% of each run, Pallas kernels for 4% -> 5%
where the time goes in v10:
time: 105 us; the launch traced here: 104 us
  blocking collectives  63.9 us (61%)
  starting transfers between devices  23.1 us (22%)
  waiting for transfers between devices  9.13 us (9%)
  Pallas kernels  6.44 us (6%)
    all_gather x1, blocking collectives, on_device(): own = lax.all_gather(features, 'z', axis=0, axis_index_groups=groups)  45.3 us
    ppermute x7, starting transfers between devices, shift(): return lax.ppermute(value, axes, pairs)  23.1 us
    all_to_all x1, blocking collectives, on_device(): lax.all_to_all(partial_value.astype(jnp.float16).reshape(row_size, rows,...  18.5 us
    ppermute x7, waiting for transfers between devices, shift(): return lax.ppermute(value, axes, pairs)  9.13 us
    pallas_call x1, Pallas kernels, spread(): pl.pallas_call(functools.partial(spread_kernel, source_count=source_count...  3.61 us
    pallas_call x2, Pallas kernels, multiply(): pl.pallas_call(functools.partial(multiply_kernel, spots=spots, across=acr...  2.83 us
  transfers between devices with their start and end apart: 7, of which 3 were waited for; matrix products, arithmetic and copies ran while one was open for 0% of the time, Pallas kernels for 5%

profile of v10, /device:TPU:1, one launch (start us, length us, event | category | flops | bytes accessed | tf_op | source)
XLA Modules:
  0.0 104.2 jit_solution(12351522510006279093)
XLA Ops:
  0.0 0.0 copy-start
  0.0 45.3 %all-gather = bf16[1024,256]{1,0:T(8,128)(2,1)S(1)} all-gather(bf16[64,256]{1,0:T(8,128)(2,1)} %param.5), channel_id=2, replica_groups={{0,8,16,24,32,40,48,56,64,72,80,88,96,104,112,120},{4,12,20,28,36,44,52..., dimensions={0}, use_global_device_ids=true | all-gather | bytes 557056 | tf_op jit(solution)/shard_map/all_gather | solution.py:159
  45.3 4.8 %collective-permute-start = (bf16[16,64,256]{2,1,0:T(8,128)(2,1)S(1)}, bf16[16,64,256]{2,1,0:T(8,128)(2,1)S(1)}, u32[]{:S(2)}, u32[]{:S(2)}) collective-permute-start(bf16[16,64,256]{2,1,0:T(8,128)(2,1)S(1)} %bitcast.3), channel_id=1, source_target_pairs={{0,2},{1,3},{2,0},{3,1},{4,6},{5,7},{6,4},{7,5},{8,10},{9,11},{10,... | collective-permute-start | bytes 1572872 | tf_op jit(solution)/shard_map/ppermute | solution.py:27
  50.1 2.3 %collective-permute-start.1 = (bf16[16,64,256]{2,1,0:T(8,128)(2,1)S(1)}, bf16[16,64,256]{2,1,0:T(8,128)(2,1)S(1)}, u32[]{:S(2)}, u32[]{:S(2)}) collective-permute-start(bf16[16,64,256]{2,1,0:T(8,128)(2,1)S(1)} %bitcast.4), channel_id=1, source_target_pairs={{0,3},{1,0},{2,1},{3,2},{4,7},{5,4},{6,5},{7,6},{8,11},{9,8},{10,9... | collective-permute-start | bytes 1572872 | tf_op jit(solution)/shard_map/ppermute | solution.py:27
  52.4 4.2 %collective-permute-start.2 = (bf16[16,64,256]{2,1,0:T(8,128)(2,1)S(1)}, bf16[16,64,256]{2,1,0:T(8,128)(2,1)S(1)}, u32[]{:S(2)}, u32[]{:S(2)}) collective-permute-start(bf16[16,64,256]{2,1,0:T(8,128)(2,1)S(1)} %bitcast.5), channel_id=1, source_target_pairs={{0,1},{1,2},{2,3},{3,0},{4,5},{5,6},{6,7},{7,4},{8,9},{9,10},{10,1... | collective-permute-start | bytes 1572872 | tf_op jit(solution)/shard_map/ppermute | solution.py:27
  56.6 2.7 %collective-permute-start.5 = (bf16[16,64,256]{2,1,0:T(8,128)(2,1)S(1)}, bf16[16,64,256]{2,1,0:T(8,128)(2,1)S(1)}, u32[]{:S(2)}, u32[]{:S(2)}) collective-permute-start(bf16[16,64,256]{2,1,0:T(8,128)(2,1)S(1)} %bitcast.6), channel_id=1, source_target_pairs={{0,5},{1,6},{2,7},{3,4},{4,9},{5,10},{6,11},{7,8},{8,13},{9,14},{1... | collective-permute-start | bytes 1572872 | tf_op jit(solution)/shard_map/ppermute | solution.py:27
  59.3 2.3 %collective-permute-start.6 = (bf16[16,64,256]{2,1,0:T(8,128)(2,1)S(1)}, bf16[16,64,256]{2,1,0:T(8,128)(2,1)S(1)}, u32[]{:S(2)}, u32[]{:S(2)}) collective-permute-start(bf16[16,64,256]{2,1,0:T(8,128)(2,1)S(1)} %bitcast.7), channel_id=1, source_target_pairs={{0,124},{1,125},{2,126},{3,127},{4,0},{5,1},{6,2},{7,3},{8,4},{9,5... | collective-permute-start | bytes 1572872 | tf_op jit(solution)/shard_map/ppermute | solution.py:27
  61.6 0.0 collective-permute-done.refs_0_
  61.7 4.1 %collective-permute-start.3 = (bf16[16,64,256]{2,1,0:T(8,128)(2,1)S(1)}, bf16[16,64,256]{2,1,0:T(8,128)(2,1)S(1)}, u32[]{:S(2)}, u32[]{:S(2)}) collective-permute-start(bf16[16,64,256]{2,1,0:T(8,128)(2,1)S(1)} %collective-permute-done.refs_0_), channel_id=1, source_target_pairs={{0,4},{1,5},{2,6},{3,7},{4,8},{5,9},{6,10},{7,11},{8,12},{9,13},{1... | collective-permute-start | bytes 1572872 | tf_op jit(solution)/shard_map/ppermute | solution.py:27
  65.8 0.4 collective-permute-done.1.refs_1_
  66.2 2.7 %collective-permute-start.4 = (bf16[16,64,256]{2,1,0:T(8,128)(2,1)S(1)}, bf16[16,64,256]{2,1,0:T(8,128)(2,1)S(1)}, u32[]{:S(2)}, u32[]{:S(2)}) collective-permute-start(bf16[16,64,256]{2,1,0:T(8,128)(2,1)S(1)} %collective-permute-done.1.refs_1_), channel_id=1, source_target_pairs={{0,124},{1,125},{2,126},{3,127},{4,0},{5,1},{6,2},{7,3},{8,4},{9,5... | collective-permute-start | bytes 1572872 | tf_op jit(solution)/shard_map/ppermute | solution.py:27
  69.6 3.6 %shard_map.55.dense = bf16[64,512,128]{2,1,0:T(8,128)(2,1)S(1)} custom-call(s32[1,1,96]{2,1,0:T(1,128)} %coord_ref.1, s32[1,1]{1,0:T(1,128)S(6)} %copy.6.count_ref, bf16[1,1,96,128,128]{4,3,2,1,0:T(8,128)(2,1)} %adj_ref.1), custom_call_target="tpu_custom_call" | custom-call | bytes 12582912 | tf_op jit(solution)/shard_map/pallas_call | solution.py:74
  73.2 4.1 %collective-permute-done.2.refs_2_ = bf16[16,64,256]{2,1,0:T(8,128)(2,1)S(1)} collective-permute-done((bf16[16,64,256]{2,1,0:T(8,128)(2,1)S(1)}, bf16[16,64,256]{2,1,0:T(8,128)(2,1)S(1)}, u32[]{:S(2)}, u32[]{:S(2)}) %collective-permute-start.2) | collective-permute-done | bytes 524320 | tf_op jit(solution)/shard_map/ppermute | solution.py:27
  77.3 1.4 %shard_map.56.refs_0_ = f32[512,256]{1,0:T(8,128)S(1)} custom-call(bf16[64,512,128]{2,1,0:T(8,128)(2,1)S(1)} %shard_map.55.dense, bf16[16,64,256]{2,1,0:T(8,128)(2,1)S(1)} %collective-permute-done.refs_0_, bf16[16,64,256]{2,1,0:T(8,128)(2,1)S(1)} %collective-permute-done.1.refs_1_, bf16[16,64,256]{2,1,0:T(8,128)(2,1)S(1)} %collective-permute-done.2.refs_2_, ...), custom_call_target="tpu_custom_call" | custom-call | flops 1073741824 | bytes 6291456 | tf_op jit(solution)/shard_map/pallas_call | solution.py:130
  78.8 0.0 collective-permute-done.5.refs_3_
  78.8 0.0 collective-permute-done.6.refs_4_
  78.8 0.0 collective-permute-done.3.refs_1_
  78.8 4.5 %collective-permute-done.4.refs_2_ = bf16[16,64,256]{2,1,0:T(8,128)(2,1)S(1)} collective-permute-done((bf16[16,64,256]{2,1,0:T(8,128)(2,1)S(1)}, bf16[16,64,256]{2,1,0:T(8,128)(2,1)S(1)}, u32[]{:S(2)}, u32[]{:S(2)}) %collective-permute-start.4) | collective-permute-done | bytes 524320 | tf_op jit(solution)/shard_map/ppermute | solution.py:27
  83.3 1.4 %shard_map.57 = f32[512,256]{1,0:T(8,128)S(1)} custom-call(bf16[64,512,128]{2,1,0:T(8,128)(2,1)S(1)} %shard_map.55.dense, f32[512,256]{1,0:T(8,128)S(1)} %shard_map.56.refs_0_, bf16[16,64,256]{2,1,0:T(8,128)(2,1)S(1)} %collective-permute-done.3.refs_1_, bf16[16,64,256]{2,1,0:T(8,128)(2,1)S(1)} %collective-permute-done.4.refs_2_, ...), custom_call_target="tpu_custom_call" | custom-call | flops 1073741824 | bytes 6291456 | tf_op jit(solution)/shard_map/pallas_call | solution.py:130
  84.8 18.5 %all_to_all.5 = f16[8,64,256]{2,1,0:T(8,128)(2,1)S(1)} all-to-all(f16[8,64,256]{2,1,0:T(8,128)(2,1)S(1)} %bitcast.9), channel_id=1, replica_groups=mesh['row'=8,'z'=32,'y'=4] {'row'}, dimensions={0} | all-to-all | bytes 524288 | tf_op jit(solution)/shard_map/all_to_all | solution.py:173
  103.4 0.0 copy-done
  103.4 0.8 fusion
  (2 shorter events, 0.1 us)
Async XLA Ops:
  0.0 103.4 %copy-start = (bf16[256,256]{1,0:T(8,128)(2,1)S(1)}, bf16[256,256]{1,0:T(8,128)(2,1)}, u32[]{:S(2)}) copy-start(bf16[256,256]{1,0:T(8,128)(2,1)} %param.9) | copy-start | bytes 393220
  45.3 16.3 %collective-permute-start = (bf16[16,64,256]{2,1,0:T(8,128)(2,1)S(1)}, bf16[16,64,256]{2,1,0:T(8,128)(2,1)S(1)}, u32[]{:S(2)}, u32[]{:S(2)}) collective-permute-start(bf16[16,64,256]{2,1,0:T(8,128)(2,1)S(1)} %bitcast.3), channel_id=1, source_target_pairs={{0,2},{1,3},{2,0},{3,1},{4,6},{5,7},{6,4},{7,5},{8,10},{9,11},{10,... | collective-permute-start | bytes 1572872 | tf_op jit(solution)/shard_map/ppermute | solution.py:27
  50.1 16.1 %collective-permute-start.1 = (bf16[16,64,256]{2,1,0:T(8,128)(2,1)S(1)}, bf16[16,64,256]{2,1,0:T(8,128)(2,1)S(1)}, u32[]{:S(2)}, u32[]{:S(2)}) collective-permute-start(bf16[16,64,256]{2,1,0:T(8,128)(2,1)S(1)} %bitcast.4), channel_id=1, source_target_pairs={{0,3},{1,0},{2,1},{3,2},{4,7},{5,4},{6,5},{7,6},{8,11},{9,8},{10,9... | collective-permute-start | bytes 1572872 | tf_op jit(solution)/shard_map/ppermute | solution.py:27
  52.4 24.9 %collective-permute-start.2 = (bf16[16,64,256]{2,1,0:T(8,128)(2,1)S(1)}, bf16[16,64,256]{2,1,0:T(8,128)(2,1)S(1)}, u32[]{:S(2)}, u32[]{:S(2)}) collective-permute-start(bf16[16,64,256]{2,1,0:T(8,128)(2,1)S(1)} %bitcast.5), channel_id=1, source_target_pairs={{0,1},{1,2},{2,3},{3,0},{4,5},{5,6},{6,7},{7,4},{8,9},{9,10},{10,1... | collective-permute-start | bytes 1572872 | tf_op jit(solution)/shard_map/ppermute | solution.py:27
  56.6 22.1 %collective-permute-start.5 = (bf16[16,64,256]{2,1,0:T(8,128)(2,1)S(1)}, bf16[16,64,256]{2,1,0:T(8,128)(2,1)S(1)}, u32[]{:S(2)}, u32[]{:S(2)}) collective-permute-start(bf16[16,64,256]{2,1,0:T(8,128)(2,1)S(1)} %bitcast.6), channel_id=1, source_target_pairs={{0,5},{1,6},{2,7},{3,4},{4,9},{5,10},{6,11},{7,8},{8,13},{9,14},{1... | collective-permute-start | bytes 1572872 | tf_op jit(solution)/shard_map/ppermute | solution.py:27
  59.3 19.5 %collective-permute-start.6 = (bf16[16,64,256]{2,1,0:T(8,128)(2,1)S(1)}, bf16[16,64,256]{2,1,0:T(8,128)(2,1)S(1)}, u32[]{:S(2)}, u32[]{:S(2)}) collective-permute-start(bf16[16,64,256]{2,1,0:T(8,128)(2,1)S(1)} %bitcast.7), channel_id=1, source_target_pairs={{0,124},{1,125},{2,126},{3,127},{4,0},{5,1},{6,2},{7,3},{8,4},{9,5... | collective-permute-start | bytes 1572872 | tf_op jit(solution)/shard_map/ppermute | solution.py:27
  61.7 17.1 %collective-permute-start.3 = (bf16[16,64,256]{2,1,0:T(8,128)(2,1)S(1)}, bf16[16,64,256]{2,1,0:T(8,128)(2,1)S(1)}, u32[]{:S(2)}, u32[]{:S(2)}) collective-permute-start(bf16[16,64,256]{2,1,0:T(8,128)(2,1)S(1)} %collective-permute-done.refs_0_), channel_id=1, source_target_pairs={{0,4},{1,5},{2,6},{3,7},{4,8},{5,9},{6,10},{7,11},{8,12},{9,13},{1... | collective-permute-start | bytes 1572872 | tf_op jit(solution)/shard_map/ppermute | solution.py:27
  66.2 17.1 %collective-permute-start.4 = (bf16[16,64,256]{2,1,0:T(8,128)(2,1)S(1)}, bf16[16,64,256]{2,1,0:T(8,128)(2,1)S(1)}, u32[]{:S(2)}, u32[]{:S(2)}) collective-permute-start(bf16[16,64,256]{2,1,0:T(8,128)(2,1)S(1)} %collective-permute-done.1.refs_1_), channel_id=1, source_target_pairs={{0,124},{1,125},{2,126},{3,127},{4,0},{5,1},{6,2},{7,3},{8,4},{9,5... | collective-permute-start | bytes 1572872 | tf_op jit(solution)/shard_map/ppermute | solution.py:27

commit v11 on v8

--- a/solution.py
+++ b/solution.py
@@ -154,7 +154,9 @@
     own = lax.all_gather(features, "z", axis=0, axis_index_groups=groups)
     spots = [2, 1, y_size - 1, 0]
     near = [ring_shift(own, "y", -spot) for spot in spots[:-1]] + [own]
-    far = [ring_shift(piece, "z", (-1) ** at) for at, piece in enumerate(near)]
+    far = [ring_shift(piece, "z", (-1) ** at) for at, piece in enumerate(near[:-1])]
+    late, _ = lax.optimization_barrier((own, far[0]))
+    far.append(ring_shift(late, "z", -1))
 
     dense = spread(adj_tiles, tile_coord, tile_count, target_count, source_count)
     first = multiply(dense, near, spots, 0, jnp.float32)

time: 105 us -> 111 us (1.057)
  the two profiles are of different devices: /device:TPU:16 before, /device:TPU:1 now
where the time goes in v11:
time: 111 us
  blocking collectives  62.2 us (56%)
  starting transfers between devices  22.1 us (20%)
  waiting for transfers between devices  18.2 us (16%)
  Pallas kernels  6.49 us (6%)
    all_gather x1, blocking collectives, on_device(): own = lax.all_gather(features, 'z', axis=0, axis_index_groups=groups)  45.3 us
    ppermute x7, starting transfers between devices, ring_shift(): return lax.ppermute(value, ('row', axis), pairs)  22.1 us
    ppermute x7, waiting for transfers between devices, ring_shift(): return lax.ppermute(value, ('row', axis), pairs)  18.2 us
    all_to_all x1, blocking collectives, on_device(): lax.all_to_all(partial_value.astype(jnp.float16).reshape(row_size, rows,...  16.9 us
    pallas_call x1, Pallas kernels, spread(): pl.pallas_call(functools.partial(spread_kernel, source_count=source_count...  3.66 us
    pallas_call x2, Pallas kernels, multiply(): pl.pallas_call(functools.partial(multiply_kernel, spots=spots, across=acr...  2.84 us
  transfers between devices with their start and end apart: 7, of which 5 were waited for; matrix products, arithmetic and copies ran while one was open for 0% of the time, Pallas kernels for 5%

profile of v11, /device:TPU:1, one launch (start us, length us, event | category | flops | bytes accessed | tf_op | source)
XLA Modules:
  0.0 110.6 jit_solution(10115344402918000024)
XLA Ops:
  0.0 0.0 copy-start
  0.0 45.3 %all-gather = bf16[1024,256]{1,0:T(8,128)(2,1)S(1)} all-gather(bf16[64,256]{1,0:T(8,128)(2,1)} %param.5), channel_id=2, replica_groups={{0,8,16,24,32,40,48,56,64,72,80,88,96,104,112,120},{4,12,20,28,36,44,52..., dimensions={0}, use_global_device_ids=true | all-gather | bytes 557056 | tf_op jit(solution)/shard_map/all_gather | solution.py:154
  45.3 4.8 %collective-permute-start = (bf16[16,64,256]{2,1,0:T(8,128)(2,1)S(1)}, bf16[16,64,256]{2,1,0:T(8,128)(2,1)S(1)}, u32[]{:S(2)}, u32[]{:S(2)}) collective-permute-start(bf16[16,64,256]{2,1,0:T(8,128)(2,1)S(1)} %bitcast.3), channel_id=1, source_target_pairs={{0,2},{1,3},{2,0},{3,1},{128,130},{129,131},{130,128},{131,129},{2... | collective-permute-start | bytes 1572872 | tf_op jit(solution)/shard_map/ppermute | solution.py:22
  50.1 2.3 %collective-permute-start.1 = (bf16[16,64,256]{2,1,0:T(8,128)(2,1)S(1)}, bf16[16,64,256]{2,1,0:T(8,128)(2,1)S(1)}, u32[]{:S(2)}, u32[]{:S(2)}) collective-permute-start(bf16[16,64,256]{2,1,0:T(8,128)(2,1)S(1)} %bitcast.4), channel_id=1, source_target_pairs={{0,3},{1,0},{2,1},{3,2},{128,129},{129,130},{130,131},{131,128},{2... | collective-permute-start | bytes 1572872 | tf_op jit(solution)/shard_map/ppermute | solution.py:22
  52.4 4.2 %collective-permute-start.2 = (bf16[16,64,256]{2,1,0:T(8,128)(2,1)S(1)}, bf16[16,64,256]{2,1,0:T(8,128)(2,1)S(1)}, u32[]{:S(2)}, u32[]{:S(2)}) collective-permute-start(bf16[16,64,256]{2,1,0:T(8,128)(2,1)S(1)} %bitcast.5), channel_id=1, source_target_pairs={{0,1},{1,2},{2,3},{3,0},{128,131},{129,128},{130,129},{131,130},{2... | collective-permute-start | bytes 1572872 | tf_op jit(solution)/shard_map/ppermute | solution.py:22
  56.6 0.2 collective-permute-done.refs_0_
  56.9 2.9 %collective-permute-start.3 = (bf16[16,64,256]{2,1,0:T(8,128)(2,1)S(1)}, bf16[16,64,256]{2,1,0:T(8,128)(2,1)S(1)}, u32[]{:S(2)}, u32[]{:S(2)}) collective-permute-start(bf16[16,64,256]{2,1,0:T(8,128)(2,1)S(1)} %collective-permute-done.refs_0_), channel_id=1, source_target_pairs={{0,4},{4,8},{8,12},{12,16},{16,20},{20,24},{24,28},{28,32},{32,36}... | collective-permute-start | bytes 1572872 | tf_op jit(solution)/shard_map/ppermute | solution.py:22
  59.8 6.5 %collective-permute-done.1.refs_1_ = bf16[16,64,256]{2,1,0:T(8,128)(2,1)S(1)} collective-permute-done((bf16[16,64,256]{2,1,0:T(8,128)(2,1)S(1)}, bf16[16,64,256]{2,1,0:T(8,128)(2,1)S(1)}, u32[]{:S(2)}, u32[]{:S(2)}) %collective-permute-start.1) | collective-permute-done | bytes 524320 | tf_op jit(solution)/shard_map/ppermute | solution.py:22
  66.2 2.7 %collective-permute-start.4 = (bf16[16,64,256]{2,1,0:T(8,128)(2,1)S(1)}, bf16[16,64,256]{2,1,0:T(8,128)(2,1)S(1)}, u32[]{:S(2)}, u32[]{:S(2)}) collective-permute-start(bf16[16,64,256]{2,1,0:T(8,128)(2,1)S(1)} %collective-permute-done.1.refs_1_), channel_id=1, source_target_pairs={{0,124},{4,0},{8,4},{12,8},{16,12},{20,16},{24,20},{28,24},{32,28}... | collective-permute-start | bytes 1572872 | tf_op jit(solution)/shard_map/ppermute | solution.py:22
  68.9 2.3 %collective-permute-done.2.refs_2_ = bf16[16,64,256]{2,1,0:T(8,128)(2,1)S(1)} collective-permute-done((bf16[16,64,256]{2,1,0:T(8,128)(2,1)S(1)}, bf16[16,64,256]{2,1,0:T(8,128)(2,1)S(1)}, u32[]{:S(2)}, u32[]{:S(2)}) %collective-permute-start.2) | collective-permute-done | bytes 524320 | tf_op jit(solution)/shard_map/ppermute | solution.py:22
  71.2 2.6 %collective-permute-start.5 = (bf16[16,64,256]{2,1,0:T(8,128)(2,1)S(1)}, bf16[16,64,256]{2,1,0:T(8,128)(2,1)S(1)}, u32[]{:S(2)}, u32[]{:S(2)}) collective-permute-start(bf16[16,64,256]{2,1,0:T(8,128)(2,1)S(1)} %collective-permute-done.2.refs_2_), channel_id=1, source_target_pairs={{0,4},{4,8},{8,12},{12,16},{16,20},{20,24},{24,28},{28,32},{32,36}... | collective-permute-start | bytes 1572872 | tf_op jit(solution)/shard_map/ppermute | solution.py:22
  73.8 0.0 collective-permute-done.3.refs_1_
  73.8 2.7 %collective-permute-start.6 = (bf16[16,64,256]{2,1,0:T(8,128)(2,1)S(1)}, bf16[16,64,256]{2,1,0:T(8,128)(2,1)S(1)}, u32[]{:S(2)}, u32[]{:S(2)}) collective-permute-start(bf16[16,64,256]{2,1,0:T(8,128)(2,1)S(1)} %bitcast.6), channel_id=1, source_target_pairs={{0,124},{4,0},{8,4},{12,8},{16,12},{20,16},{24,20},{28,24},{32,28}... | collective-permute-start | bytes 1572872 | tf_op jit(solution)/shard_map/ppermute | solution.py:22
  77.1 3.7 %shard_map.55.dense = bf16[64,512,128]{2,1,0:T(8,128)(2,1)S(1)} custom-call(s32[1,1,96]{2,1,0:T(1,128)} %coord_ref.1, s32[1,1]{1,0:T(1,128)S(6)} %copy.6.count_ref, bf16[1,1,96,128,128]{4,3,2,1,0:T(8,128)(2,1)} %adj_ref.1), custom_call_target="tpu_custom_call" | custom-call | bytes 12582912 | tf_op jit(solution)/shard_map/pallas_call | solution.py:69
  80.8 1.4 %shard_map.56.refs_0_ = f32[512,256]{1,0:T(8,128)S(1)} custom-call(bf16[64,512,128]{2,1,0:T(8,128)(2,1)S(1)} %shard_map.55.dense, bf16[16,64,256]{2,1,0:T(8,128)(2,1)S(1)} %collective-permute-done.refs_0_, bf16[16,64,256]{2,1,0:T(8,128)(2,1)S(1)} %collective-permute-done.1.refs_1_, bf16[16,64,256]{2,1,0:T(8,128)(2,1)S(1)} %collective-permute-done.2.refs_2_, ...), custom_call_target="tpu_custom_call" | custom-call | flops 1073741824 | bytes 6291456 | tf_op jit(solution)/shard_map/pallas_call | solution.py:125
  82.2 0.0 collective-permute-done.4.refs_2_
  82.2 0.8 collective-permute-done.5.refs_3_
  83.0 8.4 %collective-permute-done.6.refs_4_ = bf16[16,64,256]{2,1,0:T(8,128)(2,1)S(1)} collective-permute-done((bf16[16,64,256]{2,1,0:T(8,128)(2,1)S(1)}, bf16[16,64,256]{2,1,0:T(8,128)(2,1)S(1)}, u32[]{:S(2)}, u32[]{:S(2)}) %collective-permute-start.6) | collective-permute-done | bytes 524320 | tf_op jit(solution)/shard_map/ppermute | solution.py:22
  91.4 1.4 %shard_map.57 = f32[512,256]{1,0:T(8,128)S(1)} custom-call(bf16[64,512,128]{2,1,0:T(8,128)(2,1)S(1)} %shard_map.55.dense, f32[512,256]{1,0:T(8,128)S(1)} %shard_map.56.refs_0_, bf16[16,64,256]{2,1,0:T(8,128)(2,1)S(1)} %collective-permute-done.3.refs_1_, bf16[16,64,256]{2,1,0:T(8,128)(2,1)S(1)} %collective-permute-done.4.refs_2_, ...), custom_call_target="tpu_custom_call" | custom-call | flops 1073741824 | bytes 6291456 | tf_op jit(solution)/shard_map/pallas_call | solution.py:125
  92.9 16.9 %all_to_all.5 = f16[8,64,256]{2,1,0:T(8,128)(2,1)S(1)} all-to-all(f16[8,64,256]{2,1,0:T(8,128)(2,1)S(1)} %bitcast.8), channel_id=1, replica_groups=mesh['row'=8,'z'=32,'y'=4] {'row'}, dimensions={0} | all-to-all | bytes 524288 | tf_op jit(solution)/shard_map/all_to_all | solution.py:164
  109.9 0.0 copy-done
  109.9 0.8 fusion
  (2 shorter events, 0.1 us)
Async XLA Ops:
  0.0 109.9 %copy-start = (bf16[256,256]{1,0:T(8,128)(2,1)S(1)}, bf16[256,256]{1,0:T(8,128)(2,1)}, u32[]{:S(2)}) copy-start(bf16[256,256]{1,0:T(8,128)(2,1)} %param.9) | copy-start | bytes 393220
  45.3 11.5 %collective-permute-start = (bf16[16,64,256]{2,1,0:T(8,128)(2,1)S(1)}, bf16[16,64,256]{2,1,0:T(8,128)(2,1)S(1)}, u32[]{:S(2)}, u32[]{:S(2)}) collective-permute-start(bf16[16,64,256]{2,1,0:T(8,128)(2,1)S(1)} %bitcast.3), channel_id=1, source_target_pairs={{0,2},{1,3},{2,0},{3,1},{128,130},{129,131},{130,128},{131,129},{2... | collective-permute-start | bytes 1572872 | tf_op jit(solution)/shard_map/ppermute | solution.py:22
  50.1 16.1 %collective-permute-start.1 = (bf16[16,64,256]{2,1,0:T(8,128)(2,1)S(1)}, bf16[16,64,256]{2,1,0:T(8,128)(2,1)S(1)}, u32[]{:S(2)}, u32[]{:S(2)}) collective-permute-start(bf16[16,64,256]{2,1,0:T(8,128)(2,1)S(1)} %bitcast.4), channel_id=1, source_target_pairs={{0,3},{1,0},{2,1},{3,2},{128,129},{129,130},{130,131},{131,128},{2... | collective-permute-start | bytes 1572872 | tf_op jit(solution)/shard_map/ppermute | solution.py:22
  52.4 18.8 %collective-permute-start.2 = (bf16[16,64,256]{2,1,0:T(8,128)(2,1)S(1)}, bf16[16,64,256]{2,1,0:T(8,128)(2,1)S(1)}, u32[]{:S(2)}, u32[]{:S(2)}) collective-permute-start(bf16[16,64,256]{2,1,0:T(8,128)(2,1)S(1)} %bitcast.5), channel_id=1, source_target_pairs={{0,1},{1,2},{2,3},{3,0},{128,131},{129,128},{130,129},{131,130},{2... | collective-permute-start | bytes 1572872 | tf_op jit(solution)/shard_map/ppermute | solution.py:22
  56.9 16.9 %collective-permute-start.3 = (bf16[16,64,256]{2,1,0:T(8,128)(2,1)S(1)}, bf16[16,64,256]{2,1,0:T(8,128)(2,1)S(1)}, u32[]{:S(2)}, u32[]{:S(2)}) collective-permute-start(bf16[16,64,256]{2,1,0:T(8,128)(2,1)S(1)} %collective-permute-done.refs_0_), channel_id=1, source_target_pairs={{0,4},{4,8},{8,12},{12,16},{16,20},{20,24},{24,28},{28,32},{32,36}... | collective-permute-start | bytes 1572872 | tf_op jit(solution)/shard_map/ppermute | solution.py:22
  66.2 16.0 %collective-permute-start.4 = (bf16[16,64,256]{2,1,0:T(8,128)(2,1)S(1)}, bf16[16,64,256]{2,1,0:T(8,128)(2,1)S(1)}, u32[]{:S(2)}, u32[]{:S(2)}) collective-permute-start(bf16[16,64,256]{2,1,0:T(8,128)(2,1)S(1)} %collective-permute-done.1.refs_1_), channel_id=1, source_target_pairs={{0,124},{4,0},{8,4},{12,8},{16,12},{20,16},{24,20},{28,24},{32,28}... | collective-permute-start | bytes 1572872 | tf_op jit(solution)/shard_map/ppermute | solution.py:22
  71.2 11.8 %collective-permute-start.5 = (bf16[16,64,256]{2,1,0:T(8,128)(2,1)S(1)}, bf16[16,64,256]{2,1,0:T(8,128)(2,1)S(1)}, u32[]{:S(2)}, u32[]{:S(2)}) collective-permute-start(bf16[16,64,256]{2,1,0:T(8,128)(2,1)S(1)} %collective-permute-done.2.refs_2_), channel_id=1, source_target_pairs={{0,4},{4,8},{8,12},{12,16},{16,20},{20,24},{24,28},{28,32},{32,36}... | collective-permute-start | bytes 1572872 | tf_op jit(solution)/shard_map/ppermute | solution.py:22
  73.8 17.7 %collective-permute-start.6 = (bf16[16,64,256]{2,1,0:T(8,128)(2,1)S(1)}, bf16[16,64,256]{2,1,0:T(8,128)(2,1)S(1)}, u32[]{:S(2)}, u32[]{:S(2)}) collective-permute-start(bf16[16,64,256]{2,1,0:T(8,128)(2,1)S(1)} %bitcast.6), channel_id=1, source_target_pairs={{0,124},{4,0},{8,4},{12,8},{16,12},{20,16},{24,20},{28,24},{32,28}... | collective-permute-start | bytes 1572872 | tf_op jit(solution)/shard_map/ppermute | solution.py:22

commit v12 on v8

--- a/solution.py
+++ b/solution.py
@@ -153,8 +153,15 @@
     groups = [[i + 2 * j for j in range(half_z)] for i in range(2)]
     own = lax.all_gather(features, "z", axis=0, axis_index_groups=groups)
     spots = [2, 1, y_size - 1, 0]
-    near = [ring_shift(own, "y", -spot) for spot in spots[:-1]] + [own]
-    far = [ring_shift(piece, "z", (-1) ** at) for at, piece in enumerate(near)]
+    across = ring_shift(own, "z", -1)
+    opposite, one, other = (ring_shift(own, "y", -spot) for spot in spots[:-1])
+    near = [opposite, one, other, own]
+    far = [
+        ring_shift(opposite, "z", 1),
+        ring_shift(one, "z", -1),
+        ring_shift(across, "y", -spots[2]),
+        across,
+    ]
 
     dense = spread(adj_tiles, tile_coord, tile_count, target_count, source_count)
     first = multiply(dense, near, spots, 0, jnp.float32)

time: 105 us -> 108 us (1.029)
  the two profiles are of different devices: /device:TPU:16 before, /device:TPU:1 now
where the time goes in v12:
time: 108 us; the launch traced here: 107 us
  blocking collectives  68.7 us (64%)
  starting transfers between devices  22.6 us (21%)
  waiting for transfers between devices  8.74 us (8%)
  Pallas kernels  5.8 us (5%)
    all_gather x1, blocking collectives, on_device(): own = lax.all_gather(features, 'z', axis=0, axis_index_groups=groups)  45.3 us
    all_to_all x1, blocking collectives, on_device(): lax.all_to_all(partial_value.astype(jnp.float16).reshape(row_size, rows,...  23.4 us
    ppermute x7, starting transfers between devices, ring_shift(): return lax.ppermute(value, ('row', axis), pairs)  22.6 us
    ppermute x7, waiting for transfers between devices, ring_shift(): return lax.ppermute(value, ('row', axis), pairs)  8.74 us
    pallas_call x1, Pallas kernels, spread(): pl.pallas_call(functools.partial(spread_kernel, source_count=source_count...  2.97 us
    pallas_call x2, Pallas kernels, multiply(): pl.pallas_call(functools.partial(multiply_kernel, spots=spots, across=acr...  2.83 us
  transfers between devices with their start and end apart: 7, of which 4 were waited for; matrix products, arithmetic and copies ran while one was open for 0% of the time, Pallas kernels for 4%

profile of v12, /device:TPU:1, one launch (start us, length us, event | category | flops | bytes accessed | tf_op | source)
XLA Modules:
  0.0 107.5 jit_solution(15651421077352765544)
XLA Ops:
  0.0 0.0 copy-start
  0.0 45.3 %all-gather = bf16[1024,256]{1,0:T(8,128)(2,1)S(1)} all-gather(bf16[64,256]{1,0:T(8,128)(2,1)} %param.5), channel_id=2, replica_groups={{0,8,16,24,32,40,48,56,64,72,80,88,96,104,112,120},{4,12,20,28,36,44,52..., dimensions={0}, use_global_device_ids=true | all-gather | bytes 557056 | tf_op jit(solution)/shard_map/all_gather | solution.py:154
  45.3 4.8 %collective-permute-start = (bf16[16,64,256]{2,1,0:T(8,128)(2,1)S(1)}, bf16[16,64,256]{2,1,0:T(8,128)(2,1)S(1)}, u32[]{:S(2)}, u32[]{:S(2)}) collective-permute-start(bf16[16,64,256]{2,1,0:T(8,128)(2,1)S(1)} %bitcast.3), channel_id=1, source_target_pairs={{0,2},{1,3},{2,0},{3,1},{128,130},{129,131},{130,128},{131,129},{2... | collective-permute-start | bytes 1572872 | tf_op jit(solution)/shard_map/ppermute | solution.py:22
  50.1 2.3 %collective-permute-start.1 = (bf16[16,64,256]{2,1,0:T(8,128)(2,1)S(1)}, bf16[16,64,256]{2,1,0:T(8,128)(2,1)S(1)}, u32[]{:S(2)}, u32[]{:S(2)}) collective-permute-start(bf16[16,64,256]{2,1,0:T(8,128)(2,1)S(1)} %bitcast.4), channel_id=1, source_target_pairs={{0,3},{1,0},{2,1},{3,2},{128,129},{129,130},{130,131},{131,128},{2... | collective-permute-start | bytes 1572872 | tf_op jit(solution)/shard_map/ppermute | solution.py:22
  52.4 2.7 %collective-permute-start.5 = (bf16[16,64,256]{2,1,0:T(8,128)(2,1)S(1)}, bf16[16,64,256]{2,1,0:T(8,128)(2,1)S(1)}, u32[]{:S(2)}, u32[]{:S(2)}) collective-permute-start(bf16[16,64,256]{2,1,0:T(8,128)(2,1)S(1)} %bitcast.5), channel_id=1, source_target_pairs={{0,124},{4,0},{8,4},{12,8},{16,12},{20,16},{24,20},{28,24},{32,28}... | collective-permute-start | bytes 1572872 | tf_op jit(solution)/shard_map/ppermute | solution.py:22
  55.1 4.2 %collective-permute-start.2 = (bf16[16,64,256]{2,1,0:T(8,128)(2,1)S(1)}, bf16[16,64,256]{2,1,0:T(8,128)(2,1)S(1)}, u32[]{:S(2)}, u32[]{:S(2)}) collective-permute-start(bf16[16,64,256]{2,1,0:T(8,128)(2,1)S(1)} %bitcast.6), channel_id=1, source_target_pairs={{0,1},{1,2},{2,3},{3,0},{128,131},{129,128},{130,129},{131,130},{2... | collective-permute-start | bytes 1572872 | tf_op jit(solution)/shard_map/ppermute | solution.py:22
  59.3 0.0 collective-permute-done.refs_0_
  59.3 3.8 %collective-permute-start.3 = (bf16[16,64,256]{2,1,0:T(8,128)(2,1)S(1)}, bf16[16,64,256]{2,1,0:T(8,128)(2,1)S(1)}, u32[]{:S(2)}, u32[]{:S(2)}) collective-permute-start(bf16[16,64,256]{2,1,0:T(8,128)(2,1)S(1)} %collective-permute-done.refs_0_), channel_id=1, source_target_pairs={{0,4},{4,8},{8,12},{12,16},{16,20},{20,24},{24,28},{28,32},{32,36}... | collective-permute-start | bytes 1572872 | tf_op jit(solution)/shard_map/ppermute | solution.py:22
  63.1 3.1 %collective-permute-done.1.refs_1_ = bf16[16,64,256]{2,1,0:T(8,128)(2,1)S(1)} collective-permute-done((bf16[16,64,256]{2,1,0:T(8,128)(2,1)S(1)}, bf16[16,64,256]{2,1,0:T(8,128)(2,1)S(1)}, u32[]{:S(2)}, u32[]{:S(2)}) %collective-permute-start.1) | collective-permute-done | bytes 524320 | tf_op jit(solution)/shard_map/ppermute | solution.py:22
  66.2 2.7 %collective-permute-start.4 = (bf16[16,64,256]{2,1,0:T(8,128)(2,1)S(1)}, bf16[16,64,256]{2,1,0:T(8,128)(2,1)S(1)}, u32[]{:S(2)}, u32[]{:S(2)}) collective-permute-start(bf16[16,64,256]{2,1,0:T(8,128)(2,1)S(1)} %collective-permute-done.1.refs_1_), channel_id=1, source_target_pairs={{0,124},{4,0},{8,4},{12,8},{16,12},{20,16},{24,20},{28,24},{32,28}... | collective-permute-start | bytes 1572872 | tf_op jit(solution)/shard_map/ppermute | solution.py:22
  68.9 0.0 collective-permute-done.5.refs_4_
  68.9 2.2 %collective-permute-start.6 = (bf16[16,64,256]{2,1,0:T(8,128)(2,1)S(1)}, bf16[16,64,256]{2,1,0:T(8,128)(2,1)S(1)}, u32[]{:S(2)}, u32[]{:S(2)}) collective-permute-start(bf16[16,64,256]{2,1,0:T(8,128)(2,1)S(1)} %collective-permute-done.5.refs_4_), channel_id=1, source_target_pairs={{0,1},{1,2},{2,3},{3,0},{128,131},{129,128},{130,129},{131,130},{2... | collective-permute-start | bytes 1572872 | tf_op jit(solution)/shard_map/ppermute | solution.py:22
  71.8 3.0 %shard_map.55.dense = bf16[64,512,128]{2,1,0:T(8,128)(2,1)S(1)} custom-call(s32[1,1,96]{2,1,0:T(1,128)} %coord_ref.1, s32[1,1]{1,0:T(1,128)S(6)} %copy.6.count_ref, bf16[1,1,96,128,128]{4,3,2,1,0:T(8,128)(2,1)} %adj_ref.1), custom_call_target="tpu_custom_call" | custom-call | bytes 12582912 | tf_op jit(solution)/shard_map/pallas_call | solution.py:69
  74.8 0.3 collective-permute-done.2.refs_2_
  75.0 1.4 %shard_map.56.refs_0_ = f32[512,256]{1,0:T(8,128)S(1)} custom-call(bf16[64,512,128]{2,1,0:T(8,128)(2,1)S(1)} %shard_map.55.dense, bf16[16,64,256]{2,1,0:T(8,128)(2,1)S(1)} %collective-permute-done.refs_0_, bf16[16,64,256]{2,1,0:T(8,128)(2,1)S(1)} %collective-permute-done.1.refs_1_, bf16[16,64,256]{2,1,0:T(8,128)(2,1)S(1)} %collective-permute-done.2.refs_2_, ...), custom_call_target="tpu_custom_call" | custom-call | flops 1073741824 | bytes 6291456 | tf_op jit(solution)/shard_map/pallas_call | solution.py:125
  76.4 0.0 collective-permute-done.3.refs_1_
  76.5 3.9 %collective-permute-done.4.refs_2_ = bf16[16,64,256]{2,1,0:T(8,128)(2,1)S(1)} collective-permute-done((bf16[16,64,256]{2,1,0:T(8,128)(2,1)S(1)}, bf16[16,64,256]{2,1,0:T(8,128)(2,1)S(1)}, u32[]{:S(2)}, u32[]{:S(2)}) %collective-permute-start.4) | collective-permute-done | bytes 524320 | tf_op jit(solution)/shard_map/ppermute | solution.py:22
  80.3 1.5 %collective-permute-done.6.refs_3_ = bf16[16,64,256]{2,1,0:T(8,128)(2,1)S(1)} collective-permute-done((bf16[16,64,256]{2,1,0:T(8,128)(2,1)S(1)}, bf16[16,64,256]{2,1,0:T(8,128)(2,1)S(1)}, u32[]{:S(2)}, u32[]{:S(2)}) %collective-permute-start.6) | collective-permute-done | bytes 524320 | tf_op jit(solution)/shard_map/ppermute | solution.py:22
  81.8 1.4 %shard_map.57 = f32[512,256]{1,0:T(8,128)S(1)} custom-call(bf16[64,512,128]{2,1,0:T(8,128)(2,1)S(1)} %shard_map.55.dense, f32[512,256]{1,0:T(8,128)S(1)} %shard_map.56.refs_0_, bf16[16,64,256]{2,1,0:T(8,128)(2,1)S(1)} %collective-permute-done.3.refs_1_, bf16[16,64,256]{2,1,0:T(8,128)(2,1)S(1)} %collective-permute-done.4.refs_2_, ...), custom_call_target="tpu_custom_call" | custom-call | flops 1073741824 | bytes 6291456 | tf_op jit(solution)/shard_map/pallas_call | solution.py:125
  83.3 23.4 %all_to_all.5 = f16[8,64,256]{2,1,0:T(8,128)(2,1)S(1)} all-to-all(f16[8,64,256]{2,1,0:T(8,128)(2,1)S(1)} %bitcast.8), channel_id=1, replica_groups=mesh['row'=8,'z'=32,'y'=4] {'row'}, dimensions={0} | all-to-all | bytes 524288 | tf_op jit(solution)/shard_map/all_to_all | solution.py:169
  106.7 0.0 copy-done
  106.7 0.8 fusion
  (2 shorter events, 0.1 us)
Async XLA Ops:
  0.0 106.7 %copy-start = (bf16[256,256]{1,0:T(8,128)(2,1)S(1)}, bf16[256,256]{1,0:T(8,128)(2,1)}, u32[]{:S(2)}) copy-start(bf16[256,256]{1,0:T(8,128)(2,1)} %param.9) | copy-start | bytes 393220
  45.3 14.0 %collective-permute-start = (bf16[16,64,256]{2,1,0:T(8,128)(2,1)S(1)}, bf16[16,64,256]{2,1,0:T(8,128)(2,1)S(1)}, u32[]{:S(2)}, u32[]{:S(2)}) collective-permute-start(bf16[16,64,256]{2,1,0:T(8,128)(2,1)S(1)} %bitcast.3), channel_id=1, source_target_pairs={{0,2},{1,3},{2,0},{3,1},{128,130},{129,131},{130,128},{131,129},{2... | collective-permute-start | bytes 1572872 | tf_op jit(solution)/shard_map/ppermute | solution.py:22
  50.1 16.1 %collective-permute-start.1 = (bf16[16,64,256]{2,1,0:T(8,128)(2,1)S(1)}, bf16[16,64,256]{2,1,0:T(8,128)(2,1)S(1)}, u32[]{:S(2)}, u32[]{:S(2)}) collective-permute-start(bf16[16,64,256]{2,1,0:T(8,128)(2,1)S(1)} %bitcast.4), channel_id=1, source_target_pairs={{0,3},{1,0},{2,1},{3,2},{128,129},{129,130},{130,131},{131,128},{2... | collective-permute-start | bytes 1572872 | tf_op jit(solution)/shard_map/ppermute | solution.py:22
  52.4 16.5 %collective-permute-start.5 = (bf16[16,64,256]{2,1,0:T(8,128)(2,1)S(1)}, bf16[16,64,256]{2,1,0:T(8,128)(2,1)S(1)}, u32[]{:S(2)}, u32[]{:S(2)}) collective-permute-start(bf16[16,64,256]{2,1,0:T(8,128)(2,1)S(1)} %bitcast.5), channel_id=1, source_target_pairs={{0,124},{4,0},{8,4},{12,8},{16,12},{20,16},{24,20},{28,24},{32,28}... | collective-permute-start | bytes 1572872 | tf_op jit(solution)/shard_map/ppermute | solution.py:22
  55.1 19.9 %collective-permute-start.2 = (bf16[16,64,256]{2,1,0:T(8,128)(2,1)S(1)}, bf16[16,64,256]{2,1,0:T(8,128)(2,1)S(1)}, u32[]{:S(2)}, u32[]{:S(2)}) collective-permute-start(bf16[16,64,256]{2,1,0:T(8,128)(2,1)S(1)} %bitcast.6), channel_id=1, source_target_pairs={{0,1},{1,2},{2,3},{3,0},{128,131},{129,128},{130,129},{131,130},{2... | collective-permute-start | bytes 1572872 | tf_op jit(solution)/shard_map/ppermute | solution.py:22
  59.3 17.1 %collective-permute-start.3 = (bf16[16,64,256]{2,1,0:T(8,128)(2,1)S(1)}, bf16[16,64,256]{2,1,0:T(8,128)(2,1)S(1)}, u32[]{:S(2)}, u32[]{:S(2)}) collective-permute-start(bf16[16,64,256]{2,1,0:T(8,128)(2,1)S(1)} %collective-permute-done.refs_0_), channel_id=1, source_target_pairs={{0,4},{4,8},{8,12},{12,16},{16,20},{20,24},{24,28},{28,32},{32,36}... | collective-permute-start | bytes 1572872 | tf_op jit(solution)/shard_map/ppermute | solution.py:22
  66.2 14.1 %collective-permute-start.4 = (bf16[16,64,256]{2,1,0:T(8,128)(2,1)S(1)}, bf16[16,64,256]{2,1,0:T(8,128)(2,1)S(1)}, u32[]{:S(2)}, u32[]{:S(2)}) collective-permute-start(bf16[16,64,256]{2,1,0:T(8,128)(2,1)S(1)} %collective-permute-done.1.refs_1_), channel_id=1, source_target_pairs={{0,124},{4,0},{8,4},{12,8},{16,12},{20,16},{24,20},{28,24},{32,28}... | collective-permute-start | bytes 1572872 | tf_op jit(solution)/shard_map/ppermute | solution.py:22
  68.9 12.9 %collective-permute-start.6 = (bf16[16,64,256]{2,1,0:T(8,128)(2,1)S(1)}, bf16[16,64,256]{2,1,0:T(8,128)(2,1)S(1)}, u32[]{:S(2)}, u32[]{:S(2)}) collective-permute-start(bf16[16,64,256]{2,1,0:T(8,128)(2,1)S(1)} %collective-permute-done.5.refs_4_), channel_id=1, source_target_pairs={{0,1},{1,2},{2,3},{3,0},{128,131},{129,128},{130,129},{131,130},{2... | collective-permute-start | bytes 1572872 | tf_op jit(solution)/shard_map/ppermute | solution.py:22
